TPU v7x, 512 devices: a whole 4x4x16 slice. The times are simulated.
512 devices in a mesh: chord: 16 (over y, x), wall: 32 (over z, core).
Axes of the slice: x: 4, y: 4, z: 16, core: 2. Of those that a mesh axis runs over, the one named last changes fastest.
Arguments:
- rhs: float32 [5, 16, 64, 2048], P(None, None, 'wall', 'chord'), may hold values from -0.3 to 0.3
- jet_mask: int32 [16, 64, 2048], P(None, 'wall', 'chord'), may hold values 0 or 1
- jet_source: float32 [5], replicated, may hold values from -0.3 to 0.3
- wall_flags: int32 [16, 2048], P(None, 'chord'), may hold values from 0 to 2
- bc_table: float32 [3, 5], replicated, may hold values from 0.2 to 1.5
- xi_lower: float32 [5, 5, 16, 64, 2048], P(None, None, None, 'wall', 'chord'), may hold values from -1.2 to 1.2
- xi_upper: float32 [5, 5, 16, 64, 2048], P(None, None, None, 'wall', 'chord'), may hold values from -1.2 to 1.2
- eta_lower: float32 [5, 5, 16, 64, 2048], P(None, None, None, 'wall', 'chord'), may hold values from -1.2 to 1.2
- eta_upper: float32 [5, 5, 16, 64, 2048], P(None, None, None, 'wall', 'chord'), may hold values from -1.2 to 1.2
Outputs:
- increment: float32 [5, 16, 64, 2048], P(None, None, 'wall', 'chord')
All inputs are finite; a program needn't handle non-finite values. No bound on the sum of `jet_mask` on one device may be relied on, other than what follows from the above.
Results may differ from a plain program's by a relative error of at most 0.00019.
Values sent between devices are 32-bit elements; how exact they have to be, the bound alone decides.
No kernel may reach another device: no remote copies, remote signals or barrier semaphores. Data moves between devices by JAX's collectives and lax.ppermute only.
A program may use at most 64 MiB of HBM per device.

v0:
```python
import jax
import jax.numpy as jnp
from jax import lax
from jax.sharding import PartitionSpec as P

HIGH = lax.Precision.HIGHEST


def carried_in(part, axis, combine, identity, reverse):
    count = lax.axis_size(axis)
    place = lax.axis_index(axis)
    ahead = count - 1 - place if reverse else place
    gathered = jax.tree.map(lambda a: lax.all_gather(a, axis), part)
    state = jax.tree.map(lambda a, e: jnp.zeros_like(a) + jnp.asarray(e, a.dtype), part, identity)

    def one(hop, state):
        source = count - 1 - hop if reverse else hop
        return combine(
            state, jax.tree.map(lambda a: lax.dynamic_index_in_dim(a, source, 0, False), gathered)
        )

    return lax.fori_loop(0, ahead, one, state)


def block_product(left, right):
    return jnp.sum(left[:, :, None] * right[None, :, :], axis=1)


def compose(earlier, later):
    first_blocks, first_values = earlier
    second_blocks, second_values = later
    blocks = block_product(second_blocks, first_blocks)
    values = block_product(second_blocks, first_values) + second_values
    return (blocks, values)


def prefix_maps(blocks, values, chain_axis, reverse):
    if reverse:
        blocks = jnp.flip(blocks, chain_axis)
        values = jnp.flip(values, chain_axis)
    reach, state = lax.associative_scan(compose, (blocks, values), axis=chain_axis)
    if reverse:
        reach = jnp.flip(reach, chain_axis)
        state = jnp.flip(state, chain_axis)
    return (reach, state)


def identity_of(summary):
    blocks, values = summary
    eye = jnp.eye(5, dtype=jnp.float32).reshape((5, 5) + (1,) * (blocks.ndim - 2))
    return (jnp.broadcast_to(eye, blocks.shape), jnp.zeros_like(values))


def chain_sweep(blocks, values, chain_axis, reverse, carry_fn):
    reach, state = prefix_maps(blocks, values, chain_axis, reverse)
    edge = 0 if reverse else blocks.shape[chain_axis] - 1
    summary = (
        lax.index_in_dim(reach, edge, chain_axis, keepdims=False),
        lax.index_in_dim(state, edge, chain_axis, keepdims=False),
    )
    inflow = carry_fn(summary)[1]
    inflow = jnp.expand_dims(inflow, chain_axis)
    return state + block_product(reach, inflow)


def wall_down(summary):
    return carried_in(summary, "wall", compose, identity_of(summary), False)


def wall_up(summary):
    return carried_in(summary, "wall", compose, identity_of(summary), True)


def per_device(
    rhs, jet_mask, jet_source, wall_flags, bc_table, xi_lower, xi_upper, eta_lower, eta_upper
):
    source = rhs + jet_mask.astype(jnp.float32)[None] * jet_source[:, None, None, None]
    source = source[:, None]
    moved, lower_lines, upper_lines = (
        lax.all_to_all(source, "chord", split_axis=2, concat_axis=4, tiled=True),
        lax.all_to_all(xi_lower, "chord", split_axis=2, concat_axis=4, tiled=True),
        lax.all_to_all(xi_upper, "chord", split_axis=2, concat_axis=4, tiled=True),
    )
    ahead = prefix_maps(lower_lines, moved, 4, False)[1]
    behind = prefix_maps(upper_lines, ahead, 4, True)[1]
    solved = lax.all_to_all(behind, "chord", split_axis=4, concat_axis=2, tiled=True)
    onehot = (
        wall_flags[None] == jnp.arange(bc_table.shape[0], dtype=jnp.int32)[:, None, None]
    ).astype(jnp.float32)
    factor = jnp.einsum("fa,fki->aki", bc_table, onehot, precision=HIGH)
    first_row = (lax.axis_index("wall") == 0) & (jnp.arange(solved.shape[3], dtype=jnp.int32) == 0)
    scaled = (
        jnp.where(
            first_row[None, None, None, :, None], factor[:, None, :, None, :], jnp.float32(1.0)
        )
        * solved
    )
    lifted = chain_sweep(eta_lower, scaled, 3, False, wall_down)
    result = chain_sweep(eta_upper, lifted, 3, True, wall_up)
    return result[:, 0]


def solution(mesh):
    placed = (
        P(None, None, "wall", "chord"),
        P(None, "wall", "chord"),
        P(),
        P(None, "chord"),
        P(),
        P(None, None, None, "wall", "chord"),
        P(None, None, None, "wall", "chord"),
        P(None, None, None, "wall", "chord"),
        P(None, None, None, "wall", "chord"),
    )
    return jax.shard_map(
        per_device,
        mesh=mesh,
        in_specs=placed,
        out_specs=P(None, None, "wall", "chord"),
        check_vma=False,
    )
```

profile of v0, /device:TPU:1, one launch (start us, length us, event | category | flops | bytes accessed | tf_op | source)
XLA Modules:
  0.0 684.9 jit_solution(924621690026525459)
XLA Ops:
  7.3 1.6 fusion.10
  8.9 7.6 %all-to-all-start = ((f32[5,1,16,2,128]{4,3,0,1,2:T(2,128)}), f32[5,1,16,2,128]{4,3,0,1,2:T(2,128)S(1)}, u32[]{:S(2)}, u32[]{:S(2)}) async-start(f32[5,1,16,2,128]{4,3,0,1,2:T(2,128)} %fusion.10), calls=%async_computation | async-start | bytes 163840 | tf_op jit(solution)/shard_map/all_to_all | solution.py:80
  17.4 1.9 copy.331
  19.3 1.9 copy.356
  21.2 1.8 all-to-all-done
  23.1 4.8 all-to-all-start.1
  28.0 1.9 slice.667
  29.9 1.9 slice.589
  31.8 1.9 slice.588
  33.8 2.7 all-to-all-done.1
  36.5 4.5 all-to-all-start.2
  41.1 10.3 %slice.586 = f32[5,5,1,2,1023]{4,2,3,1,0:T(1,128)S(1)} slice(f32[5,5,1,2,2048]{4,2,3,1,0:T(1,128)S(1)} %bitcast.349), slice={[0:5:1], [0:5:1], [0:1:1], [0:2:1], [2:2048:2]} | slice | bytes 409200 | tf_op jit(solution)/shard_map/slice | solution.py:41
  51.4 10.2 %slice.587 = f32[5,5,1,2,1024]{4,2,3,1,0:T(1,128)S(1)} slice(f32[5,5,1,2,2048]{4,2,3,1,0:T(1,128)S(1)} %bitcast.350), slice={[0:5:1], [0:5:1], [0:1:1], [0:2:1], [1:2048:2]} | slice | bytes 409600 | tf_op jit(solution)/shard_map/slice | solution.py:41
  61.6 10.2 %slice.591 = f32[5,5,1,2,1024]{4,2,3,1,0:T(1,128)S(1)} slice(f32[5,5,1,2,2048]{4,2,3,1,0:T(1,128)S(1)} %bitcast.351), slice={[0:5:1], [0:5:1], [0:1:1], [0:2:1], [0:2047:2]} | slice | bytes 409600 | tf_op jit(solution)/shard_map/slice | solution.py:41
  74.3 3.9 slice.593
  78.2 3.9 slice.597
  83.5 2.5 slice.598
  86.0 2.5 slice.599
  89.0 2.5 slice.603
  92.5 1.8 slice.605
  94.3 1.8 slice.609
  96.7 1.1 slice.610
  97.8 1.2 slice.611
  118.3 1.8 slice.604
  124.8 3.9 slice.592
  131.1 1.3 pad.183
  132.6 1.3 pad.182
  134.4 2.3 pad.184
  136.7 2.3 pad.185
  139.1 1.9 slice.675
  141.0 1.9 slice.673
  143.0 10.2 %slice.671 = f32[5,5,1,2,1024]{4,2,3,1,0:T(1,128)S(1)} slice(f32[5,5,1,2,2048]{4,2,3,1,0:T(1,128)S(1)} %bitcast.346), slice={[0:5:1], [0:5:1], [0:1:1], [0:2:1], [0:2047:2]} | slice | bytes 409600 | tf_op jit(solution)/shard_map/slice | solution.py:41
  153.2 10.2 %slice.678 = f32[5,5,1,2,1024]{4,2,3,1,0:T(1,128)S(1)} slice(f32[5,5,1,2,2048]{4,2,3,1,0:T(1,128)S(1)} %bitcast.347), slice={[0:5:1], [0:5:1], [0:1:1], [0:2:1], [1:2048:2]} | slice | bytes 409600 | tf_op jit(solution)/shard_map/slice | solution.py:41
  164.2 1.5 slice.672
  168.5 1.5 slice.679
  170.7 3.9 slice.681
  174.6 3.9 slice.685
  179.9 2.5 slice.686
  182.4 2.5 slice.687
  185.4 2.5 slice.691
  188.8 1.8 slice.693
  190.7 1.8 slice.697
  193.1 1.1 slice.698
  194.2 1.2 slice.699
  214.9 1.8 slice.692
  221.4 3.9 slice.680
  227.7 10.2 %slice.669 = f32[5,5,1,2,1023]{4,2,3,1,0:T(1,128)S(1)} slice(f32[5,5,1,2,2048]{4,2,3,1,0:T(1,128)S(1)} %bitcast.348), slice={[0:5:1], [0:5:1], [0:1:1], [0:2:1], [1:2046:2]} | slice | bytes 409200 | tf_op jit(solution)/shard_map/slice | solution.py:41
  237.9 1.9 slice.755
  239.9 1.3 pad.205
  241.4 1.3 pad.204
  242.8 1.5 reverse.16
  245.9 2.3 pad.206
  248.2 2.3 pad.207
  250.6 1.5 rev.17
  253.2 3.6 reshape.765
  256.9 6.7 all-to-all-start.3
  263.9 6.3 all-to-all-done.3
  271.6 3.1 reshape.766
  277.7 74.7 %all-gather.11.cloned.1.call-done = f32[160,1,16,1,128]{4,2,3,1,0:T(8,128)} async-done(((f32[5,1,16,1,128]{4,2,3,1,0:T(8,128)}), f32[160,1,16,1,128]{4,2,3,1,0:T(8,128)}) %all-gather.11.cloned.1.call-update) | async-done | bytes 1310736 | tf_op jit(solution)/shard_map/all_gather | solution.py:13
  352.4 76.4 %all-gather.9.cloned.1.call-done = f32[160,5,16,1,128]{4,2,3,1,0:T(8,128)} async-done(((f32[5,5,16,1,128]{4,2,3,1,0:T(8,128)}), f32[160,5,16,1,128]{4,2,3,1,0:T(8,128)}) %all-gather.9.cloned.1.call-update) | async-done | bytes 6553616 | tf_op jit(solution)/shard_map/all_gather | solution.py:13
  428.8 1.8 while.26
  432.7 116.0 %all-gather.15.cloned.1.call-done = f32[160,1,16,1,128]{4,2,3,1,0:T(8,128)} async-done(((f32[5,1,16,1,128]{4,2,3,1,0:T(8,128)}), f32[160,1,16,1,128]{4,2,3,1,0:T(8,128)}) %all-gather.15.cloned.1.call-update) | async-done | bytes 1310736 | tf_op jit(solution)/shard_map/all_gather | solution.py:13
  548.7 76.3 %all-gather.13.cloned.1.call-done = f32[160,5,16,1,128]{4,2,3,1,0:T(8,128)} async-done(((f32[5,5,16,1,128]{4,2,3,1,0:T(8,128)}), f32[160,5,16,1,128]{4,2,3,1,0:T(8,128)}) %all-gather.13.cloned.1.call-update) | async-done | bytes 6553616 | tf_op jit(solution)/shard_map/all_gather | solution.py:13
  625.0 52.5 %while.27 = (s32[]{:T(128)}, f32[5,1,16,128]{3,2,0,1:T(8,128)S(1)}, s32[]{:T(128)}, f32[32,5,5,16,128]{4,3,2,1,0:T(8,128)}, f32[32,5,1,16,128]{4,3,2,1,0:T(8,128...) while((s32[]{:T(128)}, f32[5,1,16,128]{3,2,0,1:T(8,128)S(1)}, s32[]{:T(128)}, ...), condition=%wide.region_72.73_spmd, body=%wide.region_70.72_spmd.sunk | while | flops 102406 | bytes 409755 | solution.py:22
  (424 shorter events, 132.0 us)
Async XLA Ops:
  6.5 10.0 %copy-start = (f32[3,5]{1,0:T(4,128)S(1)}, f32[3,5]{1,0:T(4,128)}, u32[]{:S(2)}) copy-start(f32[3,5]{1,0:T(4,128)} %param.17) | copy-start | bytes 184
  8.9 14.2 %all-to-all-start = ((f32[5,1,16,2,128]{4,3,0,1,2:T(2,128)}), f32[5,1,16,2,128]{4,3,0,1,2:T(2,128)S(1)}, u32[]{:S(2)}, u32[]{:S(2)}) async-start(f32[5,1,16,2,128]{4,3,0,1,2:T(2,128)} %fusion.10), calls=%async_computation | async-start | bytes 163840 | tf_op jit(solution)/shard_map/all_to_all | solution.py:80
  23.1 13.4 %all-to-all-start.1 = ((f32[5,5,16,2,128]{4,3,1,0,2:T(2,128)}), f32[5,5,16,2,128]{4,3,1,0,2:T(2,128)S(1)}, u32[]{:S(2)}, u32[]{:S(2)}) async-start(f32[5,5,16,2,128]{4,3,1,0,2:T(2,128)} %copy.331), calls=%async_computation.1 | async-start | bytes 819200 | tf_op jit(solution)/shard_map/all_to_all | solution.py:81
  27.9 45.9 %copy-start.1 = (f32[5,1,1,2,2048]{4,3,0,2,1:T(2,128)}, f32[5,1,1,2,2048]{4,3,0,2,1:T(2,128)S(1)}, u32[]{:S(2)}) copy-start(f32[5,1,1,2,2048]{4,3,0,2,1:T(2,128)S(1)} %copy_bitcast_fusion.4) | copy-start | bytes 245764
  36.5 106.5 %all-to-all-start.2 = ((f32[5,5,16,2,128]{4,3,1,0,2:T(2,128)}), f32[5,5,16,2,128]{4,3,1,0,2:T(2,128)S(1)}, u32[]{:S(2)}, u32[]{:S(2)}) async-start(f32[5,5,16,2,128]{4,3,1,0,2:T(2,128)} %copy.356), calls=%async_computation.2 | async-start | bytes 819200 | tf_op jit(solution)/shard_map/all_to_all | solution.py:82
  100.8 33.5 %slice-start = ((f32[5,1,1,2,2048]{4,3,0,2,1:T(2,128)}), f32[5,1,1,2,1]{4,3,0,2,1:T(2,128)S(1)}, s32[]{:S(2)}) async-start(f32[5,1,1,2,2048]{4,3,0,2,1:T(2,128)} %copy-done.1), calls=%async_computation.8 | async-start | bytes 10240 | tf_op jit(solution)/shard_map/slice | solution.py:41
  256.9 13.3 %all-to-all-start.3 = ((f32[16,1,1280]{2,1,0:T(1,128)}), f32[16,1,1280]{2,1,0:T(1,128)S(1)}, u32[]{:S(2)}, u32[]{:S(2)}) async-start(f32[16,1,1280]{2,1,0:T(1,128)} %reshape.765), calls=%async_computation.3 | async-start | bytes 163840 | tf_op jit(solution)/shard_map/all_to_all | solution.py:86
  263.6 88.8 %all-gather.11.cloned.1.call-start = ((), (), s32[]{:S(2)}) async-start(), calls=%async_computation.5 | async-start | bytes 1351680 | tf_op jit(solution)/shard_map/all_gather | solution.py:13
  271.6 4.1 copy-start.2
  276.8 152.0 %all-gather.9.cloned.1.call-start = ((), (), s32[]{:S(2)}) async-start(), calls=%async_computation.4 | async-start | bytes 6758400 | tf_op jit(solution)/shard_map/all_gather | solution.py:13
  276.9 153.7 %copy-start.3 = (f32[5,5,16,2,128]{4,3,2,1,0:T(2,128)S(1)}, f32[5,5,16,2,128]{4,3,2,1,0:T(2,128)}, u32[]{:S(2)}) copy-start(f32[5,5,16,2,128]{4,3,2,1,0:T(2,128)} %param.21) | copy-start | bytes 1228804
  277.6 271.1 %all-gather.15.cloned.1.call-start = ((), (), s32[]{:S(2)}) async-start(), calls=%async_computation.7 | async-start | bytes 1351680 | tf_op jit(solution)/shard_map/all_gather | solution.py:13
  431.8 193.2 %all-gather.13.cloned.1.call-start = ((), (), s32[]{:S(2)}) async-start(), calls=%async_computation.6 | async-start | bytes 6758400 | tf_op jit(solution)/shard_map/all_gather | solution.py:13
Sparse Core Ops, SparseCore 0:
  276.9 75.4 all-gather.10
  354.5 74.2 all-gather.8
  431.9 116.7 all-gather.14
  550.7 74.2 all-gather.12
where the time goes:
time: 692 us; the launch traced here: 685 us
  waiting for transfers between devices  354 us (51%)
  local copies, waits for them, and re-layouts  220 us (32%)
  other arithmetic  70.5 us (10%)
  starting transfers between devices  24 us (3%)
  between operations  15.2 us (2%)
    all_gather x4, waiting for transfers between devices, carried_in(): gathered = jax.tree.map(lambda a: lax.all_gather(a, axis), part)  343 us
    slice x135, local copies, waits for them, and re-layouts, prefix_maps(): lax.associative_scan(compose, (blocks, values), axis=chain_axis)  165 us
    reduce_sum x98, other arithmetic, block_product(): return jnp.sum(left[:, :, None] * right[None, :, :], axis=1)  36.2 us
    pad x40, local copies, waits for them, and re-layouts, prefix_maps(): lax.associative_scan(compose, (blocks, values), axis=chain_axis)  35.2 us
    add x73, other arithmetic, compose(): values = block_product(second_blocks, first_values) + second_values  25.2 us
  transfers between devices with their start and end apart: 8, of which 7 were waited for; matrix products, arithmetic and copies ran while one was open for 17% of the time, Pallas kernels for 0%

commit v1 on v0

v1 whole, which is shorter than its diff:
```python
import jax
import jax.numpy as jnp
from jax import lax
from jax.experimental import pallas as pl
from jax.experimental.pallas import tpu as pltpu
from jax.sharding import PartitionSpec as P

F32 = jnp.float32
N = 5
ROWS = 48
VEC = 40
ANY = pl.BlockSpec(memory_space=pl.ANY)
HBM = pl.BlockSpec(memory_space=pltpu.HBM)
VM = pl.BlockSpec(memory_space=pltpu.VMEM)
SM = pl.BlockSpec(memory_space=pltpu.SMEM)
LIMIT = 32 << 20
WIDE = 60 << 20
LEAF = 220
STORE = LEAF + 510


def shape(*dims):
    return jax.ShapeDtypeStruct(dims, F32)


def params(limit=LIMIT):
    return pltpu.CompilerParams(vmem_limit_bytes=limit)


def cost(flops, nbytes):
    return pl.CostEstimate(flops=flops, bytes_accessed=nbytes, transcendentals=0)


def square(flat):
    return [[flat[N * i + j] for j in range(N)] for i in range(N)]


def flat(m):
    return [x for row in m for x in row]


def dot(xs, ys, start=None):
    total = start
    for x, y in zip(xs, ys):
        total = x * y if total is None else total + x * y
    return total


def mm(a, b, c=None):
    cols = list(zip(*b))
    return [
        [dot(a[i], cols[j], None if c is None else c[i][j]) for j in range(N)] for i in range(N)
    ]


def mv(a, x, c=None):
    return [dot(a[i], x, None if c is None else c[i]) for i in range(N)]


def lane_iota():
    return lax.broadcasted_iota(jnp.int32, (8, 128), 1)


def roll(x, by):
    return pltpu.roll(x, by % 128, 1)


def place():
    wall = lax.axis_index("wall")
    return lax.axis_index("chord"), wall // 2, wall % 2


def copy_all(copies):
    for c in copies:
        c.start()
    for c in copies:
        c.wait()


def pack_kernel(jet, rhs, mask, xl, xu, el, eu, send, src, rv, mk, out, own, sem):
    _, _, core = place()
    off = pl.multiple_of((1 - core) * 16, 16)
    first = [pltpu.make_async_copy(rhs, rv, sem.at[5]), pltpu.make_async_copy(mask, mk, sem.at[6])]
    copies = [
        pltpu.make_async_copy(ref.at[:, pl.ds(off, 16), :], send.at[pl.ds(25 * n, 25)], sem.at[n])
        for n, ref in enumerate((xl, xu, el, eu))
    ]
    for c in first + copies:
        c.start()
    for c in first:
        c.wait()
    keep = pl.multiple_of(core * 16, 16)
    for dst, at in ((out, off), (own, keep)):
        m = mk[pl.ds(at, 16), :].astype(F32)
        for c in range(N):
            dst[c] = rv[c, pl.ds(at, 16), :] + m * jet[c]
    copies.append(pltpu.make_async_copy(out, send.at[pl.ds(100, N)], sem.at[4]))
    copies.append(pltpu.make_async_copy(own, src, sem.at[7]))
    for c in copies[4:]:
        c.start()
    for c in copies:
        c.wait()


def compose(left, right):
    lb1, lv1, ub1, uv1, w1 = left
    lb2, lv2, ub2, uv2, w2 = right
    lb = mm(lb2, lb1)
    lv = mv(lb2, lv1, lv2)
    ub = mm(ub1, ub2)
    uv = mv(ub1, mv(w2, lv1, uv2), uv1)
    w = mm(ub1, mm(w2, lb1), w1)
    return lb, lv, ub, uv, w


def node(values):
    return (
        square(values[0:25]),
        list(values[25:30]),
        square(values[30:55]),
        list(values[55:60]),
        square(values[60:85]),
    )


def values_of(n):
    return flat(n[0]) + list(n[1]) + flat(n[2]) + list(n[3]) + flat(n[4])


def up_kernel(src, xl, xu, recv, msg, store, sl, su, ss, n1, n2, leaf, tree, sem):
    _, _, core = place()
    off = pl.multiple_of(core * 16, 16)
    copies = [
        pltpu.make_async_copy(xl.at[:, pl.ds(off, 16), :], sl.at[:, core], sem.at[0]),
        pltpu.make_async_copy(xu.at[:, pl.ds(off, 16), :], su.at[:, core], sem.at[1]),
        pltpu.make_async_copy(recv.at[pl.ds(0, 25)], sl.at[:, 1 - core], sem.at[2]),
        pltpu.make_async_copy(recv.at[pl.ds(25, 25)], su.at[:, 1 - core], sem.at[3]),
        pltpu.make_async_copy(recv.at[pl.ds(100, N)], ss.at[:, 1 - core], sem.at[4]),
        pltpu.make_async_copy(src, ss.at[:, core], sem.at[13]),
    ]
    copy_all(copies)
    lane = lane_iota()
    even = lane % 2 == 0
    low = (lane // 2) % 2 == 0

    def split(ref, c, r):
        a = ref[c, r, 0:8, :]
        b = ref[c, r, 8:16, :]
        return jnp.where(even, a, roll(b, 1)), jnp.where(even, roll(a, -1), b)

    saves = []
    for r in range(2):
        l1, l2 = zip(*[split(sl, c, r) for c in range(25)])
        v1, v2 = zip(*[split(ss, c, r) for c in range(N)])
        u1, u2 = zip(*[split(su, c, r) for c in range(25)])
        for c, x in enumerate(l1 + v1 + l2 + v2 + u1 + u2):
            leaf[r, c] = x
        dst = store.at[pl.ds(110 * r, 110)]
        saves.append(pltpu.make_async_copy(leaf.at[r], dst, sem.at[5 + r]))
        saves[-1].start()
        l1, l2, u1, u2 = square(l1), square(l2), square(u1), square(u2)
        lb = mm(l2, l1)
        lv = mv(l2, v1, v2)
        out = (lb, lv, mm(u1, u2), mv(u1, lv, v1), mm(u1, lb, l1))
        for c, x in enumerate(values_of(out)):
            n1[r, c] = x

    left, right = [], []
    for c in range(85):
        a, b = n1[0, c], n1[1, c]
        left.append(jnp.where(low, a, roll(b, 2)))
        right.append(jnp.where(low, roll(a, -2), b))
    for level in range(6):
        if level:
            left = [n2[c] for c in range(85)]
            right = [roll(x, -(2 << level)) for x in left]
        for c in range(30):
            tree[level, c] = left[c]
        for c in range(30, 85):
            tree[level, c] = right[c]
        dst = store.at[pl.ds(LEAF + 85 * level, 85)]
        saves.append(pltpu.make_async_copy(tree.at[level], dst, sem.at[7 + level]))
        saves[-1].start()
        for c, x in enumerate(values_of(compose(node(left), node(right)))):
            n2[c] = x
    group = lane // 4
    for g in range(3):
        acc = None
        for pos in range(min(32, 85 - 32 * g)):
            x = n2[32 * g + pos]
            acc = x if acc is None else jnp.where(group == pos, roll(x, 4 * pos), acc)
        for d in range(16):
            msg[d, 8 * g : 8 * g + 8, :] = acc
    for c in saves:
        c.wait()


def eta_copies(el, eu, recv, sl, su, core, sem):
    off = pl.multiple_of(core * 16, 16)
    return [
        pltpu.make_async_copy(el.at[:, pl.ds(off, 16), :], sl.at[:, core], sem.at[0]),
        pltpu.make_async_copy(eu.at[:, pl.ds(off, 16), :], su.at[:, core], sem.at[1]),
        pltpu.make_async_copy(recv.at[pl.ds(50, 25)], sl.at[:, 1 - core], sem.at[2]),
        pltpu.make_async_copy(recv.at[pl.ds(75, 25)], su.at[:, 1 - core], sem.at[3]),
    ]


def cell(ref, j):
    return square([ref[c, j // 2, pl.ds(j % 2, 8, stride=2), :] for c in range(25)])


def halves(x, y, first):
    return jnp.where(first, x, roll(y, 64)), jnp.where(first, roll(x, 64), y)


def wall_kernel(el, eu, recv, out, sl, su, sem):
    _, _, core = place()
    copy_all(eta_copies(el, eu, recv, sl, su, core, sem))
    first = lane_iota() < 64
    lb = cell(sl, 0)
    w = lb
    ub = cell(su, 0)
    for j in range(1, 4):
        lb = mm(cell(sl, j), lb)
        w = mm(ub, lb, w)
        ub = mm(ub, cell(su, j))
    values = flat(lb) + flat(ub) + flat(w)
    for r in range(38):
        a, b = halves(values[r], values[r + 37], first)
        out[pl.ds(r, 8, stride=ROWS), :] = a
        out[pl.ds(8 * ROWS + r, 8, stride=ROWS), :] = b


def down_kernel(
    table, flags, got, store, el, eu, recv, zin, scaled, zout,
    sl, su, lf, tr, cs, bh, vb, fl, sem,
):
    chord, z, core = place()
    eta = eta_copies(el, eu, recv, sl, su, core, sem)
    pre = [
        pltpu.make_async_copy(store.at[pl.ds(LEAF, 510)], tr, sem.at[4]),
        pltpu.make_async_copy(store.at[pl.ds(0, LEAF)], lf, sem.at[5]),
    ]
    kinds = pltpu.make_async_copy(flags, fl, sem.at[22])
    kinds.start()
    for c in pre + eta:
        c.start()
    lane = lane_iota()
    group = lane // 4
    for g in range(3):
        v = [got[s, 8 * g : 8 * g + 8, :] for s in range(16)]
        for bit in range(4):
            step = 1 << bit
            keep = (group // step) % 2 == 0
            fresh = list(v)
            for s in range(16):
                if s & step:
                    continue
                a, b = v[s], v[s | step]
                fresh[s] = jnp.where(keep, a, roll(b, 4 * step))
                fresh[s | step] = jnp.where(keep, roll(a, -4 * step), b)
            v = fresh
        for lo in range(16):
            if 32 * g + lo < 85:
                cs[32 * g + lo] = v[lo]
            if 32 * g + 16 + lo < 85:
                cs[32 * g + 16 + lo] = roll(v[lo], 64)

    def chain(m, t, sign):
        for bit in range(4):
            step = 1 << bit
            ok = group >= step if sign > 0 else group < 16 - step
            far = [roll(x, sign * 4 * step) for x in t]
            t = [jnp.where(ok, new, old) for new, old in zip(mv(m, far, t), t)]
            if bit < 3:
                fm = [[roll(x, sign * 4 * step) for x in row] for row in m]
                new = mm(m, fm)
                m = [[jnp.where(ok, new[i][j], m[i][j]) for j in range(N)] for i in range(N)]
        return t

    zero = jnp.zeros((8, 128), F32)
    t = chain(square([cs[c] for c in range(25)]), [cs[25 + c] for c in range(N)], 1)
    a = [jnp.where(group >= 1, roll(x, 4), zero) for x in t]
    f = mv(square([cs[60 + c] for c in range(25)]), a, [cs[55 + c] for c in range(N)])
    t = chain(square([cs[30 + c] for c in range(25)]), f, -1)
    b = [jnp.where(group < 15, roll(x, -4), zero) for x in t]
    back = (128 - 4 * chord) % 128
    a = [pltpu.roll(x, back, 1) for x in a]
    b = [pltpu.roll(x, back, 1) for x in b]

    pre[0].wait()
    for level in range(5, -1, -1):
        dist = 2 << level
        a_mid = mv(square([tr[85 * level + c] for c in range(25)]), a, [tr[85 * level + 25 + c] for c in range(N)])
        b_mid = mv(square([tr[85 * level + 30 + c] for c in range(25)]), b, [tr[85 * level + 55 + c] for c in range(N)])
        b_mid = mv(square([tr[85 * level + 60 + c] for c in range(25)]), a_mid, b_mid)
        left = (lane // dist) % 2 == 0
        if level:
            a = [jnp.where(left, x, roll(y, dist)) for x, y in zip(a, a_mid)]
            b = [jnp.where(left, x, roll(y, dist)) for x, y in zip(b_mid, b)]
    pre[1].wait()
    even = lane % 2 == 0
    for r in range(2):
        if r == 0:
            ra = [jnp.where(left, x, roll(y, 2)) for x, y in zip(a, a_mid)]
            rb = [jnp.where(left, x, roll(y, 2)) for x, y in zip(b_mid, b)]
        else:
            ra = [jnp.where(left, roll(x, -2), y) for x, y in zip(a, a_mid)]
            rb = [jnp.where(left, roll(x, -2), y) for x, y in zip(b_mid, b)]

        def part(first, count):
            return [lf[110 * r + first + c] for c in range(count)]

        a1 = mv(square(part(0, 25)), ra, part(25, N))
        a2 = mv(square(part(30, 25)), a1, part(55, N))
        b2 = mv(square(part(85, 25)), rb, a2)
        b1 = mv(square(part(60, 25)), b2, a1)
        for c in range(N):
            bh[c, r, 0:8, :] = jnp.where(even, b1[c], roll(b2[c], 1))
            bh[c, r, 8:16, :] = jnp.where(even, roll(b1[c], -1), b2[c])

    kinds.wait()
    kind = fl[pl.ds(pl.multiple_of(core * 8, 8), 8), :]
    s = []
    for j in range(4):
        s.append([bh[c, j // 2, pl.ds(j % 2, 8, stride=2), :] for c in range(N)])
    for c in range(N):
        factor = zero
        for k in range(3):
            factor = jnp.where(kind == k, table[k, c], factor)
        s[0][c] = jnp.where(z == 0, factor, 1.0) * s[0][c]
    for j in range(4):
        for c in range(N):
            scaled[j, c] = s[j][c]
    for c in eta:
        c.wait()
    t = [s[0]]
    for j in range(1, 4):
        t.append(mv(cell(sl, j), t[-1], s[j]))
    u = t[3]
    for j in range(2, -1, -1):
        u = mv(cell(su, j), u, t[j])
    first = lane < 64
    for c in range(N):
        x, y = halves(t[3][c], u[c], first)
        vb[pl.ds(c, 8, stride=8), :] = x
        vb[pl.ds(64 + c, 8, stride=8), :] = y
    for c in range(N, 8):
        vb[pl.ds(c, 8, stride=8), :] = zero
        vb[pl.ds(64 + c, 8, stride=8), :] = zero
    copy_all([
        pltpu.make_async_copy(
            vb.at[pl.ds(8 * d, 8)], zout.at[pl.ds(ROWS * d + VEC, 8)], sem.at[6 + d]
        )
        for d in range(16)
    ])


def solve_kernel(got, back, turned, ain):
    for n in range(16 * ROWS // 8):
        turned[8 * n : 8 * n + 8, :] = pltpu.roll(got[8 * n : 8 * n + 8, :], 64, 1)

    def value(z, c):
        ref = got if c < 37 else turned
        row = ROWS * z + (c if c < 37 else c - 37)
        return ref[row : row + 1, :]

    def block(z, first):
        return square([value(z, first + c) for c in range(25)])

    def vec(z, ref):
        return [ref[ROWS * z + VEC + c : ROWS * z + VEC + c + 1, :] for c in range(N)]

    zero = jnp.zeros((1, 128), F32)
    for n in range(16):
        back[8 * n : 8 * n + 8, :] = jnp.zeros((8, 128), F32)
    a = [zero] * N
    for z in range(16):
        for c in range(N):
            ain[8 * z + c : 8 * z + c + 1, :] = a[c]
        if z < 15:
            a = mv(block(z, 0), a, vec(z, got)) if z else vec(z, got)
    first = lax.broadcasted_iota(jnp.int32, (1, 128), 1) < 64
    b = [zero] * N
    for z in range(15, -1, -1):
        a = [ain[8 * z + c : 8 * z + c + 1, :] for c in range(N)]
        for c in range(N):
            back[8 * z + c : 8 * z + c + 1, :] = jnp.where(first, a[c], pltpu.roll(b[c], 64, 1))
        if z:
            f = mv(block(z, 50), a, vec(z, turned))
            b = mv(block(z, 25), b, f)


def finish_kernel(got, scaled, el, eu, recv, own, send, sl, su, res, sem):
    _, _, core = place()
    copies = eta_copies(el, eu, recv, sl, su, core, sem)
    for c in copies:
        c.start()
    first = lane_iota() < 64
    a, b = [], []
    for c in range(N):
        x = got[pl.ds(c, 8, stride=8), :]
        y = got[pl.ds(64 + c, 8, stride=8), :]
        a.append(jnp.where(first, x, roll(y, 64)))
        b.append(jnp.where(first, roll(x, 64), y))
    for c in copies:
        c.wait()
    lifted = []
    for j in range(4):
        a = mv(cell(sl, j), a, [scaled[j, c] for c in range(N)])
        lifted.append(a)
    for j in range(3, -1, -1):
        b = mv(cell(su, j), b, lifted[j])
        for c in range(N):
            res[c, j // 2, pl.ds(j % 2, 8, stride=2), :] = b[c]
    for c in range(N):
        own[c] = res[c, core]
        send[c] = res[c, 1 - core]


def dma(n):
    return pltpu.SemaphoreType.DMA((n,))


def per_device(
    rhs, jet_mask, jet_source, wall_flags, bc_table, xi_lower, xi_upper, eta_lower, eta_upper
):
    def far(x, *dims):
        return pltpu.with_memory_space_constraint(x.reshape(dims), pltpu.HBM)

    rhs, mask, flags = far(rhs, N, 32, 128), far(jet_mask, 32, 128), far(wall_flags, 16, 128)
    xl, xu, el, eu = (far(x, 25, 32, 128) for x in (xi_lower, xi_upper, eta_lower, eta_upper))
    swap = [(n, n ^ 1) for n in range(lax.axis_size("wall"))]
    groups = [list(range(c, lax.axis_size("wall"), 2)) for c in range(2)]

    def over_z(x):
        return lax.all_to_all(x, "wall", 0, 0, tiled=True, axis_index_groups=groups)

    side = pltpu.VMEM((25, 2, 16, 128), F32)
    send, src = pl.pallas_call(
        pack_kernel,
        out_shape=(shape(105, 16, 128), pltpu.HBM((N, 16, 128), F32)),
        in_specs=[SM] + [HBM] * 6,
        out_specs=(ANY, HBM),
        scratch_shapes=[
            pltpu.VMEM((N, 32, 128), F32),
            pltpu.VMEM((32, 128), jnp.int32),
            pltpu.VMEM((N, 16, 128), F32),
            pltpu.VMEM((N, 16, 128), F32),
            dma(8),
        ],
        compiler_params=params(WIDE),
        name="pack",
    )(jet_source, rhs, mask, xl, xu, el, eu)
    recv = lax.ppermute(send, "wall", swap)
    msg, store = pl.pallas_call(
        up_kernel,
        out_shape=(shape(16, 24, 128), pltpu.HBM((STORE, 8, 128), F32)),
        in_specs=[HBM, HBM, HBM, ANY],
        out_specs=(VM, HBM),
        scratch_shapes=[
            side,
            side,
            pltpu.VMEM((N, 2, 16, 128), F32),
            pltpu.VMEM((2, 85, 8, 128), F32),
            pltpu.VMEM((85, 8, 128), F32),
            pltpu.VMEM((2, 110, 8, 128), F32),
            pltpu.VMEM((6, 85, 8, 128), F32),
            dma(14),
        ],
        compiler_params=params(),
        name="chord_up",
    )(far(src, N, 16, 128), xl, xu, recv)
    zmat = pl.pallas_call(
        wall_kernel,
        out_shape=shape(16 * ROWS, 128),
        in_specs=[HBM, HBM, ANY],
        out_specs=VM,
        scratch_shapes=[side, side, dma(4)],
        compiler_params=params(),
        cost_estimate=cost(3 * 250 * 3 * 1024, 2 << 20),
        name="wall_blocks",
    )(el, eu, recv)
    got = lax.all_to_all(msg, "chord", 0, 0, tiled=True)
    scaled, zmsg = pl.pallas_call(
        down_kernel,
        out_shape=(shape(4, N, 8, 128), shape(16 * ROWS, 128)),
        in_specs=[SM, HBM, VM, HBM, HBM, HBM, ANY, ANY],
        out_specs=(VM, ANY),
        scratch_shapes=[
            side,
            side,
            pltpu.VMEM((LEAF, 8, 128), F32),
            pltpu.VMEM((510, 8, 128), F32),
            pltpu.VMEM((85, 8, 128), F32),
            pltpu.VMEM((N, 2, 16, 128), F32),
            pltpu.VMEM((128, 128), F32),
            pltpu.VMEM((16, 128), jnp.int32),
            dma(23),
        ],
        input_output_aliases={7: 1},
        compiler_params=params(),
        name="chord_down",
    )(bc_table, flags, got, far(store, STORE, 8, 128), el, eu, recv, zmat)
    zgot = over_z(zmsg.reshape(16, ROWS, 128)).reshape(16 * ROWS, 128)
    back = pl.pallas_call(
        solve_kernel,
        out_shape=shape(128, 128),
        in_specs=[VM],
        out_specs=VM,
        scratch_shapes=[pltpu.VMEM((16 * ROWS, 128), F32), pltpu.VMEM((128, 128), F32)],
        compiler_params=params(),
        name="wall_solve",
    )(zgot)
    inflow = over_z(back.reshape(16, 8, 128)).reshape(128, 128)
    own, other = pl.pallas_call(
        finish_kernel,
        out_shape=(shape(N, 16, 128), shape(N, 16, 128)),
        in_specs=[VM, VM, HBM, HBM, ANY],
        out_specs=(VM, VM),
        scratch_shapes=[side, side, pltpu.VMEM((N, 2, 16, 128), F32), dma(4)],
        compiler_params=params(),
        name="finish",
    )(inflow, scaled, el, eu, recv)
    other = lax.ppermute(other, "wall", swap)
    core = lax.axis_index("wall") % 2
    low = jnp.where(core == 0, own, other)
    high = jnp.where(core == 0, other, own)
    return jnp.concatenate([low, high], axis=1).reshape(N, 16, 2, 128)


def solution(mesh):
    placed = (
        P(None, None, "wall", "chord"),
        P(None, "wall", "chord"),
        P(),
        P(None, "chord"),
        P(),
        P(None, None, None, "wall", "chord"),
        P(None, None, None, "wall", "chord"),
        P(None, None, None, "wall", "chord"),
        P(None, None, None, "wall", "chord"),
    )
    return jax.shard_map(
        per_device,
        mesh=mesh,
        in_specs=placed,
        out_specs=P(None, None, "wall", "chord"),
        check_vma=False,
    )
```

time: 692 us -> 117 us (0.17)
  waiting for transfers between devices: 354 us -> 9.14 us
  local copies, waits for them, and re-layouts: 220 us -> 0.01 us
  other arithmetic: 70.5 us -> 0.65 us
  blocking collectives: 0 us -> 52.4 us
  Pallas kernels: 0 us -> 37.1 us
  between operations: 15.2 us -> 0.08 us
    all_gather x4 -> x0, waiting for transfers between devices: 343 us -> none  [carried_in(): gathered = jax.tree.map(lambda a: lax.all_gather(a, axis), part)]
    slice x135 -> x0, local copies, waits for them, and re-layouts: 165 us -> none  [prefix_maps(): lax.associative_scan(compose, (blocks, values), axis=chain_axis)]
    all_to_all x0 -> x2, blocking collectives: none -> 52.4 us  [over_z(): return lax.all_to_all(x, 'wall', 0, 0, tiled=True, axis_index_groups=groups)]
    pallas_call x0 -> x6, Pallas kernels: none -> 37.1 us  [the longest x1 26.8 us: per_device(): pl.pallas_call(pack_kernel, out_shape=(shape(105, 16, 128), pltpu.HBM((N,...]
    reduce_sum x98 -> x0, other arithmetic: 36.2 us -> none  [block_product(): return jnp.sum(left[:, :, None] * right[None, :, :], axis=1)]
    pad x40 -> x0, local copies, waits for them, and re-layouts: 35.2 us -> none  [prefix_maps(): lax.associative_scan(compose, (blocks, values), axis=chain_axis)]
    add x101 -> x0, other arithmetic: 26 us -> none  [the longest x73 25.2 us: compose(): values = block_product(second_blocks, first_values) + second_values]
    all_to_all x4 -> x1, starting transfers between devices: 23.7 us -> 3.53 us  [per_device(): got = lax.all_to_all(msg, 'chord', 0, 0, tiled=True)]
  transfers between devices with their start and end apart: 8 -> 3, of which waited for: 7 -> 3; matrix products, arithmetic and copies ran while one was open for 17% -> 0% of each run, Pallas kernels for 0% -> 1%
where the time goes in v1:
time: 117 us
  blocking collectives  52.4 us (45%)
  Pallas kernels  37.1 us (32%)
  starting transfers between devices  17.3 us (15%)
  waiting for transfers between devices  9.14 us (8%)
    all_to_all x2, blocking collectives, over_z(): return lax.all_to_all(x, 'wall', 0, 0, tiled=True, axis_index_groups=groups)  52.4 us
    pallas_call x1, Pallas kernels, per_device(): pl.pallas_call(pack_kernel, out_shape=(shape(105, 16, 128), pltpu.HBM((N,...  26.8 us
    ppermute x1, starting transfers between devices, per_device(): recv = lax.ppermute(send, 'wall', swap)  8.79 us
    all_to_all x1, waiting for transfers between devices, per_device(): got = lax.all_to_all(msg, 'chord', 0, 0, tiled=True)  6.1 us
    ppermute x1, starting transfers between devices, per_device(): other = lax.ppermute(other, 'wall', swap)  4.97 us
    pallas_call x1, Pallas kernels, per_device(): pl.pallas_call(up_kernel, out_shape=(shape(16, 24, 128), pltpu.HBM((STORE...  3.96 us
    all_to_all x1, starting transfers between devices, per_device(): got = lax.all_to_all(msg, 'chord', 0, 0, tiled=True)  3.53 us
    pallas_call x1, Pallas kernels, per_device(): pl.pallas_call(down_kernel, out_shape=(shape(4, N, 8, 128), shape(16 * RO...  3.23 us
  transfers between devices with their start and end apart: 3, of which 3 were waited for; matrix products, arithmetic and copies ran while one was open for 0% of the time, Pallas kernels for 1%

profile of v1, /device:TPU:1, one launch (start us, length us, event | category | flops | bytes accessed | tf_op | source)
XLA Modules:
  0.0 116.7 jit_solution(5737962253427816661)
XLA Ops:
  0.0 0.0 copy-start
  0.0 26.8 %pack.1 = (f32[105,16,128]{2,1,0:T(8,128)}, f32[5,16,128]{2,1,0:T(8,128)}) custom-call(f32[5]{0:T(128)} %jet.1, f32[5,32,128]{2,1,0:T(8,128)} %bitcast.27, s32[32,128]{1,0:T(8,128)} %bitcast.28, f32[25,32,128]{2,1,0:T(8,128)} %bitcast.23, f32[25,32,128]{2,1,0:T(8,128)} %bitcast.25, f32[25,32,128]{2,1,0:T(8,128)} %bitcast.15, f32[25,32,128]{2,1,0:T(8,128)} %bitcast.19), custom_call_target="tpu_custom_call" | custom-call | tf_op jit(solution)/shard_map/pack/pallas_call | solution.py:440
  26.8 8.8 %collective-permute-start = (f32[105,16,128]{2,1,0:T(8,128)}, f32[105,16,128]{2,1,0:T(8,128)S(1)}, u32[]{:S(2)}, u32[]{:S(2)}) collective-permute-start(f32[105,16,128]{2,1,0:T(8,128)} %get-tuple-element.14), channel_id=1, source_target_pairs={{0,1},{1,0},{2,3},{3,2},{4,5},{5,4},{6,7},{7,6},{8,9},{9,8},{10,11... | collective-permute-start | bytes 2580488 | tf_op jit(solution)/shard_map/ppermute | solution.py:455
  35.6 2.2 %collective-permute-done.recv = f32[105,16,128]{2,1,0:T(8,128)S(1)} collective-permute-done((f32[105,16,128]{2,1,0:T(8,128)}, f32[105,16,128]{2,1,0:T(8,128)S(1)}, u32[]{:S(2)}, u32[]{:S(2)}) %collective-permute-start) | collective-permute-done | bytes 860192 | tf_op jit(solution)/shard_map/ppermute | solution.py:455
  37.8 4.0 %chord_up.1 = (f32[16,24,128]{2,1,0:T(8,128)}, f32[730,8,128]{2,1,0:T(8,128)}) custom-call(f32[5,16,128]{2,1,0:T(8,128)} %get-tuple-element.13.src, f32[25,32,128]{2,1,0:T(8,128)} %bitcast.24, f32[25,32,128]{2,1,0:T(8,128)} %bitcast.26, f32[105,16,128]{2,1,0:T(8,128)S(1)} %collective-permute-done.recv), custom_call_target="tpu_custom_call" | custom-call | tf_op jit(solution)/shard_map/chord_up/pallas_call | solution.py:456
  41.8 3.5 %all-to-all-start = ((f32[16,24,128]{2,1,0:T(8,128)}), f32[16,24,128]{2,1,0:T(8,128)S(1)}, u32[]{:S(2)}, u32[]{:S(2)}) async-start(f32[16,24,128]{2,1,0:T(8,128)} %get-tuple-element.15), calls=%async_computation | async-start | bytes 393216 | tf_op jit(solution)/shard_map/all_to_all | solution.py:484
  45.3 1.6 %wall_blocks.1.zin = f32[768,128]{1,0:T(8,128)S(1)} custom-call(f32[25,32,128]{2,1,0:T(8,128)} %bitcast.16, f32[25,32,128]{2,1,0:T(8,128)} %bitcast.20, f32[105,16,128]{2,1,0:T(8,128)S(1)} %collective-permute-done.recv), custom_call_target="tpu_custom_call" | custom-call | flops 2304000 | bytes 2097152 | tf_op jit(solution)/shard_map/wall_blocks/pallas_call | solution.py:474
  46.9 6.1 %all-to-all-done.got = f32[16,24,128]{2,1,0:T(8,128)S(1)} async-done(((f32[16,24,128]{2,1,0:T(8,128)}), f32[16,24,128]{2,1,0:T(8,128)S(1)}, u32[]{:S(2)}, u32[]{:S(2)}) %all-to-all-start) | async-done | bytes 196640 | tf_op jit(solution)/shard_map/all_to_all | solution.py:484
  53.0 0.0 copy-done
  53.0 3.2 %chord_down.1 = (f32[4,5,8,128]{3,2,1,0:T(8,128)S(1)}, f32[768,128]{1,0:T(8,128)S(1)}) custom-call(f32[3,5]{1,0:T(4,128)S(1)} %copy-done, s32[16,128]{1,0:T(8,128)} %flags.1, f32[16,24,128]{2,1,0:T(8,128)S(1)} %all-to-all-done.got, f32[730,8,128]{2,1,0:T(8,128)} %get-tuple-element.16.store, ...), custom_call_target="tpu_custom_call", output_to_operand_aliasing={{1}: (7, {})} | custom-call | tf_op jit(solution)/shard_map/chord_down/pallas_call | solution.py:485
  56.2 28.6 %all_to_all.15 = f32[16,48,128]{2,1,0:T(8,128)S(1)} all-to-all(f32[16,48,128]{2,1,0:T(8,128)S(1)} %bitcast.11), channel_id=1, replica_groups={{0,2,4,6,8,10,12,14,16,18,20,22,24,26,28,30},{1,3,5,7,9,11,13,15,17,19,..., dimensions={0} | all-to-all | bytes 786432 | tf_op jit(solution)/shard_map/all_to_all | solution.py:437
  84.9 0.4 wall_solve.1
  85.3 23.8 %all_to_all.16 = f32[16,8,128]{2,1,0:T(8,128)S(1)} all-to-all(f32[16,8,128]{2,1,0:T(8,128)S(1)} %bitcast.14), channel_id=1, replica_groups={{0,2,4,6,8,10,12,14,16,18,20,22,24,26,28,30},{1,3,5,7,9,11,13,15,17,19,..., dimensions={0} | all-to-all | bytes 131072 | tf_op jit(solution)/shard_map/all_to_all | solution.py:437
  109.1 1.2 finish.1
  110.2 5.0 %collective-permute-start.1 = (f32[5,16,128]{2,1,0:T(8,128)S(1)}, f32[5,16,128]{2,1,0:T(8,128)S(1)}, u32[]{:S(2)}, u32[]{:S(2)}) collective-permute-start(f32[5,16,128]{2,1,0:T(8,128)S(1)} %get-tuple-element.20), channel_id=1, source_target_pairs={{0,1},{1,0},{2,3},{3,2},{4,5},{5,4},{6,7},{7,6},{8,9},{9,8},{10,11... | collective-permute-start | bytes 122888 | tf_op jit(solution)/shard_map/ppermute | solution.py:525
  115.2 0.8 collective-permute-done.1
  116.1 0.6 pad_maximum_fusion
  (1 shorter events, 0.0 us)
Async XLA Ops:
  0.0 53.0 %copy-start = (f32[3,5]{1,0:T(4,128)S(1)}, f32[3,5]{1,0:T(4,128)}, u32[]{:S(2)}) copy-start(f32[3,5]{1,0:T(4,128)} %table.1) | copy-start | bytes 184
  26.8 11.0 %collective-permute-start = (f32[105,16,128]{2,1,0:T(8,128)}, f32[105,16,128]{2,1,0:T(8,128)S(1)}, u32[]{:S(2)}, u32[]{:S(2)}) collective-permute-start(f32[105,16,128]{2,1,0:T(8,128)} %get-tuple-element.14), channel_id=1, source_target_pairs={{0,1},{1,0},{2,3},{3,2},{4,5},{5,4},{6,7},{7,6},{8,9},{9,8},{10,11... | collective-permute-start | bytes 2580488 | tf_op jit(solution)/shard_map/ppermute | solution.py:455
  41.8 11.2 %all-to-all-start = ((f32[16,24,128]{2,1,0:T(8,128)}), f32[16,24,128]{2,1,0:T(8,128)S(1)}, u32[]{:S(2)}, u32[]{:S(2)}) async-start(f32[16,24,128]{2,1,0:T(8,128)} %get-tuple-element.15), calls=%async_computation | async-start | bytes 393216 | tf_op jit(solution)/shard_map/all_to_all | solution.py:484
  110.2 5.8 %collective-permute-start.1 = (f32[5,16,128]{2,1,0:T(8,128)S(1)}, f32[5,16,128]{2,1,0:T(8,128)S(1)}, u32[]{:S(2)}, u32[]{:S(2)}) collective-permute-start(f32[5,16,128]{2,1,0:T(8,128)S(1)} %get-tuple-element.20), channel_id=1, source_target_pairs={{0,1},{1,0},{2,3},{3,2},{4,5},{5,4},{6,7},{7,6},{8,9},{9,8},{10,11... | collective-permute-start | bytes 122888 | tf_op jit(solution)/shard_map/ppermute | solution.py:525

commit v2 on v1

--- a/solution.py
+++ b/solution.py
@@ -14,7 +14,6 @@
 VM = pl.BlockSpec(memory_space=pltpu.VMEM)
 SM = pl.BlockSpec(memory_space=pltpu.SMEM)
 LIMIT = 32 << 20
-WIDE = 60 << 20
 LEAF = 220
 STORE = LEAF + 510
 
@@ -77,28 +76,26 @@
         c.wait()
 
 
-def pack_kernel(jet, rhs, mask, xl, xu, el, eu, send, src, rv, mk, out, own, sem):
+def pack_kernel(jet, rhs, mask, xl, xu, el, eu, send, keep, rv, mk, sem):
     _, _, core = place()
-    off = pl.multiple_of((1 - core) * 16, 16)
-    first = [pltpu.make_async_copy(rhs, rv, sem.at[5]), pltpu.make_async_copy(mask, mk, sem.at[6])]
-    copies = [
-        pltpu.make_async_copy(ref.at[:, pl.ds(off, 16), :], send.at[pl.ds(25 * n, 25)], sem.at[n])
-        for n, ref in enumerate((xl, xu, el, eu))
-    ]
-    for c in first + copies:
+    copies = [pltpu.make_async_copy(rhs, rv, sem.at[8]), pltpu.make_async_copy(mask, mk, sem.at[9])]
+    halves = ((send, pl.multiple_of((1 - core) * 16, 16)), (keep, pl.multiple_of(core * 16, 16)))
+    for m, (dst, off) in enumerate(halves):
+        for n, ref in enumerate((xl, xu, el, eu)):
+            copies.append(
+                pltpu.make_async_copy(
+                    ref.at[:, pl.ds(off, 16), :], dst.at[pl.ds(25 * n, 25)], sem.at[4 * m + n]
+                )
+            )
+    for c in copies:
         c.start()
-    for c in first:
-        c.wait()
-    keep = pl.multiple_of(core * 16, 16)
-    for dst, at in ((out, off), (own, keep)):
-        m = mk[pl.ds(at, 16), :].astype(F32)
+    copies[0].wait()
+    copies[1].wait()
+    for dst, off in halves:
+        m = mk[pl.ds(off, 16), :].astype(F32)
         for c in range(N):
-            dst[c] = rv[c, pl.ds(at, 16), :] + m * jet[c]
-    copies.append(pltpu.make_async_copy(out, send.at[pl.ds(100, N)], sem.at[4]))
-    copies.append(pltpu.make_async_copy(own, src, sem.at[7]))
-    for c in copies[4:]:
-        c.start()
-    for c in copies:
+            dst[100 + c] = rv[c, pl.ds(off, 16), :] + m * jet[c]
+    for c in copies[2:]:
         c.wait()
 
 
@@ -127,17 +124,13 @@
     return flat(n[0]) + list(n[1]) + flat(n[2]) + list(n[3]) + flat(n[4])
 
 
-def up_kernel(src, xl, xu, recv, msg, store, sl, su, ss, n1, n2, leaf, tree, sem):
+def up_kernel(keep, recv, msg, store, sl, su, ss, n1, n2, leaf, tree, sem):
     _, _, core = place()
-    off = pl.multiple_of(core * 16, 16)
-    copies = [
-        pltpu.make_async_copy(xl.at[:, pl.ds(off, 16), :], sl.at[:, core], sem.at[0]),
-        pltpu.make_async_copy(xu.at[:, pl.ds(off, 16), :], su.at[:, core], sem.at[1]),
-        pltpu.make_async_copy(recv.at[pl.ds(0, 25)], sl.at[:, 1 - core], sem.at[2]),
-        pltpu.make_async_copy(recv.at[pl.ds(25, 25)], su.at[:, 1 - core], sem.at[3]),
-        pltpu.make_async_copy(recv.at[pl.ds(100, N)], ss.at[:, 1 - core], sem.at[4]),
-        pltpu.make_async_copy(src, ss.at[:, core], sem.at[13]),
-    ]
+    copies = []
+    for n, (dst, first, count) in enumerate(((sl, 0, 25), (su, 25, 25), (ss, 100, N))):
+        part = pl.ds(first, count)
+        copies.append(pltpu.make_async_copy(keep.at[part], dst.at[:, core], sem.at[2 * n]))
+        copies.append(pltpu.make_async_copy(recv.at[part], dst.at[:, 1 - core], sem.at[2 * n + 1]))
     copy_all(copies)
     lane = lane_iota()
     even = lane % 2 == 0
@@ -156,7 +149,7 @@
         for c, x in enumerate(l1 + v1 + l2 + v2 + u1 + u2):
             leaf[r, c] = x
         dst = store.at[pl.ds(110 * r, 110)]
-        saves.append(pltpu.make_async_copy(leaf.at[r], dst, sem.at[5 + r]))
+        saves.append(pltpu.make_async_copy(leaf.at[r], dst, sem.at[6 + r]))
         saves[-1].start()
         l1, l2, u1, u2 = square(l1), square(l2), square(u1), square(u2)
         lb = mm(l2, l1)
@@ -179,7 +172,7 @@
         for c in range(30, 85):
             tree[level, c] = right[c]
         dst = store.at[pl.ds(LEAF + 85 * level, 85)]
-        saves.append(pltpu.make_async_copy(tree.at[level], dst, sem.at[7 + level]))
+        saves.append(pltpu.make_async_copy(tree.at[level], dst, sem.at[8 + level]))
         saves[-1].start()
         for c, x in enumerate(values_of(compose(node(left), node(right)))):
             n2[c] = x
@@ -195,11 +188,10 @@
         c.wait()
 
 
-def eta_copies(el, eu, recv, sl, su, core, sem):
-    off = pl.multiple_of(core * 16, 16)
+def eta_copies(keep, recv, sl, su, core, sem):
     return [
-        pltpu.make_async_copy(el.at[:, pl.ds(off, 16), :], sl.at[:, core], sem.at[0]),
-        pltpu.make_async_copy(eu.at[:, pl.ds(off, 16), :], su.at[:, core], sem.at[1]),
+        pltpu.make_async_copy(keep.at[pl.ds(50, 25)], sl.at[:, core], sem.at[0]),
+        pltpu.make_async_copy(keep.at[pl.ds(75, 25)], su.at[:, core], sem.at[1]),
         pltpu.make_async_copy(recv.at[pl.ds(50, 25)], sl.at[:, 1 - core], sem.at[2]),
         pltpu.make_async_copy(recv.at[pl.ds(75, 25)], su.at[:, 1 - core], sem.at[3]),
     ]
@@ -213,9 +205,9 @@
     return jnp.where(first, x, roll(y, 64)), jnp.where(first, roll(x, 64), y)
 
 
-def wall_kernel(el, eu, recv, out, sl, su, sem):
+def wall_kernel(keep, recv, out, sl, su, sem):
     _, _, core = place()
-    copy_all(eta_copies(el, eu, recv, sl, su, core, sem))
+    copy_all(eta_copies(keep, recv, sl, su, core, sem))
     first = lane_iota() < 64
     lb = cell(sl, 0)
     w = lb
@@ -232,11 +224,11 @@
 
 
 def down_kernel(
-    table, flags, got, store, el, eu, recv, zin, scaled, zout,
+    table, flags, got, store, keep, recv, zin, scaled, zout,
     sl, su, lf, tr, cs, bh, vb, fl, sem,
 ):
     chord, z, core = place()
-    eta = eta_copies(el, eu, recv, sl, su, core, sem)
+    eta = eta_copies(keep, recv, sl, su, core, sem)
     pre = [
         pltpu.make_async_copy(store.at[pl.ds(LEAF, 510)], tr, sem.at[4]),
         pltpu.make_async_copy(store.at[pl.ds(0, LEAF)], lf, sem.at[5]),
@@ -251,14 +243,14 @@
         v = [got[s, 8 * g : 8 * g + 8, :] for s in range(16)]
         for bit in range(4):
             step = 1 << bit
-            keep = (group // step) % 2 == 0
+            same = (group // step) % 2 == 0
             fresh = list(v)
             for s in range(16):
                 if s & step:
                     continue
                 a, b = v[s], v[s | step]
-                fresh[s] = jnp.where(keep, a, roll(b, 4 * step))
-                fresh[s | step] = jnp.where(keep, roll(a, -4 * step), b)
+                fresh[s] = jnp.where(same, a, roll(b, 4 * step))
+                fresh[s | step] = jnp.where(same, roll(a, -4 * step), b)
             v = fresh
         for lo in range(16):
             if 32 * g + lo < 85:
@@ -391,9 +383,9 @@
             b = mv(block(z, 25), b, f)
 
 
-def finish_kernel(got, scaled, el, eu, recv, own, send, sl, su, res, sem):
+def finish_kernel(got, scaled, keep, recv, own, send, sl, su, res, sem):
     _, _, core = place()
-    copies = eta_copies(el, eu, recv, sl, su, core, sem)
+    copies = eta_copies(keep, recv, sl, su, core, sem)
     for c in copies:
         c.start()
     first = lane_iota() < 64
@@ -437,26 +429,20 @@
         return lax.all_to_all(x, "wall", 0, 0, tiled=True, axis_index_groups=groups)
 
     side = pltpu.VMEM((25, 2, 16, 128), F32)
-    send, src = pl.pallas_call(
+    send, keep = pl.pallas_call(
         pack_kernel,
-        out_shape=(shape(105, 16, 128), pltpu.HBM((N, 16, 128), F32)),
+        out_shape=(shape(105, 16, 128), shape(105, 16, 128)),
         in_specs=[SM] + [HBM] * 6,
-        out_specs=(ANY, HBM),
-        scratch_shapes=[
-            pltpu.VMEM((N, 32, 128), F32),
-            pltpu.VMEM((32, 128), jnp.int32),
-            pltpu.VMEM((N, 16, 128), F32),
-            pltpu.VMEM((N, 16, 128), F32),
-            dma(8),
-        ],
-        compiler_params=params(WIDE),
+        out_specs=(VM, VM),
+        scratch_shapes=[pltpu.VMEM((N, 32, 128), F32), pltpu.VMEM((32, 128), jnp.int32), dma(10)],
+        compiler_params=params(),
         name="pack",
     )(jet_source, rhs, mask, xl, xu, el, eu)
     recv = lax.ppermute(send, "wall", swap)
     msg, store = pl.pallas_call(
         up_kernel,
         out_shape=(shape(16, 24, 128), pltpu.HBM((STORE, 8, 128), F32)),
-        in_specs=[HBM, HBM, HBM, ANY],
+        in_specs=[ANY, ANY],
         out_specs=(VM, HBM),
         scratch_shapes=[
             side,
@@ -470,22 +456,22 @@
         ],
         compiler_params=params(),
         name="chord_up",
-    )(far(src, N, 16, 128), xl, xu, recv)
+    )(keep, recv)
     zmat = pl.pallas_call(
         wall_kernel,
         out_shape=shape(16 * ROWS, 128),
-        in_specs=[HBM, HBM, ANY],
+        in_specs=[ANY, ANY],
         out_specs=VM,
         scratch_shapes=[side, side, dma(4)],
         compiler_params=params(),
         cost_estimate=cost(3 * 250 * 3 * 1024, 2 << 20),
         name="wall_blocks",
-    )(el, eu, recv)
+    )(keep, recv)
     got = lax.all_to_all(msg, "chord", 0, 0, tiled=True)
     scaled, zmsg = pl.pallas_call(
         down_kernel,
         out_shape=(shape(4, N, 8, 128), shape(16 * ROWS, 128)),
-        in_specs=[SM, HBM, VM, HBM, HBM, HBM, ANY, ANY],
+        in_specs=[SM, HBM, VM, HBM, ANY, ANY, ANY],
         out_specs=(VM, ANY),
         scratch_shapes=[
             side,
@@ -498,10 +484,10 @@
             pltpu.VMEM((16, 128), jnp.int32),
             dma(23),
         ],
-        input_output_aliases={7: 1},
+        input_output_aliases={6: 1},
         compiler_params=params(),
         name="chord_down",
-    )(bc_table, flags, got, far(store, STORE, 8, 128), el, eu, recv, zmat)
+    )(bc_table, flags, got, far(store, STORE, 8, 128), keep, recv, zmat)
     zgot = over_z(zmsg.reshape(16, ROWS, 128)).reshape(16 * ROWS, 128)
     back = pl.pallas_call(
         solve_kernel,
@@ -516,12 +502,12 @@
     own, other = pl.pallas_call(
         finish_kernel,
         out_shape=(shape(N, 16, 128), shape(N, 16, 128)),
-        in_specs=[VM, VM, HBM, HBM, ANY],
+        in_specs=[VM, VM, ANY, ANY],
         out_specs=(VM, VM),
         scratch_shapes=[side, side, pltpu.VMEM((N, 2, 16, 128), F32), dma(4)],
         compiler_params=params(),
         name="finish",
-    )(inflow, scaled, el, eu, recv)
+    )(inflow, scaled, keep, recv)
     other = lax.ppermute(other, "wall", swap)
     core = lax.axis_index("wall") % 2
     low = jnp.where(core == 0, own, other)

time: 117 us -> 91.2 us (0.78)
  Pallas kernels: 37.1 us -> 9.83 us
    pallas_call x2, Pallas kernels: 28.4 us -> 2.84 us  [the longest x1 2.16 us: per_device(): pl.pallas_call(pack_kernel, out_shape=(shape(105, 16, 128), shape(105, 16...]
where the time goes in v2:
time: 91.2 us; the launch traced here: 90.8 us
  blocking collectives  52.4 us (57%)
  starting transfers between devices  17.3 us (19%)
  waiting for transfers between devices  9.85 us (11%)
  Pallas kernels  9.83 us (11%)
    all_to_all x2, blocking collectives, over_z(): return lax.all_to_all(x, 'wall', 0, 0, tiled=True, axis_index_groups=groups)  52.4 us
    ppermute x1, starting transfers between devices, per_device(): recv = lax.ppermute(send, 'wall', swap)  8.79 us
    all_to_all x1, waiting for transfers between devices, per_device(): got = lax.all_to_all(msg, 'chord', 0, 0, tiled=True)  7.01 us
    ppermute x1, starting transfers between devices, per_device(): other = lax.ppermute(other, 'wall', swap)  4.97 us
    all_to_all x1, starting transfers between devices, per_device(): got = lax.all_to_all(msg, 'chord', 0, 0, tiled=True)  3.53 us
    pallas_call x1, Pallas kernels, per_device(): pl.pallas_call(down_kernel, out_shape=(shape(4, N, 8, 128), shape(16 * RO...  3.23 us
    pallas_call x1, Pallas kernels, per_device(): pl.pallas_call(up_kernel, out_shape=(shape(16, 24, 128), pltpu.HBM((STORE...  3.03 us
    pallas_call x1, Pallas kernels, per_device(): pl.pallas_call(pack_kernel, out_shape=(shape(105, 16, 128), shape(105, 16...  2.16 us
  transfers between devices with their start and end apart: 3, of which 3 were waited for; matrix products, arithmetic and copies ran while one was open for 0% of the time, Pallas kernels for 1%

profile of v2, /device:TPU:1, one launch (start us, length us, event | category | flops | bytes accessed | tf_op | source)
XLA Modules:
  0.0 90.8 jit_solution(10687564442592417697)
XLA Ops:
  0.0 0.0 copy-start
  0.0 0.0 copy-start.1
  0.0 0.7 copy-done.1
  0.7 2.2 %pack.1 = (f32[105,16,128]{2,1,0:T(8,128)S(1)}, f32[105,16,128]{2,1,0:T(8,128)S(1)}) custom-call(f32[5]{0:T(128)S(1)} %copy-done.1, f32[5,32,128]{2,1,0:T(8,128)} %bitcast.19, s32[32,128]{1,0:T(8,128)} %bitcast.20, f32[25,32,128]{2,1,0:T(8,128)} %bitcast.15, f32[25,32,128]{2,1,0:T(8,128)} %bitcast.16, f32[25,32,128]{2,1,0:T(8,128)} %bitcast.17, ...), custom_call_target="tpu_custom_call" | custom-call | tf_op jit(solution)/shard_map/pack/pallas_call | solution.py:432
  2.8 8.8 %collective-permute-start = (f32[105,16,128]{2,1,0:T(8,128)S(1)}, f32[105,16,128]{2,1,0:T(8,128)S(1)}, u32[]{:S(2)}, u32[]{:S(2)}) collective-permute-start(f32[105,16,128]{2,1,0:T(8,128)S(1)} %get-tuple-element.14), channel_id=1, source_target_pairs={{0,1},{1,0},{2,3},{3,2},{4,5},{5,4},{6,7},{7,6},{8,9},{9,8},{10,11... | collective-permute-start | bytes 2580488 | tf_op jit(solution)/shard_map/ppermute | solution.py:441
  11.6 2.0 %collective-permute-done.recv = f32[105,16,128]{2,1,0:T(8,128)S(1)} collective-permute-done((f32[105,16,128]{2,1,0:T(8,128)S(1)}, f32[105,16,128]{2,1,0:T(8,128)S(1)}, u32[]{:S(2)}, u32[]{:S(2)}) %collective-permute-start) | collective-permute-done | bytes 860192 | tf_op jit(solution)/shard_map/ppermute | solution.py:441
  13.6 3.0 %chord_up.1 = (f32[16,24,128]{2,1,0:T(8,128)}, f32[730,8,128]{2,1,0:T(8,128)}) custom-call(f32[105,16,128]{2,1,0:T(8,128)S(1)} %get-tuple-element.13.keep, f32[105,16,128]{2,1,0:T(8,128)S(1)} %collective-permute-done.recv), custom_call_target="tpu_custom_call" | custom-call | tf_op jit(solution)/shard_map/chord_up/pallas_call | solution.py:442
  16.7 3.5 %all-to-all-start = ((f32[16,24,128]{2,1,0:T(8,128)}), f32[16,24,128]{2,1,0:T(8,128)S(1)}, u32[]{:S(2)}, u32[]{:S(2)}) async-start(f32[16,24,128]{2,1,0:T(8,128)} %get-tuple-element.15), calls=%async_computation | async-start | bytes 393216 | tf_op jit(solution)/shard_map/all_to_all | solution.py:470
  20.2 0.7 wall_blocks.1.zin
  20.9 7.0 %all-to-all-done.got = f32[16,24,128]{2,1,0:T(8,128)S(1)} async-done(((f32[16,24,128]{2,1,0:T(8,128)}), f32[16,24,128]{2,1,0:T(8,128)S(1)}, u32[]{:S(2)}, u32[]{:S(2)}) %all-to-all-start) | async-done | bytes 196640 | tf_op jit(solution)/shard_map/all_to_all | solution.py:470
  27.9 0.0 copy-done
  27.9 3.2 %chord_down.1 = (f32[4,5,8,128]{3,2,1,0:T(8,128)S(1)}, f32[768,128]{1,0:T(8,128)S(1)}) custom-call(f32[3,5]{1,0:T(4,128)S(1)} %copy-done, s32[16,128]{1,0:T(8,128)} %flags.1, f32[16,24,128]{2,1,0:T(8,128)S(1)} %all-to-all-done.got, f32[730,8,128]{2,1,0:T(8,128)} %get-tuple-element.16.store, ...), custom_call_target="tpu_custom_call", output_to_operand_aliasing={{1}: (6, {})} | custom-call | tf_op jit(solution)/shard_map/chord_down/pallas_call | solution.py:471
  31.1 28.6 %all_to_all.15 = f32[16,48,128]{2,1,0:T(8,128)S(1)} all-to-all(f32[16,48,128]{2,1,0:T(8,128)S(1)} %bitcast.11), channel_id=1, replica_groups={{0,2,4,6,8,10,12,14,16,18,20,22,24,26,28,30},{1,3,5,7,9,11,13,15,17,19,..., dimensions={0} | all-to-all | bytes 786432 | tf_op jit(solution)/shard_map/all_to_all | solution.py:429
  59.8 0.4 wall_solve.1
  60.2 23.8 %all_to_all.16 = f32[16,8,128]{2,1,0:T(8,128)S(1)} all-to-all(f32[16,8,128]{2,1,0:T(8,128)S(1)} %bitcast.14), channel_id=1, replica_groups={{0,2,4,6,8,10,12,14,16,18,20,22,24,26,28,30},{1,3,5,7,9,11,13,15,17,19,..., dimensions={0} | all-to-all | bytes 131072 | tf_op jit(solution)/shard_map/all_to_all | solution.py:429
  84.0 0.3 finish.1
  84.3 5.0 %collective-permute-start.1 = (f32[5,16,128]{2,1,0:T(8,128)S(1)}, f32[5,16,128]{2,1,0:T(8,128)S(1)}, u32[]{:S(2)}, u32[]{:S(2)}) collective-permute-start(f32[5,16,128]{2,1,0:T(8,128)S(1)} %get-tuple-element.20), channel_id=1, source_target_pairs={{0,1},{1,0},{2,3},{3,2},{4,5},{5,4},{6,7},{7,6},{8,9},{9,8},{10,11... | collective-permute-start | bytes 122888 | tf_op jit(solution)/shard_map/ppermute | solution.py:511
  89.3 0.8 collective-permute-done.1
  90.1 0.6 pad_maximum_fusion
  (1 shorter events, 0.0 us)
Async XLA Ops:
  0.0 27.9 %copy-start = (f32[3,5]{1,0:T(4,128)S(1)}, f32[3,5]{1,0:T(4,128)}, u32[]{:S(2)}) copy-start(f32[3,5]{1,0:T(4,128)} %table.1) | copy-start | bytes 184
  0.0 0.7 copy-start.1
  2.8 10.8 %collective-permute-start = (f32[105,16,128]{2,1,0:T(8,128)S(1)}, f32[105,16,128]{2,1,0:T(8,128)S(1)}, u32[]{:S(2)}, u32[]{:S(2)}) collective-permute-start(f32[105,16,128]{2,1,0:T(8,128)S(1)} %get-tuple-element.14), channel_id=1, source_target_pairs={{0,1},{1,0},{2,3},{3,2},{4,5},{5,4},{6,7},{7,6},{8,9},{9,8},{10,11... | collective-permute-start | bytes 2580488 | tf_op jit(solution)/shard_map/ppermute | solution.py:441
  16.7 11.2 %all-to-all-start = ((f32[16,24,128]{2,1,0:T(8,128)}), f32[16,24,128]{2,1,0:T(8,128)S(1)}, u32[]{:S(2)}, u32[]{:S(2)}) async-start(f32[16,24,128]{2,1,0:T(8,128)} %get-tuple-element.15), calls=%async_computation | async-start | bytes 393216 | tf_op jit(solution)/shard_map/all_to_all | solution.py:470
  84.3 5.8 %collective-permute-start.1 = (f32[5,16,128]{2,1,0:T(8,128)S(1)}, f32[5,16,128]{2,1,0:T(8,128)S(1)}, u32[]{:S(2)}, u32[]{:S(2)}) collective-permute-start(f32[5,16,128]{2,1,0:T(8,128)S(1)} %get-tuple-element.20), channel_id=1, source_target_pairs={{0,1},{1,0},{2,3},{3,2},{4,5},{5,4},{6,7},{7,6},{8,9},{9,8},{10,11... | collective-permute-start | bytes 122888 | tf_op jit(solution)/shard_map/ppermute | solution.py:511

commit v3 on v2

--- a/solution.py
+++ b/solution.py
@@ -7,8 +7,8 @@
 
 F32 = jnp.float32
 N = 5
-ROWS = 48
-VEC = 40
+ROWS = 24
+VEC = 19
 ANY = pl.BlockSpec(memory_space=pl.ANY)
 HBM = pl.BlockSpec(memory_space=pltpu.HBM)
 VM = pl.BlockSpec(memory_space=pltpu.VMEM)
@@ -208,7 +208,6 @@
 def wall_kernel(keep, recv, out, sl, su, sem):
     _, _, core = place()
     copy_all(eta_copies(keep, recv, sl, su, core, sem))
-    first = lane_iota() < 64
     lb = cell(sl, 0)
     w = lb
     ub = cell(su, 0)
@@ -216,16 +215,48 @@
         lb = mm(cell(sl, j), lb)
         w = mm(ub, lb, w)
         ub = mm(ub, cell(su, j))
-    values = flat(lb) + flat(ub) + flat(w)
-    for r in range(38):
-        a, b = halves(values[r], values[r + 37], first)
-        out[pl.ds(r, 8, stride=ROWS), :] = a
-        out[pl.ds(8 * ROWS + r, 8, stride=ROWS), :] = b
+    for c, x in enumerate(flat(lb) + flat(ub) + flat(w)):
+        out[c] = x
+
+
+def pair_copies(mine, other, both, odd, sem):
+    return [
+        pltpu.make_async_copy(mine, both.at[odd], sem.at[0]),
+        pltpu.make_async_copy(other, both.at[1 - odd], sem.at[1]),
+    ]
+
+
+def pair_kernel(vecs, mine, other, out, give, both, comp, sem):
+    _, z, _ = place()
+    odd = z % 2
+    even = odd == 0
+    copy_all(pair_copies(mine, other, both, odd, sem))
+    lb_e, ub_e, w_e = [square([both[0, 25 * n + c] for c in range(25)]) for n in range(3)]
+    lb_o, ub_o, w_o = [square([both[1, 25 * n + c] for c in range(25)]) for n in range(3)]
+    w = mm(ub_e, mm(w_o, lb_e), w_e)
+    for c, x in enumerate(flat(mm(lb_o, lb_e)) + flat(mm(ub_e, ub_o)) + flat(w)):
+        comp[c] = x
+    lv = [vecs[c] for c in range(N)]
+    uv = [vecs[N + c] for c in range(N)]
+    for c in range(N):
+        give[c] = jnp.where(even, lv[c], uv[c])
+    new_lv = [jnp.where(even, x, y) for x, y in zip(mv(lb_o, lv), lv)]
+    inner = [jnp.where(even, x, y) for x, y in zip(mv(w_o, lv), uv)]
+    new_uv = [jnp.where(even, x + y, x) for x, y in zip(mv(ub_e, inner), uv)]
+    first = lane_iota() < 64
+    base = 37 * odd
+    for r in range(ROWS):
+        if r < VEC:
+            x, y = comp[base + r], comp[base + VEC + r]
+        else:
+            x, y = new_lv[r - VEC], new_uv[r - VEC]
+        x, y = halves(x, y, first)
+        out[pl.ds(r, 8, stride=ROWS), :] = x
+        out[pl.ds(8 * ROWS + r, 8, stride=ROWS), :] = y
 
 
 def down_kernel(
-    table, flags, got, store, keep, recv, zin, scaled, zout,
-    sl, su, lf, tr, cs, bh, vb, fl, sem,
+    table, flags, got, store, keep, recv, scaled, vecs, sl, su, lf, tr, cs, bh, fl, sem
 ):
     chord, z, core = place()
     eta = eta_copies(keep, recv, sl, su, core, sem)
@@ -233,7 +264,7 @@
         pltpu.make_async_copy(store.at[pl.ds(LEAF, 510)], tr, sem.at[4]),
         pltpu.make_async_copy(store.at[pl.ds(0, LEAF)], lf, sem.at[5]),
     ]
-    kinds = pltpu.make_async_copy(flags, fl, sem.at[22])
+    kinds = pltpu.make_async_copy(flags, fl, sem.at[6])
     kinds.start()
     for c in pre + eta:
         c.start()
@@ -332,61 +363,65 @@
     u = t[3]
     for j in range(2, -1, -1):
         u = mv(cell(su, j), u, t[j])
-    first = lane < 64
     for c in range(N):
-        x, y = halves(t[3][c], u[c], first)
-        vb[pl.ds(c, 8, stride=8), :] = x
-        vb[pl.ds(64 + c, 8, stride=8), :] = y
-    for c in range(N, 8):
-        vb[pl.ds(c, 8, stride=8), :] = zero
-        vb[pl.ds(64 + c, 8, stride=8), :] = zero
-    copy_all([
-        pltpu.make_async_copy(
-            vb.at[pl.ds(8 * d, 8)], zout.at[pl.ds(ROWS * d + VEC, 8)], sem.at[6 + d]
-        )
-        for d in range(16)
-    ])
+        vecs[c] = t[3][c]
+        vecs[N + c] = u[c]
 
 
 def solve_kernel(got, back, turned, ain):
     for n in range(16 * ROWS // 8):
         turned[8 * n : 8 * n + 8, :] = pltpu.roll(got[8 * n : 8 * n + 8, :], 64, 1)
 
-    def value(z, c):
-        ref = got if c < 37 else turned
-        row = ROWS * z + (c if c < 37 else c - 37)
-        return ref[row : row + 1, :]
-
-    def block(z, first):
-        return square([value(z, first + c) for c in range(25)])
-
-    def vec(z, ref):
-        return [ref[ROWS * z + VEC + c : ROWS * z + VEC + c + 1, :] for c in range(N)]
+    def value(pair, c):
+        odd = int(c > 37)
+        c -= 37 * odd
+        row = ROWS * (2 * pair + odd) + c % VEC
+        return (turned if c >= VEC else got)[row : row + 1, :]
+
+    def block(pair, first):
+        return square([value(pair, first + c) for c in range(25)])
+
+    def vec(pair, ref):
+        row = 2 * ROWS * pair + VEC
+        return [
+            ref[row + c : row + c + 1, :] + ref[row + ROWS + c : row + ROWS + c + 1, :]
+            for c in range(N)
+        ]
 
     zero = jnp.zeros((1, 128), F32)
     for n in range(16):
         back[8 * n : 8 * n + 8, :] = jnp.zeros((8, 128), F32)
     a = [zero] * N
-    for z in range(16):
+    for m in range(8):
         for c in range(N):
-            ain[8 * z + c : 8 * z + c + 1, :] = a[c]
-        if z < 15:
-            a = mv(block(z, 0), a, vec(z, got)) if z else vec(z, got)
+            ain[8 * m + c : 8 * m + c + 1, :] = a[c]
+        if m < 7:
+            a = mv(block(m, 0), a, vec(m, got)) if m else vec(m, got)
     first = lax.broadcasted_iota(jnp.int32, (1, 128), 1) < 64
     b = [zero] * N
-    for z in range(15, -1, -1):
-        a = [ain[8 * z + c : 8 * z + c + 1, :] for c in range(N)]
+    for m in range(7, -1, -1):
+        a = [ain[8 * m + c : 8 * m + c + 1, :] for c in range(N)]
         for c in range(N):
-            back[8 * z + c : 8 * z + c + 1, :] = jnp.where(first, a[c], pltpu.roll(b[c], 64, 1))
-        if z:
-            f = mv(block(z, 50), a, vec(z, turned))
-            b = mv(block(z, 25), b, f)
-
-
-def finish_kernel(got, scaled, keep, recv, own, send, sl, su, res, sem):
-    _, _, core = place()
+            x = jnp.where(first, a[c], pltpu.roll(b[c], 64, 1))
+            back[16 * m + c : 16 * m + c + 1, :] = x
+            back[16 * m + 8 + c : 16 * m + 8 + c + 1, :] = x
+        if m:
+            f = mv(block(m, 50), a, vec(m, turned))
+            b = mv(block(m, 25), b, f)
+
+
+def finish_kernel(
+    got, scaled, keep, recv, vecs, taken, mine, other, own, send, sl, su, res, both, sem
+):
+    _, z, core = place()
+    odd = z % 2
+    even = odd == 0
     copies = eta_copies(keep, recv, sl, su, core, sem)
-    for c in copies:
+    pair = [
+        pltpu.make_async_copy(mine, both.at[odd], sem.at[4]),
+        pltpu.make_async_copy(other, both.at[1 - odd], sem.at[5]),
+    ]
+    for c in pair + copies:
         c.start()
     first = lane_iota() < 64
     a, b = [], []
@@ -395,6 +430,14 @@
         y = got[pl.ds(64 + c, 8, stride=8), :]
         a.append(jnp.where(first, x, roll(y, 64)))
         b.append(jnp.where(first, roll(x, 64), y))
+    for c in pair:
+        c.wait()
+    lv_e = [jnp.where(even, vecs[c], taken[c]) for c in range(N)]
+    mid = mv(square([both[0, c] for c in range(25)]), a, lv_e)
+    low = mv(square([both[1, 50 + c] for c in range(25)]), mid, [taken[c] for c in range(N)])
+    low = mv(square([both[1, 25 + c] for c in range(25)]), b, low)
+    a = [jnp.where(even, x, y) for x, y in zip(a, mid)]
+    b = [jnp.where(even, x, y) for x, y in zip(low, b)]
     for c in copies:
         c.wait()
     lifted = []
@@ -423,6 +466,7 @@
     rhs, mask, flags = far(rhs, N, 32, 128), far(jet_mask, 32, 128), far(wall_flags, 16, 128)
     xl, xu, el, eu = (far(x, 25, 32, 128) for x in (xi_lower, xi_upper, eta_lower, eta_upper))
     swap = [(n, n ^ 1) for n in range(lax.axis_size("wall"))]
+    near = [(n, n ^ 2) for n in range(lax.axis_size("wall"))]
     groups = [list(range(c, lax.axis_size("wall"), 2)) for c in range(2)]
 
     def over_z(x):
@@ -457,9 +501,9 @@
         compiler_params=params(),
         name="chord_up",
     )(keep, recv)
-    zmat = pl.pallas_call(
+    mine = pl.pallas_call(
         wall_kernel,
-        out_shape=shape(16 * ROWS, 128),
+        out_shape=shape(75, 8, 128),
         in_specs=[ANY, ANY],
         out_specs=VM,
         scratch_shapes=[side, side, dma(4)],
@@ -467,12 +511,13 @@
         cost_estimate=cost(3 * 250 * 3 * 1024, 2 << 20),
         name="wall_blocks",
     )(keep, recv)
+    other = lax.ppermute(mine, "wall", near)
     got = lax.all_to_all(msg, "chord", 0, 0, tiled=True)
-    scaled, zmsg = pl.pallas_call(
+    scaled, vecs = pl.pallas_call(
         down_kernel,
-        out_shape=(shape(4, N, 8, 128), shape(16 * ROWS, 128)),
-        in_specs=[SM, HBM, VM, HBM, ANY, ANY, ANY],
-        out_specs=(VM, ANY),
+        out_shape=(shape(4, N, 8, 128), shape(2 * N, 8, 128)),
+        in_specs=[SM, HBM, VM, HBM, ANY, ANY],
+        out_specs=(VM, VM),
         scratch_shapes=[
             side,
             side,
@@ -480,15 +525,24 @@
             pltpu.VMEM((510, 8, 128), F32),
             pltpu.VMEM((85, 8, 128), F32),
             pltpu.VMEM((N, 2, 16, 128), F32),
-            pltpu.VMEM((128, 128), F32),
             pltpu.VMEM((16, 128), jnp.int32),
-            dma(23),
+            dma(7),
         ],
-        input_output_aliases={6: 1},
         compiler_params=params(),
         name="chord_down",
-    )(bc_table, flags, got, far(store, STORE, 8, 128), keep, recv, zmat)
+    )(bc_table, flags, got, far(store, STORE, 8, 128), keep, recv)
+    both = pltpu.VMEM((2, 75, 8, 128), F32)
+    zmsg, give = pl.pallas_call(
+        pair_kernel,
+        out_shape=(shape(16 * ROWS, 128), shape(N, 8, 128)),
+        in_specs=[VM, ANY, ANY],
+        out_specs=(VM, VM),
+        scratch_shapes=[both, pltpu.VMEM((75, 8, 128), F32), dma(2)],
+        compiler_params=params(),
+        name="wall_pair",
+    )(vecs, mine, other)
     zgot = over_z(zmsg.reshape(16, ROWS, 128)).reshape(16 * ROWS, 128)
+    taken = lax.ppermute(give, "wall", near)
     back = pl.pallas_call(
         solve_kernel,
         out_shape=shape(128, 128),
@@ -499,19 +553,19 @@
         name="wall_solve",
     )(zgot)
     inflow = over_z(back.reshape(16, 8, 128)).reshape(128, 128)
-    own, other = pl.pallas_call(
+    own, theirs = pl.pallas_call(
         finish_kernel,
         out_shape=(shape(N, 16, 128), shape(N, 16, 128)),
-        in_specs=[VM, VM, ANY, ANY],
+        in_specs=[VM, VM, ANY, ANY, VM, VM, ANY, ANY],
         out_specs=(VM, VM),
-        scratch_shapes=[side, side, pltpu.VMEM((N, 2, 16, 128), F32), dma(4)],
+        scratch_shapes=[side, side, pltpu.VMEM((N, 2, 16, 128), F32), both, dma(6)],
         compiler_params=params(),
         name="finish",
-    )(inflow, scaled, keep, recv)
-    other = lax.ppermute(other, "wall", swap)
+    )(inflow, scaled, keep, recv, vecs, taken, mine, other)
+    theirs = lax.ppermute(theirs, "wall", swap)
     core = lax.axis_index("wall") % 2
-    low = jnp.where(core == 0, own, other)
-    high = jnp.where(core == 0, other, own)
+    low = jnp.where(core == 0, own, theirs)
+    high = jnp.where(core == 0, theirs, own)
     return jnp.concatenate([low, high], axis=1).reshape(N, 16, 2, 128)
 
 

time: 91.2 us -> 86.1 us (0.944)
  blocking collectives: 52.4 us -> 36.2 us
  starting transfers between devices: 17.3 us -> 27 us
  waiting for transfers between devices: 9.85 us -> 11.2 us
    all_to_all x2 -> x1, blocking collectives: 52.4 us -> 26.2 us  [over_z(): return lax.all_to_all(x, 'wall', 0, 0, tiled=True, axis_index_groups=groups)]
    all_to_all x0 -> x1, blocking collectives: none -> 10 us  [per_device(): got = lax.all_to_all(msg, 'chord', 0, 0, tiled=True)]
    ppermute x1 -> x3, starting transfers between devices: 4.97 us -> 11.2 us  [the longest x1 6.01 us: per_device(): theirs = lax.ppermute(theirs, 'wall', swap)]
    all_to_all x1, starting transfers between devices: 3.53 us -> 7.02 us  [over_z(): return lax.all_to_all(x, 'wall', 0, 0, tiled=True, axis_index_groups=groups)]
    ppermute x1 -> x3, waiting for transfers between devices: 0.84 us -> 2.36 us  [the longest x1 1.52 us: per_device(): taken = lax.ppermute(give, 'wall', near)]
    pallas_call x2 -> x3, Pallas kernels: 3.9 us -> 3.84 us  [the longest x1 2.91 us: per_device(): pl.pallas_call(down_kernel, out_shape=(shape(4, N, 8, 128), shape(2 * N,...]
  transfers between devices with their start and end apart: 3 -> 5, of which waited for: 3 -> 4; matrix products, arithmetic and copies ran while one was open for 0% -> 0% of each run, Pallas kernels for 1% -> 6%
where the time goes in v3:
time: 86.1 us; the launch traced here: 85.6 us
  blocking collectives  36.2 us (42%)
  starting transfers between devices  27 us (31%)
  waiting for transfers between devices  11.2 us (13%)
  Pallas kernels  9.82 us (11%)
    all_to_all x1, blocking collectives, over_z(): return lax.all_to_all(x, 'wall', 0, 0, tiled=True, axis_index_groups=groups)  26.2 us
    all_to_all x1, blocking collectives, per_device(): got = lax.all_to_all(msg, 'chord', 0, 0, tiled=True)  10 us
    ppermute x1, starting transfers between devices, per_device(): recv = lax.ppermute(send, 'wall', swap)  8.79 us
    all_to_all x1, starting transfers between devices, over_z(): return lax.all_to_all(x, 'wall', 0, 0, tiled=True, axis_index_groups=groups)  7.02 us
    all_to_all x1, waiting for transfers between devices, over_z(): return lax.all_to_all(x, 'wall', 0, 0, tiled=True, axis_index_groups=groups)  6.89 us
    ppermute x1, starting transfers between devices, per_device(): theirs = lax.ppermute(theirs, 'wall', swap)  6.01 us
    ppermute x1, starting transfers between devices, per_device(): taken = lax.ppermute(give, 'wall', near)  3.26 us
    pallas_call x1, Pallas kernels, per_device(): pl.pallas_call(down_kernel, out_shape=(shape(4, N, 8, 128), shape(2 * N,...  2.91 us
  transfers between devices with their start and end apart: 5, of which 4 were waited for; matrix products, arithmetic and copies ran while one was open for 0% of the time, Pallas kernels for 6%

profile of v3, /device:TPU:1, one launch (start us, length us, event | category | flops | bytes accessed | tf_op | source)
XLA Modules:
  0.0 85.6 jit_solution(5446797716375695103)
XLA Ops:
  0.0 0.0 copy-start
  0.0 0.0 copy-start.1
  0.0 0.7 copy-done.1
  0.7 2.2 %pack.1 = (f32[105,16,128]{2,1,0:T(8,128)S(1)}, f32[105,16,128]{2,1,0:T(8,128)S(1)}) custom-call(f32[5]{0:T(128)S(1)} %copy-done.1, f32[5,32,128]{2,1,0:T(8,128)} %bitcast.18, s32[32,128]{1,0:T(8,128)} %bitcast.19, f32[25,32,128]{2,1,0:T(8,128)} %bitcast.14, f32[25,32,128]{2,1,0:T(8,128)} %bitcast.15, f32[25,32,128]{2,1,0:T(8,128)} %bitcast.16, ...), custom_call_target="tpu_custom_call" | custom-call | tf_op jit(solution)/shard_map/pack/pallas_call | solution.py:476
  2.8 8.8 %collective-permute-start = (f32[105,16,128]{2,1,0:T(8,128)S(1)}, f32[105,16,128]{2,1,0:T(8,128)S(1)}, u32[]{:S(2)}, u32[]{:S(2)}) collective-permute-start(f32[105,16,128]{2,1,0:T(8,128)S(1)} %get-tuple-element.16), channel_id=1, source_target_pairs={{0,1},{1,0},{2,3},{3,2},{4,5},{5,4},{6,7},{7,6},{8,9},{9,8},{10,11... | collective-permute-start | bytes 2580488 | tf_op jit(solution)/shard_map/ppermute | solution.py:485
  11.6 2.0 %collective-permute-done.recv = f32[105,16,128]{2,1,0:T(8,128)S(1)} collective-permute-done((f32[105,16,128]{2,1,0:T(8,128)S(1)}, f32[105,16,128]{2,1,0:T(8,128)S(1)}, u32[]{:S(2)}, u32[]{:S(2)}) %collective-permute-start) | collective-permute-done | bytes 860192 | tf_op jit(solution)/shard_map/ppermute | solution.py:485
  13.6 0.5 wall_blocks.1.mine
  14.1 1.9 %collective-permute-start.1 = (f32[75,8,128]{2,1,0:T(8,128)S(1)}, f32[75,8,128]{2,1,0:T(8,128)S(1)}, u32[]{:S(2)}, u32[]{:S(2)}) collective-permute-start(f32[75,8,128]{2,1,0:T(8,128)S(1)} %wall_blocks.1.mine), channel_id=1, source_target_pairs={{0,2},{1,3},{2,0},{3,1},{4,6},{5,7},{6,4},{7,5},{8,10},{9,11},{10,... | collective-permute-start | bytes 921608 | tf_op jit(solution)/shard_map/ppermute | solution.py:514
  16.0 2.4 %chord_up.1 = (f32[16,24,128]{2,1,0:T(8,128)S(1)}, f32[730,8,128]{2,1,0:T(8,128)}) custom-call(f32[105,16,128]{2,1,0:T(8,128)S(1)} %get-tuple-element.15.keep, f32[105,16,128]{2,1,0:T(8,128)S(1)} %collective-permute-done.recv), custom_call_target="tpu_custom_call" | custom-call | tf_op jit(solution)/shard_map/chord_up/pallas_call | solution.py:486
  18.4 10.0 %all_to_all.15.got = f32[16,24,128]{2,1,0:T(8,128)S(1)} all-to-all(f32[16,24,128]{2,1,0:T(8,128)S(1)} %get-tuple-element.17), channel_id=1, replica_groups=mesh['chord'=16,'wall'=32] {'chord'}, dimensions={0} | all-to-all | bytes 393216 | tf_op jit(solution)/shard_map/all_to_all | solution.py:515
  28.4 0.0 copy-done
  28.4 2.9 %chord_down.1 = (f32[4,5,8,128]{3,2,1,0:T(8,128)S(1)}, f32[10,8,128]{2,1,0:T(8,128)S(1)}) custom-call(f32[3,5]{1,0:T(4,128)S(1)} %copy-done, s32[16,128]{1,0:T(8,128)} %flags.1, f32[16,24,128]{2,1,0:T(8,128)S(1)} %all_to_all.15.got, f32[730,8,128]{2,1,0:T(8,128)} %get-tuple-element.18.store, f32[105,16,128]{2,1,0:T(8,128)S(1)} %get-tuple-element.15.keep, ...), custom_call_target="tpu_custom_call" | custom-call | tf_op jit(solution)/shard_map/chord_down/pallas_call | solution.py:516
  31.3 0.0 collective-permute-done.1.other
  31.3 0.5 wall_pair.1
  31.8 26.2 %all_to_all.16 = f32[16,24,128]{2,1,0:T(8,128)S(1)} all-to-all(f32[16,24,128]{2,1,0:T(8,128)S(1)} %bitcast.13), channel_id=1, replica_groups={{0,2,4,6,8,10,12,14,16,18,20,22,24,26,28,30},{1,3,5,7,9,11,13,15,17,19,..., dimensions={0} | all-to-all | bytes 393216 | tf_op jit(solution)/shard_map/all_to_all | solution.py:473
  58.0 0.9 %wall_solve.1 = f32[128,128]{1,0:T(8,128)} custom-call(f32[384,128]{1,0:T(8,128)S(1)} %bitcast.11), custom_call_target="tpu_custom_call" | custom-call | tf_op jit(solution)/shard_map/wall_solve/pallas_call | solution.py:546
  58.9 7.0 %all-to-all-start.2 = ((f32[16,8,128]{2,1,0:T(8,128)}), f32[16,8,128]{2,1,0:T(8,128)S(1)}, u32[]{:S(2)}, u32[]{:S(2)}) async-start(f32[16,8,128]{2,1,0:T(8,128)} %bitcast.8), calls=%async_computation.2 | async-start | bytes 131072 | tf_op jit(solution)/shard_map/all_to_all | solution.py:473
  65.9 3.3 %collective-permute-start.2 = (f32[5,8,128]{2,1,0:T(8,128)S(1)}, f32[5,8,128]{2,1,0:T(8,128)S(1)}, u32[]{:S(2)}, u32[]{:S(2)}) collective-permute-start(f32[5,8,128]{2,1,0:T(8,128)S(1)} %get-tuple-element.22), channel_id=1, source_target_pairs={{0,2},{1,3},{2,0},{3,1},{4,6},{5,7},{6,4},{7,5},{8,10},{9,11},{10,... | collective-permute-start | bytes 61448 | tf_op jit(solution)/shard_map/ppermute | solution.py:545
  69.2 1.5 %collective-permute-done.2.taken = f32[5,8,128]{2,1,0:T(8,128)S(1)} collective-permute-done((f32[5,8,128]{2,1,0:T(8,128)S(1)}, f32[5,8,128]{2,1,0:T(8,128)S(1)}, u32[]{:S(2)}, u32[]{:S(2)}) %collective-permute-start.2) | collective-permute-done | bytes 20512 | tf_op jit(solution)/shard_map/ppermute | solution.py:545
  70.7 6.9 %all-to-all-done.2 = f32[16,8,128]{2,1,0:T(8,128)S(1)} async-done(((f32[16,8,128]{2,1,0:T(8,128)}), f32[16,8,128]{2,1,0:T(8,128)S(1)}, u32[]{:S(2)}, u32[]{:S(2)}) %all-to-all-start.2) | async-done | bytes 65568 | tf_op jit(solution)/shard_map/all_to_all | solution.py:473
  77.6 0.5 finish.1
  78.1 6.0 %collective-permute-start.3 = (f32[5,16,128]{2,1,0:T(8,128)S(1)}, f32[5,16,128]{2,1,0:T(8,128)S(1)}, u32[]{:S(2)}, u32[]{:S(2)}) collective-permute-start(f32[5,16,128]{2,1,0:T(8,128)S(1)} %get-tuple-element.24), channel_id=1, source_target_pairs={{0,1},{1,0},{2,3},{3,2},{4,5},{5,4},{6,7},{7,6},{8,9},{9,8},{10,11... | collective-permute-start | bytes 122888 | tf_op jit(solution)/shard_map/ppermute | solution.py:565
  84.2 0.8 collective-permute-done.3
  85.0 0.6 pad_maximum_fusion
  (1 shorter events, 0.0 us)
Async XLA Ops:
  0.0 28.4 %copy-start = (f32[3,5]{1,0:T(4,128)S(1)}, f32[3,5]{1,0:T(4,128)}, u32[]{:S(2)}) copy-start(f32[3,5]{1,0:T(4,128)} %table.1) | copy-start | bytes 184
  0.0 0.7 copy-start.1
  2.8 10.8 %collective-permute-start = (f32[105,16,128]{2,1,0:T(8,128)S(1)}, f32[105,16,128]{2,1,0:T(8,128)S(1)}, u32[]{:S(2)}, u32[]{:S(2)}) collective-permute-start(f32[105,16,128]{2,1,0:T(8,128)S(1)} %get-tuple-element.16), channel_id=1, source_target_pairs={{0,1},{1,0},{2,3},{3,2},{4,5},{5,4},{6,7},{7,6},{8,9},{9,8},{10,11... | collective-permute-start | bytes 2580488 | tf_op jit(solution)/shard_map/ppermute | solution.py:485
  14.1 17.2 %collective-permute-start.1 = (f32[75,8,128]{2,1,0:T(8,128)S(1)}, f32[75,8,128]{2,1,0:T(8,128)S(1)}, u32[]{:S(2)}, u32[]{:S(2)}) collective-permute-start(f32[75,8,128]{2,1,0:T(8,128)S(1)} %wall_blocks.1.mine), channel_id=1, source_target_pairs={{0,2},{1,3},{2,0},{3,1},{4,6},{5,7},{6,4},{7,5},{8,10},{9,11},{10,... | collective-permute-start | bytes 921608 | tf_op jit(solution)/shard_map/ppermute | solution.py:514
  58.9 18.7 %all-to-all-start.2 = ((f32[16,8,128]{2,1,0:T(8,128)}), f32[16,8,128]{2,1,0:T(8,128)S(1)}, u32[]{:S(2)}, u32[]{:S(2)}) async-start(f32[16,8,128]{2,1,0:T(8,128)} %bitcast.8), calls=%async_computation.2 | async-start | bytes 131072 | tf_op jit(solution)/shard_map/all_to_all | solution.py:473
  65.9 4.8 %collective-permute-start.2 = (f32[5,8,128]{2,1,0:T(8,128)S(1)}, f32[5,8,128]{2,1,0:T(8,128)S(1)}, u32[]{:S(2)}, u32[]{:S(2)}) collective-permute-start(f32[5,8,128]{2,1,0:T(8,128)S(1)} %get-tuple-element.22), channel_id=1, source_target_pairs={{0,2},{1,3},{2,0},{3,1},{4,6},{5,7},{6,4},{7,5},{8,10},{9,11},{10,... | collective-permute-start | bytes 61448 | tf_op jit(solution)/shard_map/ppermute | solution.py:545
  78.1 6.9 %collective-permute-start.3 = (f32[5,16,128]{2,1,0:T(8,128)S(1)}, f32[5,16,128]{2,1,0:T(8,128)S(1)}, u32[]{:S(2)}, u32[]{:S(2)}) collective-permute-start(f32[5,16,128]{2,1,0:T(8,128)S(1)} %get-tuple-element.24), channel_id=1, source_target_pairs={{0,1},{1,0},{2,3},{3,2},{4,5},{5,4},{6,7},{7,6},{8,9},{9,8},{10,11... | collective-permute-start | bytes 122888 | tf_op jit(solution)/shard_map/ppermute | solution.py:565

commit v4 on v3

--- a/solution.py
+++ b/solution.py
@@ -76,29 +76,6 @@
         c.wait()
 
 
-def pack_kernel(jet, rhs, mask, xl, xu, el, eu, send, keep, rv, mk, sem):
-    _, _, core = place()
-    copies = [pltpu.make_async_copy(rhs, rv, sem.at[8]), pltpu.make_async_copy(mask, mk, sem.at[9])]
-    halves = ((send, pl.multiple_of((1 - core) * 16, 16)), (keep, pl.multiple_of(core * 16, 16)))
-    for m, (dst, off) in enumerate(halves):
-        for n, ref in enumerate((xl, xu, el, eu)):
-            copies.append(
-                pltpu.make_async_copy(
-                    ref.at[:, pl.ds(off, 16), :], dst.at[pl.ds(25 * n, 25)], sem.at[4 * m + n]
-                )
-            )
-    for c in copies:
-        c.start()
-    copies[0].wait()
-    copies[1].wait()
-    for dst, off in halves:
-        m = mk[pl.ds(off, 16), :].astype(F32)
-        for c in range(N):
-            dst[100 + c] = rv[c, pl.ds(off, 16), :] + m * jet[c]
-    for c in copies[2:]:
-        c.wait()
-
-
 def compose(left, right):
     lb1, lv1, ub1, uv1, w1 = left
     lb2, lv2, ub2, uv2, w2 = right
@@ -124,21 +101,39 @@
     return flat(n[0]) + list(n[1]) + flat(n[2]) + list(n[3]) + flat(n[4])
 
 
-def up_kernel(keep, recv, msg, store, sl, su, ss, n1, n2, leaf, tree, sem):
-    _, _, core = place()
-    copies = []
-    for n, (dst, first, count) in enumerate(((sl, 0, 25), (su, 25, 25), (ss, 100, N))):
-        part = pl.ds(first, count)
-        copies.append(pltpu.make_async_copy(keep.at[part], dst.at[:, core], sem.at[2 * n]))
-        copies.append(pltpu.make_async_copy(recv.at[part], dst.at[:, 1 - core], sem.at[2 * n + 1]))
-    copy_all(copies)
+def up_kernel(
+    jet, rhs, mask, xl, xu, el, eu, msg, store, send, keep,
+    sl, su, ss, mk, n1, n2, leaf, tree, sem,
+):
+    core = place()[2]
+    copies = [
+        pltpu.make_async_copy(src, dst, sem.at[n])
+        for n, (src, dst) in enumerate(((rhs, ss), (mask, mk), (xl, sl), (xu, su)))
+    ]
+    for c in copies:
+        c.start()
+    copies[0].wait()
+    copies[1].wait()
+    m = mk[...].astype(F32)
+    for c in range(N):
+        ss[c] = ss[c] + m * jet[c]
+    copies[2].wait()
+    copies[3].wait()
+    eta = []
+    for n, (dst, half) in enumerate(((send, 1 - core), (keep, core))):
+        off = pl.multiple_of(half * 16, 16)
+        for k, ref in enumerate((el, eu)):
+            part = dst.at[pl.ds(25 * k, 25)]
+            at = sem.at[14 + 2 * n + k]
+            eta.append(pltpu.make_async_copy(ref.at[:, pl.ds(off, 16), :], part, at))
+            eta[-1].start()
     lane = lane_iota()
     even = lane % 2 == 0
     low = (lane // 2) % 2 == 0
 
     def split(ref, c, r):
-        a = ref[c, r, 0:8, :]
-        b = ref[c, r, 8:16, :]
+        a = ref[c, 16 * r : 16 * r + 8, :]
+        b = ref[c, 16 * r + 8 : 16 * r + 16, :]
         return jnp.where(even, a, roll(b, 1)), jnp.where(even, roll(a, -1), b)
 
     saves = []
@@ -184,16 +179,16 @@
             acc = x if acc is None else jnp.where(group == pos, roll(x, 4 * pos), acc)
         for d in range(16):
             msg[d, 8 * g : 8 * g + 8, :] = acc
-    for c in saves:
+    for c in saves + eta:
         c.wait()
 
 
 def eta_copies(keep, recv, sl, su, core, sem):
     return [
-        pltpu.make_async_copy(keep.at[pl.ds(50, 25)], sl.at[:, core], sem.at[0]),
-        pltpu.make_async_copy(keep.at[pl.ds(75, 25)], su.at[:, core], sem.at[1]),
-        pltpu.make_async_copy(recv.at[pl.ds(50, 25)], sl.at[:, 1 - core], sem.at[2]),
-        pltpu.make_async_copy(recv.at[pl.ds(75, 25)], su.at[:, 1 - core], sem.at[3]),
+        pltpu.make_async_copy(keep.at[pl.ds(0, 25)], sl.at[:, core], sem.at[0]),
+        pltpu.make_async_copy(keep.at[pl.ds(25, 25)], su.at[:, core], sem.at[1]),
+        pltpu.make_async_copy(recv.at[pl.ds(0, 25)], sl.at[:, 1 - core], sem.at[2]),
+        pltpu.make_async_copy(recv.at[pl.ds(25, 25)], su.at[:, 1 - core], sem.at[3]),
     ]
 
 
@@ -219,27 +214,48 @@
         out[c] = x
 
 
-def pair_copies(mine, other, both, odd, sem):
+def sources(here, there, slots, core):
+    for c in range(N):
+        slots[c, core] = here[c]
+        slots[c, 1 - core] = there[c]
     return [
-        pltpu.make_async_copy(mine, both.at[odd], sem.at[0]),
-        pltpu.make_async_copy(other, both.at[1 - odd], sem.at[1]),
-    ]
-
-
-def pair_kernel(vecs, mine, other, out, give, both, comp, sem):
-    _, z, _ = place()
+        [slots[c, j // 2, pl.ds(j % 2, 8, stride=2), :] for c in range(N)] for j in range(4)
+    ]
+
+
+def pair_kernel(
+    here, there, keep, recv, mine, other, out, give, hold, sl, su, slots, both, comp, sem
+):
+    _, z, core = place()
     odd = z % 2
     even = odd == 0
-    copy_all(pair_copies(mine, other, both, odd, sem))
+    pair = [
+        pltpu.make_async_copy(mine, both.at[odd], sem.at[4]),
+        pltpu.make_async_copy(other, both.at[1 - odd], sem.at[5]),
+    ]
+    eta = eta_copies(keep, recv, sl, su, core, sem)
+    for c in eta + pair:
+        c.start()
+    s = sources(here, there, slots, core)
+    for c in eta:
+        c.wait()
+    t = [s[0]]
+    for j in range(1, 4):
+        t.append(mv(cell(sl, j), t[-1], s[j]))
+    lv = t[3]
+    uv = t[3]
+    for j in range(2, -1, -1):
+        uv = mv(cell(su, j), uv, t[j])
+    for c in pair:
+        c.wait()
     lb_e, ub_e, w_e = [square([both[0, 25 * n + c] for c in range(25)]) for n in range(3)]
     lb_o, ub_o, w_o = [square([both[1, 25 * n + c] for c in range(25)]) for n in range(3)]
     w = mm(ub_e, mm(w_o, lb_e), w_e)
     for c, x in enumerate(flat(mm(lb_o, lb_e)) + flat(mm(ub_e, ub_o)) + flat(w)):
         comp[c] = x
-    lv = [vecs[c] for c in range(N)]
-    uv = [vecs[N + c] for c in range(N)]
     for c in range(N):
         give[c] = jnp.where(even, lv[c], uv[c])
+        hold[c] = lv[c]
     new_lv = [jnp.where(even, x, y) for x, y in zip(mv(lb_o, lv), lv)]
     inner = [jnp.where(even, x, y) for x, y in zip(mv(w_o, lv), uv)]
     new_uv = [jnp.where(even, x + y, x) for x, y in zip(mv(ub_e, inner), uv)]
@@ -256,17 +272,15 @@
 
 
 def down_kernel(
-    table, flags, got, store, keep, recv, scaled, vecs, sl, su, lf, tr, cs, bh, fl, sem
+    table, flags, got, store, here, send, lf, tr, cs, bh, fl, sem
 ):
     chord, z, core = place()
-    eta = eta_copies(keep, recv, sl, su, core, sem)
     pre = [
-        pltpu.make_async_copy(store.at[pl.ds(LEAF, 510)], tr, sem.at[4]),
-        pltpu.make_async_copy(store.at[pl.ds(0, LEAF)], lf, sem.at[5]),
-    ]
-    kinds = pltpu.make_async_copy(flags, fl, sem.at[6])
-    kinds.start()
-    for c in pre + eta:
+        pltpu.make_async_copy(store.at[pl.ds(LEAF, 510)], tr, sem.at[0]),
+        pltpu.make_async_copy(store.at[pl.ds(0, LEAF)], lf, sem.at[1]),
+        pltpu.make_async_copy(flags, fl, sem.at[2]),
+    ]
+    for c in pre:
         c.start()
     lane = lane_iota()
     group = lane // 4
@@ -342,30 +356,19 @@
             bh[c, r, 0:8, :] = jnp.where(even, b1[c], roll(b2[c], 1))
             bh[c, r, 8:16, :] = jnp.where(even, roll(b1[c], -1), b2[c])
 
-    kinds.wait()
-    kind = fl[pl.ds(pl.multiple_of(core * 8, 8), 8), :]
-    s = []
-    for j in range(4):
-        s.append([bh[c, j // 2, pl.ds(j % 2, 8, stride=2), :] for c in range(N)])
+    pre[2].wait()
+    wall = (z == 0) & (core == 0)
+    for half in range(2):
+        kind = fl[8 * half : 8 * half + 8, :]
+        for c in range(N):
+            factor = zero
+            for k in range(3):
+                factor = jnp.where(kind == k, table[k, c], factor)
+            row = bh[c, half, pl.ds(0, 8, stride=2), :]
+            bh[c, half, pl.ds(0, 8, stride=2), :] = jnp.where(wall, factor, 1.0) * row
     for c in range(N):
-        factor = zero
-        for k in range(3):
-            factor = jnp.where(kind == k, table[k, c], factor)
-        s[0][c] = jnp.where(z == 0, factor, 1.0) * s[0][c]
-    for j in range(4):
-        for c in range(N):
-            scaled[j, c] = s[j][c]
-    for c in eta:
-        c.wait()
-    t = [s[0]]
-    for j in range(1, 4):
-        t.append(mv(cell(sl, j), t[-1], s[j]))
-    u = t[3]
-    for j in range(2, -1, -1):
-        u = mv(cell(su, j), u, t[j])
-    for c in range(N):
-        vecs[c] = t[3][c]
-        vecs[N + c] = u[c]
+        here[c] = bh[c, core]
+        send[c] = bh[c, 1 - core]
 
 
 def solve_kernel(got, back, turned, ain):
@@ -411,7 +414,7 @@
 
 
 def finish_kernel(
-    got, scaled, keep, recv, vecs, taken, mine, other, own, send, sl, su, res, both, sem
+    got, here, there, keep, recv, hold, taken, mine, other, own, send, sl, su, res, both, sem
 ):
     _, z, core = place()
     odd = z % 2
@@ -432,7 +435,7 @@
         b.append(jnp.where(first, roll(x, 64), y))
     for c in pair:
         c.wait()
-    lv_e = [jnp.where(even, vecs[c], taken[c]) for c in range(N)]
+    lv_e = [jnp.where(even, hold[c], taken[c]) for c in range(N)]
     mid = mv(square([both[0, c] for c in range(25)]), a, lv_e)
     low = mv(square([both[1, 50 + c] for c in range(25)]), mid, [taken[c] for c in range(N)])
     low = mv(square([both[1, 25 + c] for c in range(25)]), b, low)
@@ -440,9 +443,10 @@
     b = [jnp.where(even, x, y) for x, y in zip(low, b)]
     for c in copies:
         c.wait()
+    s = sources(here, there, res, core)
     lifted = []
     for j in range(4):
-        a = mv(cell(sl, j), a, [scaled[j, c] for c in range(N)])
+        a = mv(cell(sl, j), a, s[j])
         lifted.append(a)
     for j in range(3, -1, -1):
         b = mv(cell(su, j), b, lifted[j])
@@ -473,34 +477,34 @@
         return lax.all_to_all(x, "wall", 0, 0, tiled=True, axis_index_groups=groups)
 
     side = pltpu.VMEM((25, 2, 16, 128), F32)
-    send, keep = pl.pallas_call(
-        pack_kernel,
-        out_shape=(shape(105, 16, 128), shape(105, 16, 128)),
+    cells = pltpu.VMEM((N, 2, 16, 128), F32)
+    both = pltpu.VMEM((2, 75, 8, 128), F32)
+    msg, store, send, keep = pl.pallas_call(
+        up_kernel,
+        out_shape=(
+            shape(16, 24, 128),
+            pltpu.HBM((STORE, 8, 128), F32),
+            shape(50, 16, 128),
+            shape(50, 16, 128),
+        ),
         in_specs=[SM] + [HBM] * 6,
-        out_specs=(VM, VM),
-        scratch_shapes=[pltpu.VMEM((N, 32, 128), F32), pltpu.VMEM((32, 128), jnp.int32), dma(10)],
-        compiler_params=params(),
-        name="pack",
-    )(jet_source, rhs, mask, xl, xu, el, eu)
-    recv = lax.ppermute(send, "wall", swap)
-    msg, store = pl.pallas_call(
-        up_kernel,
-        out_shape=(shape(16, 24, 128), pltpu.HBM((STORE, 8, 128), F32)),
-        in_specs=[ANY, ANY],
-        out_specs=(VM, HBM),
+        out_specs=(VM, HBM, VM, VM),
         scratch_shapes=[
-            side,
-            side,
-            pltpu.VMEM((N, 2, 16, 128), F32),
+            pltpu.VMEM((25, 32, 128), F32),
+            pltpu.VMEM((25, 32, 128), F32),
+            pltpu.VMEM((N, 32, 128), F32),
+            pltpu.VMEM((32, 128), jnp.int32),
             pltpu.VMEM((2, 85, 8, 128), F32),
             pltpu.VMEM((85, 8, 128), F32),
             pltpu.VMEM((2, 110, 8, 128), F32),
             pltpu.VMEM((6, 85, 8, 128), F32),
-            dma(14),
+            dma(18),
         ],
         compiler_params=params(),
+        cost_estimate=cost(9000 * 1024, 4 << 20),
         name="chord_up",
-    )(keep, recv)
+    )(jet_source, rhs, mask, xl, xu, el, eu)
+    recv = lax.ppermute(send, "wall", swap)
     mine = pl.pallas_call(
         wall_kernel,
         out_shape=shape(75, 8, 128),
@@ -513,34 +517,33 @@
     )(keep, recv)
     other = lax.ppermute(mine, "wall", near)
     got = lax.all_to_all(msg, "chord", 0, 0, tiled=True)
-    scaled, vecs = pl.pallas_call(
+    here, away = pl.pallas_call(
         down_kernel,
-        out_shape=(shape(4, N, 8, 128), shape(2 * N, 8, 128)),
-        in_specs=[SM, HBM, VM, HBM, ANY, ANY],
+        out_shape=(shape(N, 16, 128), shape(N, 16, 128)),
+        in_specs=[SM, HBM, VM, HBM],
         out_specs=(VM, VM),
         scratch_shapes=[
-            side,
-            side,
             pltpu.VMEM((LEAF, 8, 128), F32),
             pltpu.VMEM((510, 8, 128), F32),
             pltpu.VMEM((85, 8, 128), F32),
-            pltpu.VMEM((N, 2, 16, 128), F32),
+            cells,
             pltpu.VMEM((16, 128), jnp.int32),
-            dma(7),
+            dma(3),
         ],
         compiler_params=params(),
+        cost_estimate=cost(50_000_000_000, 4 << 20),
         name="chord_down",
-    )(bc_table, flags, got, far(store, STORE, 8, 128), keep, recv)
-    both = pltpu.VMEM((2, 75, 8, 128), F32)
-    zmsg, give = pl.pallas_call(
+    )(bc_table, flags, got, far(store, STORE, 8, 128))
+    there = lax.ppermute(away, "wall", swap)
+    zmsg, give, hold = pl.pallas_call(
         pair_kernel,
-        out_shape=(shape(16 * ROWS, 128), shape(N, 8, 128)),
-        in_specs=[VM, ANY, ANY],
-        out_specs=(VM, VM),
-        scratch_shapes=[both, pltpu.VMEM((75, 8, 128), F32), dma(2)],
+        out_shape=(shape(16 * ROWS, 128), shape(N, 8, 128), shape(N, 8, 128)),
+        in_specs=[VM, VM, ANY, ANY, ANY, ANY],
+        out_specs=(VM, VM, VM),
+        scratch_shapes=[side, side, cells, both, pltpu.VMEM((75, 8, 128), F32), dma(6)],
         compiler_params=params(),
         name="wall_pair",
-    )(vecs, mine, other)
+    )(here, there, keep, recv, mine, other)
     zgot = over_z(zmsg.reshape(16, ROWS, 128)).reshape(16 * ROWS, 128)
     taken = lax.ppermute(give, "wall", near)
     back = pl.pallas_call(
@@ -556,12 +559,12 @@
     own, theirs = pl.pallas_call(
         finish_kernel,
         out_shape=(shape(N, 16, 128), shape(N, 16, 128)),
-        in_specs=[VM, VM, ANY, ANY, VM, VM, ANY, ANY],
+        in_specs=[VM, VM, VM, ANY, ANY, VM, VM, ANY, ANY],
         out_specs=(VM, VM),
-        scratch_shapes=[side, side, pltpu.VMEM((N, 2, 16, 128), F32), both, dma(6)],
+        scratch_shapes=[side, side, cells, both, dma(6)],
         compiler_params=params(),
         name="finish",
-    )(inflow, scaled, keep, recv, vecs, taken, mine, other)
+    )(inflow, here, there, keep, recv, hold, taken, mine, other)
     theirs = lax.ppermute(theirs, "wall", swap)
     core = lax.axis_index("wall") % 2
     low = jnp.where(core == 0, own, theirs)

time: 86.1 us -> 86.8 us (level)
  blocking collectives: 36.2 us -> 25.6 us
  starting transfers between devices: 27 us -> 32.6 us
  waiting for transfers between devices: 11.2 us -> 15.6 us
  Pallas kernels: 9.82 us -> 11.1 us
    all_to_all x1 -> x0, blocking collectives: 10 us -> none  [per_device(): got = lax.all_to_all(msg, 'chord', 0, 0, tiled=True)]
    all_to_all x0 -> x1, waiting for transfers between devices: none -> 5.53 us  [per_device(): got = lax.all_to_all(msg, 'chord', 0, 0, tiled=True)]
    all_to_all x0 -> x1, starting transfers between devices: none -> 3.53 us  [per_device(): got = lax.all_to_all(msg, 'chord', 0, 0, tiled=True)]
    ppermute x0 -> x1, starting transfers between devices: none -> 2.85 us  [per_device(): there = lax.ppermute(away, 'wall', swap)]
    pallas_call x1, Pallas kernels: 2.37 us -> 4.66 us  [per_device(): pl.pallas_call(up_kernel, out_shape=(shape(16, 24, 128), pltpu.HBM((STORE...]
    ppermute x1, starting transfers between devices: 6.01 us -> 3.83 us  [per_device(): theirs = lax.ppermute(theirs, 'wall', swap)]
    ppermute x1, waiting for transfers between devices: 2 us -> 0.01 us  [per_device(): recv = lax.ppermute(send, 'wall', swap)]
    all_to_all x1, starting transfers between devices: 7.02 us -> 8.41 us  [over_z(): return lax.all_to_all(x, 'wall', 0, 0, tiled=True, axis_index_groups=groups)]
  transfers between devices with their start and end apart: 5 -> 7, of which waited for: 4 -> 5; matrix products, arithmetic and copies ran while one was open for 0% -> 0% of each run, Pallas kernels for 6% -> 5%
where the time goes in v4:
time: 86.8 us; the launch traced here: 86.3 us
  starting transfers between devices  32.6 us (38%)
  blocking collectives  25.6 us (29%)
  waiting for transfers between devices  15.6 us (18%)
  Pallas kernels  11.1 us (13%)
    all_to_all x1, blocking collectives, over_z(): return lax.all_to_all(x, 'wall', 0, 0, tiled=True, axis_index_groups=groups)  25.6 us
    ppermute x1, starting transfers between devices, per_device(): recv = lax.ppermute(send, 'wall', swap)  8.79 us
    all_to_all x1, starting transfers between devices, over_z(): return lax.all_to_all(x, 'wall', 0, 0, tiled=True, axis_index_groups=groups)  8.41 us
    all_to_all x1, waiting for transfers between devices, over_z(): return lax.all_to_all(x, 'wall', 0, 0, tiled=True, axis_index_groups=groups)  6.59 us
    all_to_all x1, waiting for transfers between devices, per_device(): got = lax.all_to_all(msg, 'chord', 0, 0, tiled=True)  5.53 us
    pallas_call x1, Pallas kernels, per_device(): pl.pallas_call(up_kernel, out_shape=(shape(16, 24, 128), pltpu.HBM((STORE...  4.66 us
    pallas_call x1, Pallas kernels, per_device(): pl.pallas_call(down_kernel, out_shape=(shape(N, 16, 128), shape(N, 16, 12...  3.86 us
    ppermute x1, starting transfers between devices, per_device(): theirs = lax.ppermute(theirs, 'wall', swap)  3.83 us
  transfers between devices with their start and end apart: 7, of which 5 were waited for; matrix products, arithmetic and copies ran while one was open for 0% of the time, Pallas kernels for 5%

profile of v4, /device:TPU:1, one launch (start us, length us, event | category | flops | bytes accessed | tf_op | source)
XLA Modules:
  0.0 86.3 jit_solution(9196811659358987134)
XLA Ops:
  0.0 0.0 copy-start.1
  0.0 0.0 copy-start
  0.0 0.7 copy-done
  0.7 4.7 %chord_up.1 = (f32[16,24,128]{2,1,0:T(8,128)}, f32[730,8,128]{2,1,0:T(8,128)}, f32[50,16,128]{2,1,0:T(8,128)S(1)}, f32[50,16,128]{2,1,0:T(8,128)S(1)}) custom-call(f32[5]{0:T(128)S(1)} %copy-done, f32[5,32,128]{2,1,0:T(8,128)} %bitcast.18, s32[32,128]{1,0:T(8,128)} %bitcast.19, f32[25,32,128]{2,1,0:T(8,128)} %bitcast.14, f32[25,32,128]{2,1,0:T(8,128)} %bitcast.15, ...), custom_call_target="tpu_custom_call" | custom-call | flops 9216000 | bytes 4194304 | tf_op jit(solution)/shard_map/chord_up/pallas_call | solution.py:482
  5.3 8.8 %collective-permute-start.1 = (f32[50,16,128]{2,1,0:T(8,128)S(1)}, f32[50,16,128]{2,1,0:T(8,128)S(1)}, u32[]{:S(2)}, u32[]{:S(2)}) collective-permute-start(f32[50,16,128]{2,1,0:T(8,128)S(1)} %get-tuple-element.21), channel_id=1, source_target_pairs={{0,1},{1,0},{2,3},{3,2},{4,5},{5,4},{6,7},{7,6},{8,9},{9,8},{10,11... | collective-permute-start | bytes 1228808 | tf_op jit(solution)/shard_map/ppermute | solution.py:507
  14.1 3.5 %all-to-all-start = ((f32[16,24,128]{2,1,0:T(8,128)}), f32[16,24,128]{2,1,0:T(8,128)S(1)}, u32[]{:S(2)}, u32[]{:S(2)}) async-start(f32[16,24,128]{2,1,0:T(8,128)} %get-tuple-element.16), calls=%async_computation | async-start | bytes 393216 | tf_op jit(solution)/shard_map/all_to_all | solution.py:519
  17.7 0.0 collective-permute-done.1.recv
  17.7 0.5 wall_blocks.1.mine
  18.2 1.9 %collective-permute-start.2 = (f32[75,8,128]{2,1,0:T(8,128)S(1)}, f32[75,8,128]{2,1,0:T(8,128)S(1)}, u32[]{:S(2)}, u32[]{:S(2)}) collective-permute-start(f32[75,8,128]{2,1,0:T(8,128)S(1)} %wall_blocks.1.mine), channel_id=1, source_target_pairs={{0,2},{1,3},{2,0},{3,1},{4,6},{5,7},{6,4},{7,5},{8,10},{9,11},{10,... | collective-permute-start | bytes 921608 | tf_op jit(solution)/shard_map/ppermute | solution.py:518
  20.1 5.5 %all-to-all-done.got = f32[16,24,128]{2,1,0:T(8,128)S(1)} async-done(((f32[16,24,128]{2,1,0:T(8,128)}), f32[16,24,128]{2,1,0:T(8,128)S(1)}, u32[]{:S(2)}, u32[]{:S(2)}) %all-to-all-start) | async-done | bytes 196640 | tf_op jit(solution)/shard_map/all_to_all | solution.py:519
  25.6 0.0 copy-done.1
  25.6 3.9 %chord_down.1 = (f32[5,16,128]{2,1,0:T(8,128)S(1)}, f32[5,16,128]{2,1,0:T(8,128)S(1)}) custom-call(f32[3,5]{1,0:T(4,128)S(1)} %copy-done.1, s32[16,128]{1,0:T(8,128)} %flags.1, f32[16,24,128]{2,1,0:T(8,128)S(1)} %all-to-all-done.got, f32[730,8,128]{2,1,0:T(8,128)} %get-tuple-element.17.store), custom_call_target="tpu_custom_call" | custom-call | flops 49999998976 | bytes 4194304 | tf_op jit(solution)/shard_map/chord_down/pallas_call | solution.py:520
  29.5 2.8 %collective-permute-start = (f32[5,16,128]{2,1,0:T(8,128)S(1)}, f32[5,16,128]{2,1,0:T(8,128)S(1)}, u32[]{:S(2)}, u32[]{:S(2)}) collective-permute-start(f32[5,16,128]{2,1,0:T(8,128)S(1)} %get-tuple-element.19), channel_id=1, source_target_pairs={{0,1},{1,0},{2,3},{3,2},{4,5},{5,4},{6,7},{7,6},{8,9},{9,8},{10,11... | collective-permute-start | bytes 122888 | tf_op jit(solution)/shard_map/ppermute | solution.py:537
  32.4 0.8 collective-permute-done.there
  33.2 0.0 collective-permute-done.2.other
  33.2 0.7 wall_pair.1
  33.9 25.6 %all_to_all.15 = f32[16,24,128]{2,1,0:T(8,128)S(1)} all-to-all(f32[16,24,128]{2,1,0:T(8,128)S(1)} %bitcast.13), channel_id=1, replica_groups={{0,2,4,6,8,10,12,14,16,18,20,22,24,26,28,30},{1,3,5,7,9,11,13,15,17,19,..., dimensions={0} | all-to-all | bytes 393216 | tf_op jit(solution)/shard_map/all_to_all | solution.py:477
  59.4 0.9 %wall_solve.1 = f32[128,128]{1,0:T(8,128)} custom-call(f32[384,128]{1,0:T(8,128)S(1)} %bitcast.11), custom_call_target="tpu_custom_call" | custom-call | tf_op jit(solution)/shard_map/wall_solve/pallas_call | solution.py:549
  60.4 8.4 %all-to-all-start.2 = ((f32[16,8,128]{2,1,0:T(8,128)}), f32[16,8,128]{2,1,0:T(8,128)S(1)}, u32[]{:S(2)}, u32[]{:S(2)}) async-start(f32[16,8,128]{2,1,0:T(8,128)} %bitcast.8), calls=%async_computation.2 | async-start | bytes 131072 | tf_op jit(solution)/shard_map/all_to_all | solution.py:477
  68.8 3.3 %collective-permute-start.3 = (f32[5,8,128]{2,1,0:T(8,128)S(1)}, f32[5,8,128]{2,1,0:T(8,128)S(1)}, u32[]{:S(2)}, u32[]{:S(2)}) collective-permute-start(f32[5,8,128]{2,1,0:T(8,128)S(1)} %get-tuple-element.24), channel_id=1, source_target_pairs={{0,2},{1,3},{2,0},{3,1},{4,6},{5,7},{6,4},{7,5},{8,10},{9,11},{10,... | collective-permute-start | bytes 61448 | tf_op jit(solution)/shard_map/ppermute | solution.py:548
  72.1 1.8 %collective-permute-done.3.taken = f32[5,8,128]{2,1,0:T(8,128)S(1)} collective-permute-done((f32[5,8,128]{2,1,0:T(8,128)S(1)}, f32[5,8,128]{2,1,0:T(8,128)S(1)}, u32[]{:S(2)}, u32[]{:S(2)}) %collective-permute-start.3) | collective-permute-done | bytes 20512 | tf_op jit(solution)/shard_map/ppermute | solution.py:548
  73.9 6.6 %all-to-all-done.2 = f32[16,8,128]{2,1,0:T(8,128)S(1)} async-done(((f32[16,8,128]{2,1,0:T(8,128)}), f32[16,8,128]{2,1,0:T(8,128)S(1)}, u32[]{:S(2)}, u32[]{:S(2)}) %all-to-all-start.2) | async-done | bytes 65568 | tf_op jit(solution)/shard_map/all_to_all | solution.py:477
  80.5 0.5 finish.1
  81.0 3.8 %collective-permute-start.4 = (f32[5,16,128]{2,1,0:T(8,128)S(1)}, f32[5,16,128]{2,1,0:T(8,128)S(1)}, u32[]{:S(2)}, u32[]{:S(2)}) collective-permute-start(f32[5,16,128]{2,1,0:T(8,128)S(1)} %get-tuple-element.26), channel_id=1, source_target_pairs={{0,1},{1,0},{2,3},{3,2},{4,5},{5,4},{6,7},{7,6},{8,9},{9,8},{10,11... | collective-permute-start | bytes 122888 | tf_op jit(solution)/shard_map/ppermute | solution.py:568
  84.9 0.8 collective-permute-done.4
  85.7 0.6 pad_maximum_fusion
  (1 shorter events, 0.0 us)
Async XLA Ops:
  0.0 25.6 %copy-start.1 = (f32[3,5]{1,0:T(4,128)S(1)}, f32[3,5]{1,0:T(4,128)}, u32[]{:S(2)}) copy-start(f32[3,5]{1,0:T(4,128)} %table.1) | copy-start | bytes 184
  0.0 0.7 copy-start
  5.3 12.3 %collective-permute-start.1 = (f32[50,16,128]{2,1,0:T(8,128)S(1)}, f32[50,16,128]{2,1,0:T(8,128)S(1)}, u32[]{:S(2)}, u32[]{:S(2)}) collective-permute-start(f32[50,16,128]{2,1,0:T(8,128)S(1)} %get-tuple-element.21), channel_id=1, source_target_pairs={{0,1},{1,0},{2,3},{3,2},{4,5},{5,4},{6,7},{7,6},{8,9},{9,8},{10,11... | collective-permute-start | bytes 1228808 | tf_op jit(solution)/shard_map/ppermute | solution.py:507
  14.1 11.5 %all-to-all-start = ((f32[16,24,128]{2,1,0:T(8,128)}), f32[16,24,128]{2,1,0:T(8,128)S(1)}, u32[]{:S(2)}, u32[]{:S(2)}) async-start(f32[16,24,128]{2,1,0:T(8,128)} %get-tuple-element.16), calls=%async_computation | async-start | bytes 393216 | tf_op jit(solution)/shard_map/all_to_all | solution.py:519
  18.2 15.0 %collective-permute-start.2 = (f32[75,8,128]{2,1,0:T(8,128)S(1)}, f32[75,8,128]{2,1,0:T(8,128)S(1)}, u32[]{:S(2)}, u32[]{:S(2)}) collective-permute-start(f32[75,8,128]{2,1,0:T(8,128)S(1)} %wall_blocks.1.mine), channel_id=1, source_target_pairs={{0,2},{1,3},{2,0},{3,1},{4,6},{5,7},{6,4},{7,5},{8,10},{9,11},{10,... | collective-permute-start | bytes 921608 | tf_op jit(solution)/shard_map/ppermute | solution.py:518
  29.5 3.7 %collective-permute-start = (f32[5,16,128]{2,1,0:T(8,128)S(1)}, f32[5,16,128]{2,1,0:T(8,128)S(1)}, u32[]{:S(2)}, u32[]{:S(2)}) collective-permute-start(f32[5,16,128]{2,1,0:T(8,128)S(1)} %get-tuple-element.19), channel_id=1, source_target_pairs={{0,1},{1,0},{2,3},{3,2},{4,5},{5,4},{6,7},{7,6},{8,9},{9,8},{10,11... | collective-permute-start | bytes 122888 | tf_op jit(solution)/shard_map/ppermute | solution.py:537
  60.4 20.1 %all-to-all-start.2 = ((f32[16,8,128]{2,1,0:T(8,128)}), f32[16,8,128]{2,1,0:T(8,128)S(1)}, u32[]{:S(2)}, u32[]{:S(2)}) async-start(f32[16,8,128]{2,1,0:T(8,128)} %bitcast.8), calls=%async_computation.2 | async-start | bytes 131072 | tf_op jit(solution)/shard_map/all_to_all | solution.py:477
  68.8 5.1 %collective-permute-start.3 = (f32[5,8,128]{2,1,0:T(8,128)S(1)}, f32[5,8,128]{2,1,0:T(8,128)S(1)}, u32[]{:S(2)}, u32[]{:S(2)}) collective-permute-start(f32[5,8,128]{2,1,0:T(8,128)S(1)} %get-tuple-element.24), channel_id=1, source_target_pairs={{0,2},{1,3},{2,0},{3,1},{4,6},{5,7},{6,4},{7,5},{8,10},{9,11},{10,... | collective-permute-start | bytes 61448 | tf_op jit(solution)/shard_map/ppermute | solution.py:548
  81.0 4.7 %collective-permute-start.4 = (f32[5,16,128]{2,1,0:T(8,128)S(1)}, f32[5,16,128]{2,1,0:T(8,128)S(1)}, u32[]{:S(2)}, u32[]{:S(2)}) collective-permute-start(f32[5,16,128]{2,1,0:T(8,128)S(1)} %get-tuple-element.26), channel_id=1, source_target_pairs={{0,1},{1,0},{2,3},{3,2},{4,5},{5,4},{6,7},{7,6},{8,9},{9,8},{10,11... | collective-permute-start | bytes 122888 | tf_op jit(solution)/shard_map/ppermute | solution.py:568

commit v5 on v4

--- a/solution.py
+++ b/solution.py
@@ -14,8 +14,7 @@
 VM = pl.BlockSpec(memory_space=pltpu.VMEM)
 SM = pl.BlockSpec(memory_space=pltpu.SMEM)
 LIMIT = 32 << 20
-LEAF = 220
-STORE = LEAF + 510
+LEVELS = 6
 
 
 def shape(*dims):
@@ -102,31 +101,35 @@
 
 
 def up_kernel(
-    jet, rhs, mask, xl, xu, el, eu, msg, store, send, keep,
-    sl, su, ss, mk, n1, n2, leaf, tree, sem,
+    jet, rhs, mask, xl, xu, el, eu, msg, send, keep, leaf0, leaf1, store,
+    tree, sl, su, ss, mk, jt, n1, n2, sem,
 ):
+    leaves = (leaf0, leaf1)
     core = place()[2]
     copies = [
         pltpu.make_async_copy(src, dst, sem.at[n])
-        for n, (src, dst) in enumerate(((rhs, ss), (mask, mk), (xl, sl), (xu, su)))
-    ]
+        for n, (src, dst) in enumerate(((jet, jt), (mask, mk), (rhs, ss)))
+    ]
+    for r in range(2):
+        rows = pl.ds(16 * r, 16)
+        for n, (src, dst) in enumerate(((xl, sl), (xu, su))):
+            at = sem.at[3 + 2 * r + n]
+            copies.append(pltpu.make_async_copy(src.at[:, rows, :], dst.at[:, rows, :], at))
     for c in copies:
         c.start()
-    copies[0].wait()
-    copies[1].wait()
+    for c in copies[:3]:
+        c.wait()
     m = mk[...].astype(F32)
     for c in range(N):
-        ss[c] = ss[c] + m * jet[c]
-    copies[2].wait()
-    copies[3].wait()
-    eta = []
+        ss[c] = ss[c] + m * jt[c]
+    moves = []
     for n, (dst, half) in enumerate(((send, 1 - core), (keep, core))):
         off = pl.multiple_of(half * 16, 16)
         for k, ref in enumerate((el, eu)):
             part = dst.at[pl.ds(25 * k, 25)]
-            at = sem.at[14 + 2 * n + k]
-            eta.append(pltpu.make_async_copy(ref.at[:, pl.ds(off, 16), :], part, at))
-            eta[-1].start()
+            at = sem.at[7 + 2 * n + k]
+            moves.append(pltpu.make_async_copy(ref.at[:, pl.ds(off, 16), :], part, at))
+            moves[-1].start()
     lane = lane_iota()
     even = lane % 2 == 0
     low = (lane // 2) % 2 == 0
@@ -136,16 +139,14 @@
         b = ref[c, 16 * r + 8 : 16 * r + 16, :]
         return jnp.where(even, a, roll(b, 1)), jnp.where(even, roll(a, -1), b)
 
-    saves = []
     for r in range(2):
+        copies[3 + 2 * r].wait()
+        copies[4 + 2 * r].wait()
         l1, l2 = zip(*[split(sl, c, r) for c in range(25)])
         v1, v2 = zip(*[split(ss, c, r) for c in range(N)])
         u1, u2 = zip(*[split(su, c, r) for c in range(25)])
         for c, x in enumerate(l1 + v1 + l2 + v2 + u1 + u2):
-            leaf[r, c] = x
-        dst = store.at[pl.ds(110 * r, 110)]
-        saves.append(pltpu.make_async_copy(leaf.at[r], dst, sem.at[6 + r]))
-        saves[-1].start()
+            leaves[r][c] = x
         l1, l2, u1, u2 = square(l1), square(l2), square(u1), square(u2)
         lb = mm(l2, l1)
         lv = mv(l2, v1, v2)
@@ -158,7 +159,7 @@
         a, b = n1[0, c], n1[1, c]
         left.append(jnp.where(low, a, roll(b, 2)))
         right.append(jnp.where(low, roll(a, -2), b))
-    for level in range(6):
+    for level in range(LEVELS):
         if level:
             left = [n2[c] for c in range(85)]
             right = [roll(x, -(2 << level)) for x in left]
@@ -166,9 +167,8 @@
             tree[level, c] = left[c]
         for c in range(30, 85):
             tree[level, c] = right[c]
-        dst = store.at[pl.ds(LEAF + 85 * level, 85)]
-        saves.append(pltpu.make_async_copy(tree.at[level], dst, sem.at[8 + level]))
-        saves[-1].start()
+        moves.append(pltpu.make_async_copy(tree.at[level], store.at[level], sem.at[11 + level]))
+        moves[-1].start()
         for c, x in enumerate(values_of(compose(node(left), node(right)))):
             n2[c] = x
     group = lane // 4
@@ -179,7 +179,7 @@
             acc = x if acc is None else jnp.where(group == pos, roll(x, 4 * pos), acc)
         for d in range(16):
             msg[d, 8 * g : 8 * g + 8, :] = acc
-    for c in saves + eta:
+    for c in moves:
         c.wait()
 
 
@@ -272,16 +272,17 @@
 
 
 def down_kernel(
-    table, flags, got, store, here, send, lf, tr, cs, bh, fl, sem
+    table, flags, got, leaf0, leaf1, store, here, send, tree, cs, bh, fl, sem
 ):
     chord, z, core = place()
-    pre = [
-        pltpu.make_async_copy(store.at[pl.ds(LEAF, 510)], tr, sem.at[0]),
-        pltpu.make_async_copy(store.at[pl.ds(0, LEAF)], lf, sem.at[1]),
-        pltpu.make_async_copy(flags, fl, sem.at[2]),
-    ]
-    for c in pre:
+    fetch = [
+        pltpu.make_async_copy(store.at[level], tree.at[level], sem.at[level])
+        for level in range(LEVELS)
+    ]
+    kinds = pltpu.make_async_copy(flags, fl, sem.at[LEVELS])
+    for c in fetch[::-1]:
         c.start()
+    kinds.start()
     lane = lane_iota()
     group = lane // 4
     for g in range(3):
@@ -325,17 +326,16 @@
     a = [pltpu.roll(x, back, 1) for x in a]
     b = [pltpu.roll(x, back, 1) for x in b]
 
-    pre[0].wait()
     for level in range(5, -1, -1):
         dist = 2 << level
-        a_mid = mv(square([tr[85 * level + c] for c in range(25)]), a, [tr[85 * level + 25 + c] for c in range(N)])
-        b_mid = mv(square([tr[85 * level + 30 + c] for c in range(25)]), b, [tr[85 * level + 55 + c] for c in range(N)])
-        b_mid = mv(square([tr[85 * level + 60 + c] for c in range(25)]), a_mid, b_mid)
+        fetch[level].wait()
+        a_mid = mv(square([tree[level, c] for c in range(25)]), a, [tree[level, 25 + c] for c in range(N)])
+        b_mid = mv(square([tree[level, 30 + c] for c in range(25)]), b, [tree[level, 55 + c] for c in range(N)])
+        b_mid = mv(square([tree[level, 60 + c] for c in range(25)]), a_mid, b_mid)
         left = (lane // dist) % 2 == 0
         if level:
             a = [jnp.where(left, x, roll(y, dist)) for x, y in zip(a, a_mid)]
             b = [jnp.where(left, x, roll(y, dist)) for x, y in zip(b_mid, b)]
-    pre[1].wait()
     even = lane % 2 == 0
     for r in range(2):
         if r == 0:
@@ -346,7 +346,7 @@
             rb = [jnp.where(left, roll(x, -2), y) for x, y in zip(b_mid, b)]
 
         def part(first, count):
-            return [lf[110 * r + first + c] for c in range(count)]
+            return [(leaf0, leaf1)[r][first + c] for c in range(count)]
 
         a1 = mv(square(part(0, 25)), ra, part(25, N))
         a2 = mv(square(part(30, 25)), a1, part(55, N))
@@ -356,7 +356,7 @@
             bh[c, r, 0:8, :] = jnp.where(even, b1[c], roll(b2[c], 1))
             bh[c, r, 8:16, :] = jnp.where(even, roll(b1[c], -1), b2[c])
 
-    pre[2].wait()
+    kinds.wait()
     wall = (z == 0) & (core == 0)
     for half in range(2):
         kind = fl[8 * half : 8 * half + 8, :]
@@ -479,31 +479,33 @@
     side = pltpu.VMEM((25, 2, 16, 128), F32)
     cells = pltpu.VMEM((N, 2, 16, 128), F32)
     both = pltpu.VMEM((2, 75, 8, 128), F32)
-    msg, store, send, keep = pl.pallas_call(
+    msg, send, keep, leaf0, leaf1, store = pl.pallas_call(
         up_kernel,
         out_shape=(
             shape(16, 24, 128),
-            pltpu.HBM((STORE, 8, 128), F32),
             shape(50, 16, 128),
             shape(50, 16, 128),
+            shape(110, 8, 128),
+            shape(110, 8, 128),
+            pltpu.HBM((LEVELS, 85, 8, 128), F32),
         ),
-        in_specs=[SM] + [HBM] * 6,
-        out_specs=(VM, HBM, VM, VM),
+        in_specs=[HBM] * 7,
+        out_specs=(VM, VM, VM, VM, VM, HBM),
         scratch_shapes=[
+            pltpu.VMEM((LEVELS, 85, 8, 128), F32),
             pltpu.VMEM((25, 32, 128), F32),
             pltpu.VMEM((25, 32, 128), F32),
             pltpu.VMEM((N, 32, 128), F32),
             pltpu.VMEM((32, 128), jnp.int32),
+            pltpu.SMEM((N,), F32),
             pltpu.VMEM((2, 85, 8, 128), F32),
             pltpu.VMEM((85, 8, 128), F32),
-            pltpu.VMEM((2, 110, 8, 128), F32),
-            pltpu.VMEM((6, 85, 8, 128), F32),
-            dma(18),
+            dma(17),
         ],
         compiler_params=params(),
         cost_estimate=cost(9000 * 1024, 4 << 20),
         name="chord_up",
-    )(jet_source, rhs, mask, xl, xu, el, eu)
+    )(far(jet_source, N), rhs, mask, xl, xu, el, eu)
     recv = lax.ppermute(send, "wall", swap)
     mine = pl.pallas_call(
         wall_kernel,
@@ -520,20 +522,19 @@
     here, away = pl.pallas_call(
         down_kernel,
         out_shape=(shape(N, 16, 128), shape(N, 16, 128)),
-        in_specs=[SM, HBM, VM, HBM],
+        in_specs=[SM, HBM, VM, VM, VM, HBM],
         out_specs=(VM, VM),
         scratch_shapes=[
-            pltpu.VMEM((LEAF, 8, 128), F32),
-            pltpu.VMEM((510, 8, 128), F32),
+            pltpu.VMEM((LEVELS, 85, 8, 128), F32),
             pltpu.VMEM((85, 8, 128), F32),
             cells,
             pltpu.VMEM((16, 128), jnp.int32),
-            dma(3),
+            dma(7),
         ],
         compiler_params=params(),
         cost_estimate=cost(50_000_000_000, 4 << 20),
         name="chord_down",
-    )(bc_table, flags, got, far(store, STORE, 8, 128))
+    )(bc_table, flags, got, leaf0, leaf1, far(store, LEVELS, 85, 8, 128))
     there = lax.ppermute(away, "wall", swap)
     zmsg, give, hold = pl.pallas_call(
         pair_kernel,

time: 86.8 us -> 85.2 us (0.982)
  Pallas kernels: 11.1 us -> 10.1 us
where the time goes in v5:
time: 85.2 us; the launch traced here: 84.7 us
  starting transfers between devices  32.6 us (38%)
  blocking collectives  25.6 us (30%)
  waiting for transfers between devices  15.6 us (18%)
  Pallas kernels  10.1 us (12%)
    all_to_all x1, blocking collectives, over_z(): return lax.all_to_all(x, 'wall', 0, 0, tiled=True, axis_index_groups=groups)  25.6 us
    ppermute x1, starting transfers between devices, per_device(): recv = lax.ppermute(send, 'wall', swap)  8.79 us
    all_to_all x1, starting transfers between devices, over_z(): return lax.all_to_all(x, 'wall', 0, 0, tiled=True, axis_index_groups=groups)  8.41 us
    all_to_all x1, waiting for transfers between devices, over_z(): return lax.all_to_all(x, 'wall', 0, 0, tiled=True, axis_index_groups=groups)  6.59 us
    all_to_all x1, waiting for transfers between devices, per_device(): got = lax.all_to_all(msg, 'chord', 0, 0, tiled=True)  5.53 us
    pallas_call x1, Pallas kernels, per_device(): pl.pallas_call(up_kernel, out_shape=(shape(16, 24, 128), shape(50, 16, 12...  4.12 us
    ppermute x1, starting transfers between devices, per_device(): theirs = lax.ppermute(theirs, 'wall', swap)  3.83 us
    all_to_all x1, starting transfers between devices, per_device(): got = lax.all_to_all(msg, 'chord', 0, 0, tiled=True)  3.53 us
  transfers between devices with their start and end apart: 7, of which 5 were waited for; matrix products, arithmetic and copies ran while one was open for 0% of the time, Pallas kernels for 5%

profile of v5, /device:TPU:1, one launch (start us, length us, event | category | flops | bytes accessed | tf_op | source)
XLA Modules:
  0.0 84.7 jit_solution(14531686273537019016)
XLA Ops:
  0.0 0.0 copy-start
  0.0 4.1 %chord_up.1 = (f32[16,24,128]{2,1,0:T(8,128)}, f32[50,16,128]{2,1,0:T(8,128)S(1)}, f32[50,16,128]{2,1,0:T(8,128)S(1)}, f32[110,8,128]{2,1,0:T(8,128)S(1)}, f32[1...) custom-call(f32[5]{0:T(128)} %jet.1, f32[5,32,128]{2,1,0:T(8,128)} %bitcast.18, s32[32,128]{1,0:T(8,128)} %bitcast.19, ...), custom_call_target="tpu_custom_call" | custom-call | flops 9216000 | bytes 4194304 | tf_op jit(solution)/shard_map/chord_up/pallas_call | solution.py:482
  4.1 8.8 %collective-permute-start.1 = (f32[50,16,128]{2,1,0:T(8,128)S(1)}, f32[50,16,128]{2,1,0:T(8,128)S(1)}, u32[]{:S(2)}, u32[]{:S(2)}) collective-permute-start(f32[50,16,128]{2,1,0:T(8,128)S(1)} %get-tuple-element.25), channel_id=1, source_target_pairs={{0,1},{1,0},{2,3},{3,2},{4,5},{5,4},{6,7},{7,6},{8,9},{9,8},{10,11... | collective-permute-start | bytes 1228808 | tf_op jit(solution)/shard_map/ppermute | solution.py:509
  12.9 3.5 %all-to-all-start = ((f32[16,24,128]{2,1,0:T(8,128)}), f32[16,24,128]{2,1,0:T(8,128)S(1)}, u32[]{:S(2)}, u32[]{:S(2)}) async-start(f32[16,24,128]{2,1,0:T(8,128)} %get-tuple-element.18), calls=%async_computation | async-start | bytes 393216 | tf_op jit(solution)/shard_map/all_to_all | solution.py:521
  16.5 0.0 collective-permute-done.1.recv
  16.5 0.5 wall_blocks.1.mine
  17.0 1.9 %collective-permute-start.2 = (f32[75,8,128]{2,1,0:T(8,128)S(1)}, f32[75,8,128]{2,1,0:T(8,128)S(1)}, u32[]{:S(2)}, u32[]{:S(2)}) collective-permute-start(f32[75,8,128]{2,1,0:T(8,128)S(1)} %wall_blocks.1.mine), channel_id=1, source_target_pairs={{0,2},{1,3},{2,0},{3,1},{4,6},{5,7},{6,4},{7,5},{8,10},{9,11},{10,... | collective-permute-start | bytes 921608 | tf_op jit(solution)/shard_map/ppermute | solution.py:520
  18.9 5.5 %all-to-all-done.got = f32[16,24,128]{2,1,0:T(8,128)S(1)} async-done(((f32[16,24,128]{2,1,0:T(8,128)}), f32[16,24,128]{2,1,0:T(8,128)S(1)}, u32[]{:S(2)}, u32[]{:S(2)}) %all-to-all-start) | async-done | bytes 196640 | tf_op jit(solution)/shard_map/all_to_all | solution.py:521
  24.4 0.0 copy-done
  24.4 3.4 %chord_down.1 = (f32[5,16,128]{2,1,0:T(8,128)S(1)}, f32[5,16,128]{2,1,0:T(8,128)S(1)}) custom-call(f32[3,5]{1,0:T(4,128)S(1)} %copy-done, s32[16,128]{1,0:T(8,128)} %flags.1, f32[16,24,128]{2,1,0:T(8,128)S(1)} %all-to-all-done.got, f32[110,8,128]{2,1,0:T(8,128)S(1)} %get-tuple-element.19.leaf0, f32[110,8,128]{2,1,0:T(8,128)S(1)} %get-tuple-element.20.leaf1, ...), custom_call_target="tpu_custom_call" | custom-call | flops 49999998976 | bytes 4194304 | tf_op jit(solution)/shard_map/chord_down/pallas_call | solution.py:522
  27.9 2.8 %collective-permute-start = (f32[5,16,128]{2,1,0:T(8,128)S(1)}, f32[5,16,128]{2,1,0:T(8,128)S(1)}, u32[]{:S(2)}, u32[]{:S(2)}) collective-permute-start(f32[5,16,128]{2,1,0:T(8,128)S(1)} %get-tuple-element.23), channel_id=1, source_target_pairs={{0,1},{1,0},{2,3},{3,2},{4,5},{5,4},{6,7},{7,6},{8,9},{9,8},{10,11... | collective-permute-start | bytes 122888 | tf_op jit(solution)/shard_map/ppermute | solution.py:538
  30.7 0.8 %collective-permute-done.there = f32[5,16,128]{2,1,0:T(8,128)S(1)} collective-permute-done((f32[5,16,128]{2,1,0:T(8,128)S(1)}, f32[5,16,128]{2,1,0:T(8,128)S(1)}, u32[]{:S(2)}, u32[]{:S(2)}) %collective-permute-start) | collective-permute-done | bytes 40992 | tf_op jit(solution)/shard_map/ppermute | solution.py:538
  31.6 0.0 collective-permute-done.2.other
  31.6 0.7 wall_pair.1
  32.2 25.6 %all_to_all.15 = f32[16,24,128]{2,1,0:T(8,128)S(1)} all-to-all(f32[16,24,128]{2,1,0:T(8,128)S(1)} %bitcast.13), channel_id=1, replica_groups={{0,2,4,6,8,10,12,14,16,18,20,22,24,26,28,30},{1,3,5,7,9,11,13,15,17,19,..., dimensions={0} | all-to-all | bytes 393216 | tf_op jit(solution)/shard_map/all_to_all | solution.py:477
  57.8 0.9 %wall_solve.1 = f32[128,128]{1,0:T(8,128)} custom-call(f32[384,128]{1,0:T(8,128)S(1)} %bitcast.11), custom_call_target="tpu_custom_call" | custom-call | tf_op jit(solution)/shard_map/wall_solve/pallas_call | solution.py:550
  58.7 8.4 %all-to-all-start.2 = ((f32[16,8,128]{2,1,0:T(8,128)}), f32[16,8,128]{2,1,0:T(8,128)S(1)}, u32[]{:S(2)}, u32[]{:S(2)}) async-start(f32[16,8,128]{2,1,0:T(8,128)} %bitcast.8), calls=%async_computation.2 | async-start | bytes 131072 | tf_op jit(solution)/shard_map/all_to_all | solution.py:477
  67.2 3.3 %collective-permute-start.3 = (f32[5,8,128]{2,1,0:T(8,128)S(1)}, f32[5,8,128]{2,1,0:T(8,128)S(1)}, u32[]{:S(2)}, u32[]{:S(2)}) collective-permute-start(f32[5,8,128]{2,1,0:T(8,128)S(1)} %get-tuple-element.28), channel_id=1, source_target_pairs={{0,2},{1,3},{2,0},{3,1},{4,6},{5,7},{6,4},{7,5},{8,10},{9,11},{10,... | collective-permute-start | bytes 61448 | tf_op jit(solution)/shard_map/ppermute | solution.py:549
  70.4 1.8 %collective-permute-done.3.taken = f32[5,8,128]{2,1,0:T(8,128)S(1)} collective-permute-done((f32[5,8,128]{2,1,0:T(8,128)S(1)}, f32[5,8,128]{2,1,0:T(8,128)S(1)}, u32[]{:S(2)}, u32[]{:S(2)}) %collective-permute-start.3) | collective-permute-done | bytes 20512 | tf_op jit(solution)/shard_map/ppermute | solution.py:549
  72.2 6.6 %all-to-all-done.2 = f32[16,8,128]{2,1,0:T(8,128)S(1)} async-done(((f32[16,8,128]{2,1,0:T(8,128)}), f32[16,8,128]{2,1,0:T(8,128)S(1)}, u32[]{:S(2)}, u32[]{:S(2)}) %all-to-all-start.2) | async-done | bytes 65568 | tf_op jit(solution)/shard_map/all_to_all | solution.py:477
  78.8 0.5 finish.1
  79.4 3.8 %collective-permute-start.4 = (f32[5,16,128]{2,1,0:T(8,128)S(1)}, f32[5,16,128]{2,1,0:T(8,128)S(1)}, u32[]{:S(2)}, u32[]{:S(2)}) collective-permute-start(f32[5,16,128]{2,1,0:T(8,128)S(1)} %get-tuple-element.30), channel_id=1, source_target_pairs={{0,1},{1,0},{2,3},{3,2},{4,5},{5,4},{6,7},{7,6},{8,9},{9,8},{10,11... | collective-permute-start | bytes 122888 | tf_op jit(solution)/shard_map/ppermute | solution.py:569
  83.2 0.8 collective-permute-done.4
  84.1 0.6 pad_maximum_fusion
  (1 shorter events, 0.0 us)
Async XLA Ops:
  0.0 24.4 %copy-start = (f32[3,5]{1,0:T(4,128)S(1)}, f32[3,5]{1,0:T(4,128)}, u32[]{:S(2)}) copy-start(f32[3,5]{1,0:T(4,128)} %table.1) | copy-start | bytes 184
  4.1 12.3 %collective-permute-start.1 = (f32[50,16,128]{2,1,0:T(8,128)S(1)}, f32[50,16,128]{2,1,0:T(8,128)S(1)}, u32[]{:S(2)}, u32[]{:S(2)}) collective-permute-start(f32[50,16,128]{2,1,0:T(8,128)S(1)} %get-tuple-element.25), channel_id=1, source_target_pairs={{0,1},{1,0},{2,3},{3,2},{4,5},{5,4},{6,7},{7,6},{8,9},{9,8},{10,11... | collective-permute-start | bytes 1228808 | tf_op jit(solution)/shard_map/ppermute | solution.py:509
  12.9 11.5 %all-to-all-start = ((f32[16,24,128]{2,1,0:T(8,128)}), f32[16,24,128]{2,1,0:T(8,128)S(1)}, u32[]{:S(2)}, u32[]{:S(2)}) async-start(f32[16,24,128]{2,1,0:T(8,128)} %get-tuple-element.18), calls=%async_computation | async-start | bytes 393216 | tf_op jit(solution)/shard_map/all_to_all | solution.py:521
  17.0 14.6 %collective-permute-start.2 = (f32[75,8,128]{2,1,0:T(8,128)S(1)}, f32[75,8,128]{2,1,0:T(8,128)S(1)}, u32[]{:S(2)}, u32[]{:S(2)}) collective-permute-start(f32[75,8,128]{2,1,0:T(8,128)S(1)} %wall_blocks.1.mine), channel_id=1, source_target_pairs={{0,2},{1,3},{2,0},{3,1},{4,6},{5,7},{6,4},{7,5},{8,10},{9,11},{10,... | collective-permute-start | bytes 921608 | tf_op jit(solution)/shard_map/ppermute | solution.py:520
  27.9 3.7 %collective-permute-start = (f32[5,16,128]{2,1,0:T(8,128)S(1)}, f32[5,16,128]{2,1,0:T(8,128)S(1)}, u32[]{:S(2)}, u32[]{:S(2)}) collective-permute-start(f32[5,16,128]{2,1,0:T(8,128)S(1)} %get-tuple-element.23), channel_id=1, source_target_pairs={{0,1},{1,0},{2,3},{3,2},{4,5},{5,4},{6,7},{7,6},{8,9},{9,8},{10,11... | collective-permute-start | bytes 122888 | tf_op jit(solution)/shard_map/ppermute | solution.py:538
  58.7 20.1 %all-to-all-start.2 = ((f32[16,8,128]{2,1,0:T(8,128)}), f32[16,8,128]{2,1,0:T(8,128)S(1)}, u32[]{:S(2)}, u32[]{:S(2)}) async-start(f32[16,8,128]{2,1,0:T(8,128)} %bitcast.8), calls=%async_computation.2 | async-start | bytes 131072 | tf_op jit(solution)/shard_map/all_to_all | solution.py:477
  67.2 5.1 %collective-permute-start.3 = (f32[5,8,128]{2,1,0:T(8,128)S(1)}, f32[5,8,128]{2,1,0:T(8,128)S(1)}, u32[]{:S(2)}, u32[]{:S(2)}) collective-permute-start(f32[5,8,128]{2,1,0:T(8,128)S(1)} %get-tuple-element.28), channel_id=1, source_target_pairs={{0,2},{1,3},{2,0},{3,1},{4,6},{5,7},{6,4},{7,5},{8,10},{9,11},{10,... | collective-permute-start | bytes 61448 | tf_op jit(solution)/shard_map/ppermute | solution.py:549
  79.4 4.7 %collective-permute-start.4 = (f32[5,16,128]{2,1,0:T(8,128)S(1)}, f32[5,16,128]{2,1,0:T(8,128)S(1)}, u32[]{:S(2)}, u32[]{:S(2)}) collective-permute-start(f32[5,16,128]{2,1,0:T(8,128)S(1)} %get-tuple-element.30), channel_id=1, source_target_pairs={{0,1},{1,0},{2,3},{3,2},{4,5},{5,4},{6,7},{7,6},{8,9},{9,8},{10,11... | collective-permute-start | bytes 122888 | tf_op jit(solution)/shard_map/ppermute | solution.py:569

commit v6 on v5

--- a/solution.py
+++ b/solution.py
@@ -7,8 +7,9 @@
 
 F32 = jnp.float32
 N = 5
-ROWS = 24
+ROWS = 32
 VEC = 19
+GIVE = 24
 ANY = pl.BlockSpec(memory_space=pl.ANY)
 HBM = pl.BlockSpec(memory_space=pltpu.HBM)
 VM = pl.BlockSpec(memory_space=pltpu.VMEM)
@@ -224,7 +225,7 @@
 
 
 def pair_kernel(
-    here, there, keep, recv, mine, other, out, give, hold, sl, su, slots, both, comp, sem
+    here, there, keep, recv, mine, other, out, hold, sl, su, slots, both, comp, sem
 ):
     _, z, core = place()
     odd = z % 2
@@ -253,19 +254,21 @@
     w = mm(ub_e, mm(w_o, lb_e), w_e)
     for c, x in enumerate(flat(mm(lb_o, lb_e)) + flat(mm(ub_e, ub_o)) + flat(w)):
         comp[c] = x
+    give = [jnp.where(even, x, y) for x, y in zip(lv, uv)] + [lv[0]]
     for c in range(N):
-        give[c] = jnp.where(even, lv[c], uv[c])
         hold[c] = lv[c]
     new_lv = [jnp.where(even, x, y) for x, y in zip(mv(lb_o, lv), lv)]
     inner = [jnp.where(even, x, y) for x, y in zip(mv(w_o, lv), uv)]
     new_uv = [jnp.where(even, x + y, x) for x, y in zip(mv(ub_e, inner), uv)]
     first = lane_iota() < 64
     base = 37 * odd
-    for r in range(ROWS):
+    for r in range(GIVE + 3):
         if r < VEC:
             x, y = comp[base + r], comp[base + VEC + r]
+        elif r < GIVE:
+            x, y = new_lv[r - VEC], new_uv[r - VEC]
         else:
-            x, y = new_lv[r - VEC], new_uv[r - VEC]
+            x, y = give[2 * (r - GIVE)], give[2 * (r - GIVE) + 1]
         x, y = halves(x, y, first)
         out[pl.ds(r, 8, stride=ROWS), :] = x
         out[pl.ds(8 * ROWS + r, 8, stride=ROWS), :] = y
@@ -392,8 +395,9 @@
         ]
 
     zero = jnp.zeros((1, 128), F32)
-    for n in range(16):
-        back[8 * n : 8 * n + 8, :] = jnp.zeros((8, 128), F32)
+    for z in range(16):
+        row = ROWS * (z ^ 1) + GIVE
+        back[8 * z + N : 8 * z + 8, :] = got[row : row + 3, :]
     a = [zero] * N
     for m in range(8):
         for c in range(N):
@@ -414,7 +418,7 @@
 
 
 def finish_kernel(
-    got, here, there, keep, recv, hold, taken, mine, other, own, send, sl, su, res, both, sem
+    got, here, there, keep, recv, hold, mine, other, own, send, sl, su, res, both, sem
 ):
     _, z, core = place()
     odd = z % 2
@@ -427,17 +431,21 @@
     for c in pair + copies:
         c.start()
     first = lane_iota() < 64
-    a, b = [], []
-    for c in range(N):
+    a, b, taken = [], [], []
+    for c in range(8):
         x = got[pl.ds(c, 8, stride=8), :]
         y = got[pl.ds(64 + c, 8, stride=8), :]
-        a.append(jnp.where(first, x, roll(y, 64)))
-        b.append(jnp.where(first, roll(x, 64), y))
+        x, y = jnp.where(first, x, roll(y, 64)), jnp.where(first, roll(x, 64), y)
+        if c < N:
+            a.append(x)
+            b.append(y)
+        else:
+            taken += [x, y]
     for c in pair:
         c.wait()
     lv_e = [jnp.where(even, hold[c], taken[c]) for c in range(N)]
     mid = mv(square([both[0, c] for c in range(25)]), a, lv_e)
-    low = mv(square([both[1, 50 + c] for c in range(25)]), mid, [taken[c] for c in range(N)])
+    low = mv(square([both[1, 50 + c] for c in range(25)]), mid, taken[:N])
     low = mv(square([both[1, 25 + c] for c in range(25)]), b, low)
     a = [jnp.where(even, x, y) for x, y in zip(a, mid)]
     b = [jnp.where(even, x, y) for x, y in zip(low, b)]
@@ -455,6 +463,14 @@
     for c in range(N):
         own[c] = res[c, core]
         send[c] = res[c, 1 - core]
+
+
+def join_kernel(own, theirs, out):
+    core = place()[2]
+    for half, ref in ((core, own), (1 - core, theirs)):
+        off = pl.multiple_of(half * 16, 16)
+        for c in range(N):
+            out[c, pl.ds(off, 16), :] = ref[c]
 
 
 def dma(n):
@@ -536,17 +552,16 @@
         name="chord_down",
     )(bc_table, flags, got, leaf0, leaf1, far(store, LEVELS, 85, 8, 128))
     there = lax.ppermute(away, "wall", swap)
-    zmsg, give, hold = pl.pallas_call(
+    zmsg, hold = pl.pallas_call(
         pair_kernel,
-        out_shape=(shape(16 * ROWS, 128), shape(N, 8, 128), shape(N, 8, 128)),
+        out_shape=(shape(16 * ROWS, 128), shape(N, 8, 128)),
         in_specs=[VM, VM, ANY, ANY, ANY, ANY],
-        out_specs=(VM, VM, VM),
+        out_specs=(VM, VM),
         scratch_shapes=[side, side, cells, both, pltpu.VMEM((75, 8, 128), F32), dma(6)],
         compiler_params=params(),
         name="wall_pair",
     )(here, there, keep, recv, mine, other)
     zgot = over_z(zmsg.reshape(16, ROWS, 128)).reshape(16 * ROWS, 128)
-    taken = lax.ppermute(give, "wall", near)
     back = pl.pallas_call(
         solve_kernel,
         out_shape=shape(128, 128),
@@ -560,17 +575,22 @@
     own, theirs = pl.pallas_call(
         finish_kernel,
         out_shape=(shape(N, 16, 128), shape(N, 16, 128)),
-        in_specs=[VM, VM, VM, ANY, ANY, VM, VM, ANY, ANY],
+        in_specs=[VM, VM, VM, ANY, ANY, VM, ANY, ANY],
         out_specs=(VM, VM),
         scratch_shapes=[side, side, cells, both, dma(6)],
         compiler_params=params(),
         name="finish",
-    )(inflow, here, there, keep, recv, hold, taken, mine, other)
+    )(inflow, here, there, keep, recv, hold, mine, other)
     theirs = lax.ppermute(theirs, "wall", swap)
-    core = lax.axis_index("wall") % 2
-    low = jnp.where(core == 0, own, theirs)
-    high = jnp.where(core == 0, theirs, own)
-    return jnp.concatenate([low, high], axis=1).reshape(N, 16, 2, 128)
+    out = pl.pallas_call(
+        join_kernel,
+        out_shape=shape(N, 32, 128),
+        in_specs=[VM, VM],
+        out_specs=VM,
+        compiler_params=params(),
+        name="join",
+    )(own, theirs)
+    return out.reshape(N, 16, 2, 128)
 
 
 def solution(mesh):

time: 85.2 us -> 87.2 us (1.023)
  blocking collectives: 25.6 us -> 48.2 us
  starting transfers between devices: 32.6 us -> 21.1 us
  waiting for transfers between devices: 15.6 us -> 7.24 us
    all_to_all x1 -> x2, blocking collectives: 25.6 us -> 48.2 us  [over_z(): return lax.all_to_all(x, 'wall', 0, 0, tiled=True, axis_index_groups=groups)]
    all_to_all x1 -> x0, starting transfers between devices: 8.41 us -> none  [over_z(): return lax.all_to_all(x, 'wall', 0, 0, tiled=True, axis_index_groups=groups)]
    all_to_all x1 -> x0, waiting for transfers between devices: 6.59 us -> none  [over_z(): return lax.all_to_all(x, 'wall', 0, 0, tiled=True, axis_index_groups=groups)]
    ppermute x1 -> x0, starting transfers between devices: 3.26 us -> none  [per_device(): taken = lax.ppermute(give, 'wall', near)]
    ppermute x1 -> x0, waiting for transfers between devices: 1.82 us -> none  [per_device(): taken = lax.ppermute(give, 'wall', near)]
  transfers between devices with their start and end apart: 7 -> 5, of which waited for: 5 -> 3; matrix products, arithmetic and copies ran while one was open for 0% -> 0% of each run, Pallas kernels for 5% -> 5%
where the time goes in v6:
time: 87.2 us; the launch traced here: 86.8 us
  blocking collectives  48.2 us (55%)
  starting transfers between devices  21.1 us (24%)
  Pallas kernels  10.2 us (12%)
  waiting for transfers between devices  7.24 us (8%)
    all_to_all x2, blocking collectives, over_z(): return lax.all_to_all(x, 'wall', 0, 0, tiled=True, axis_index_groups=groups)  48.2 us
    ppermute x1, starting transfers between devices, per_device(): recv = lax.ppermute(send, 'wall', swap)  8.79 us
    all_to_all x1, waiting for transfers between devices, per_device(): got = lax.all_to_all(msg, 'chord', 0, 0, tiled=True)  5.53 us
    pallas_call x1, Pallas kernels, per_device(): pl.pallas_call(up_kernel, out_shape=(shape(16, 24, 128), shape(50, 16, 12...  4.11 us
    ppermute x1, starting transfers between devices, per_device(): theirs = lax.ppermute(theirs, 'wall', swap)  3.98 us
    all_to_all x1, starting transfers between devices, per_device(): got = lax.all_to_all(msg, 'chord', 0, 0, tiled=True)  3.53 us
    pallas_call x1, Pallas kernels, per_device(): pl.pallas_call(down_kernel, out_shape=(shape(N, 16, 128), shape(N, 16, 12...  3.43 us
    ppermute x1, starting transfers between devices, per_device(): there = lax.ppermute(away, 'wall', swap)  2.85 us
  transfers between devices with their start and end apart: 5, of which 3 were waited for; matrix products, arithmetic and copies ran while one was open for 0% of the time, Pallas kernels for 5%

profile of v6, /device:TPU:1, one launch (start us, length us, event | category | flops | bytes accessed | tf_op | source)
XLA Modules:
  0.0 86.8 jit_solution(9206774279218162199)
XLA Ops:
  0.0 0.0 copy-start
  0.0 4.1 %chord_up.1 = (f32[16,24,128]{2,1,0:T(8,128)}, f32[50,16,128]{2,1,0:T(8,128)S(1)}, f32[50,16,128]{2,1,0:T(8,128)S(1)}, f32[110,8,128]{2,1,0:T(8,128)S(1)}, f32[1...) custom-call(f32[5]{0:T(128)} %jet.1, f32[5,32,128]{2,1,0:T(8,128)} %bitcast.19, s32[32,128]{1,0:T(8,128)} %bitcast.20, ...), custom_call_target="tpu_custom_call" | custom-call | flops 9216000 | bytes 4194304 | tf_op jit(solution)/shard_map/chord_up/pallas_call | solution.py:498
  4.1 8.8 %collective-permute-start.1 = (f32[50,16,128]{2,1,0:T(8,128)S(1)}, f32[50,16,128]{2,1,0:T(8,128)S(1)}, u32[]{:S(2)}, u32[]{:S(2)}) collective-permute-start(f32[50,16,128]{2,1,0:T(8,128)S(1)} %get-tuple-element.24), channel_id=1, source_target_pairs={{0,1},{1,0},{2,3},{3,2},{4,5},{5,4},{6,7},{7,6},{8,9},{9,8},{10,11... | collective-permute-start | bytes 1228808 | tf_op jit(solution)/shard_map/ppermute | solution.py:525
  12.9 3.5 %all-to-all-start = ((f32[16,24,128]{2,1,0:T(8,128)}), f32[16,24,128]{2,1,0:T(8,128)S(1)}, u32[]{:S(2)}, u32[]{:S(2)}) async-start(f32[16,24,128]{2,1,0:T(8,128)} %get-tuple-element.17), calls=%async_computation | async-start | bytes 393216 | tf_op jit(solution)/shard_map/all_to_all | solution.py:537
  16.5 0.0 collective-permute-done.1.recv
  16.5 0.5 wall_blocks.1.mine
  16.9 1.9 %collective-permute-start.2 = (f32[75,8,128]{2,1,0:T(8,128)S(1)}, f32[75,8,128]{2,1,0:T(8,128)S(1)}, u32[]{:S(2)}, u32[]{:S(2)}) collective-permute-start(f32[75,8,128]{2,1,0:T(8,128)S(1)} %wall_blocks.1.mine), channel_id=1, source_target_pairs={{0,2},{1,3},{2,0},{3,1},{4,6},{5,7},{6,4},{7,5},{8,10},{9,11},{10,... | collective-permute-start | bytes 921608 | tf_op jit(solution)/shard_map/ppermute | solution.py:536
  18.9 5.5 %all-to-all-done.got = f32[16,24,128]{2,1,0:T(8,128)S(1)} async-done(((f32[16,24,128]{2,1,0:T(8,128)}), f32[16,24,128]{2,1,0:T(8,128)S(1)}, u32[]{:S(2)}, u32[]{:S(2)}) %all-to-all-start) | async-done | bytes 196640 | tf_op jit(solution)/shard_map/all_to_all | solution.py:537
  24.4 0.0 copy-done
  24.4 3.4 %chord_down.1 = (f32[5,16,128]{2,1,0:T(8,128)S(1)}, f32[5,16,128]{2,1,0:T(8,128)S(1)}) custom-call(f32[3,5]{1,0:T(4,128)S(1)} %copy-done, s32[16,128]{1,0:T(8,128)} %flags.1, f32[16,24,128]{2,1,0:T(8,128)S(1)} %all-to-all-done.got, f32[110,8,128]{2,1,0:T(8,128)S(1)} %get-tuple-element.18.leaf0, f32[110,8,128]{2,1,0:T(8,128)S(1)} %get-tuple-element.19.leaf1, ...), custom_call_target="tpu_custom_call" | custom-call | flops 49999998976 | bytes 4194304 | tf_op jit(solution)/shard_map/chord_down/pallas_call | solution.py:538
  27.9 2.8 %collective-permute-start = (f32[5,16,128]{2,1,0:T(8,128)S(1)}, f32[5,16,128]{2,1,0:T(8,128)S(1)}, u32[]{:S(2)}, u32[]{:S(2)}) collective-permute-start(f32[5,16,128]{2,1,0:T(8,128)S(1)} %get-tuple-element.22), channel_id=1, source_target_pairs={{0,1},{1,0},{2,3},{3,2},{4,5},{5,4},{6,7},{7,6},{8,9},{9,8},{10,11... | collective-permute-start | bytes 122888 | tf_op jit(solution)/shard_map/ppermute | solution.py:554
  30.7 0.8 collective-permute-done.there
  31.6 0.0 collective-permute-done.2.other
  31.6 0.7 wall_pair.1
  32.3 26.6 %all_to_all.15 = f32[16,32,128]{2,1,0:T(8,128)S(1)} all-to-all(f32[16,32,128]{2,1,0:T(8,128)S(1)} %bitcast.14), channel_id=1, replica_groups={{0,2,4,6,8,10,12,14,16,18,20,22,24,26,28,30},{1,3,5,7,9,11,13,15,17,19,..., dimensions={0} | all-to-all | bytes 524288 | tf_op jit(solution)/shard_map/all_to_all | solution.py:493
  59.0 0.3 wall_solve.1
  59.3 21.5 %all_to_all.16 = f32[16,8,128]{2,1,0:T(8,128)S(1)} all-to-all(f32[16,8,128]{2,1,0:T(8,128)S(1)} %bitcast.13), channel_id=1, replica_groups={{0,2,4,6,8,10,12,14,16,18,20,22,24,26,28,30},{1,3,5,7,9,11,13,15,17,19,..., dimensions={0} | all-to-all | bytes 131072 | tf_op jit(solution)/shard_map/all_to_all | solution.py:493
  80.8 0.5 finish.1
  81.3 4.0 %collective-permute-start.3 = (f32[5,16,128]{2,1,0:T(8,128)S(1)}, f32[5,16,128]{2,1,0:T(8,128)S(1)}, u32[]{:S(2)}, u32[]{:S(2)}) collective-permute-start(f32[5,16,128]{2,1,0:T(8,128)S(1)} %get-tuple-element.28), channel_id=1, source_target_pairs={{0,1},{1,0},{2,3},{3,2},{4,5},{5,4},{6,7},{7,6},{8,9},{9,8},{10,11... | collective-permute-start | bytes 122888 | tf_op jit(solution)/shard_map/ppermute | solution.py:584
  85.3 0.8 collective-permute-done.3.theirs
  86.2 0.6 join.1
Async XLA Ops:
  0.0 24.4 %copy-start = (f32[3,5]{1,0:T(4,128)S(1)}, f32[3,5]{1,0:T(4,128)}, u32[]{:S(2)}) copy-start(f32[3,5]{1,0:T(4,128)} %table.1) | copy-start | bytes 184
  4.1 12.3 %collective-permute-start.1 = (f32[50,16,128]{2,1,0:T(8,128)S(1)}, f32[50,16,128]{2,1,0:T(8,128)S(1)}, u32[]{:S(2)}, u32[]{:S(2)}) collective-permute-start(f32[50,16,128]{2,1,0:T(8,128)S(1)} %get-tuple-element.24), channel_id=1, source_target_pairs={{0,1},{1,0},{2,3},{3,2},{4,5},{5,4},{6,7},{7,6},{8,9},{9,8},{10,11... | collective-permute-start | bytes 1228808 | tf_op jit(solution)/shard_map/ppermute | solution.py:525
  12.9 11.5 %all-to-all-start = ((f32[16,24,128]{2,1,0:T(8,128)}), f32[16,24,128]{2,1,0:T(8,128)S(1)}, u32[]{:S(2)}, u32[]{:S(2)}) async-start(f32[16,24,128]{2,1,0:T(8,128)} %get-tuple-element.17), calls=%async_computation | async-start | bytes 393216 | tf_op jit(solution)/shard_map/all_to_all | solution.py:537
  16.9 14.6 %collective-permute-start.2 = (f32[75,8,128]{2,1,0:T(8,128)S(1)}, f32[75,8,128]{2,1,0:T(8,128)S(1)}, u32[]{:S(2)}, u32[]{:S(2)}) collective-permute-start(f32[75,8,128]{2,1,0:T(8,128)S(1)} %wall_blocks.1.mine), channel_id=1, source_target_pairs={{0,2},{1,3},{2,0},{3,1},{4,6},{5,7},{6,4},{7,5},{8,10},{9,11},{10,... | collective-permute-start | bytes 921608 | tf_op jit(solution)/shard_map/ppermute | solution.py:536
  27.9 3.7 %collective-permute-start = (f32[5,16,128]{2,1,0:T(8,128)S(1)}, f32[5,16,128]{2,1,0:T(8,128)S(1)}, u32[]{:S(2)}, u32[]{:S(2)}) collective-permute-start(f32[5,16,128]{2,1,0:T(8,128)S(1)} %get-tuple-element.22), channel_id=1, source_target_pairs={{0,1},{1,0},{2,3},{3,2},{4,5},{5,4},{6,7},{7,6},{8,9},{9,8},{10,11... | collective-permute-start | bytes 122888 | tf_op jit(solution)/shard_map/ppermute | solution.py:554
  81.3 4.8 %collective-permute-start.3 = (f32[5,16,128]{2,1,0:T(8,128)S(1)}, f32[5,16,128]{2,1,0:T(8,128)S(1)}, u32[]{:S(2)}, u32[]{:S(2)}) collective-permute-start(f32[5,16,128]{2,1,0:T(8,128)S(1)} %get-tuple-element.28), channel_id=1, source_target_pairs={{0,1},{1,0},{2,3},{3,2},{4,5},{5,4},{6,7},{7,6},{8,9},{9,8},{10,11... | collective-permute-start | bytes 122888 | tf_op jit(solution)/shard_map/ppermute | solution.py:584

commit v7 on v3

--- a/solution.py
+++ b/solution.py
@@ -1,3 +1,5 @@
+import functools
+
 import jax
 import jax.numpy as jnp
 from jax import lax
@@ -12,10 +14,8 @@
 ANY = pl.BlockSpec(memory_space=pl.ANY)
 HBM = pl.BlockSpec(memory_space=pltpu.HBM)
 VM = pl.BlockSpec(memory_space=pltpu.VMEM)
-SM = pl.BlockSpec(memory_space=pltpu.SMEM)
 LIMIT = 32 << 20
-LEAF = 220
-STORE = LEAF + 510
+LEVELS = 6
 
 
 def shape(*dims):
@@ -76,26 +76,25 @@
         c.wait()
 
 
-def pack_kernel(jet, rhs, mask, xl, xu, el, eu, send, keep, rv, mk, sem):
-    _, _, core = place()
-    copies = [pltpu.make_async_copy(rhs, rv, sem.at[8]), pltpu.make_async_copy(mask, mk, sem.at[9])]
-    halves = ((send, pl.multiple_of((1 - core) * 16, 16)), (keep, pl.multiple_of(core * 16, 16)))
-    for m, (dst, off) in enumerate(halves):
-        for n, ref in enumerate((xl, xu, el, eu)):
-            copies.append(
-                pltpu.make_async_copy(
-                    ref.at[:, pl.ds(off, 16), :], dst.at[pl.ds(25 * n, 25)], sem.at[4 * m + n]
-                )
-            )
+def pack_kernel(away, jet, rhs, mask, xl, xu, el, eu, dst, rv, mk, jt, sem):
+    core = place()[2]
+    off = pl.multiple_of((1 - core if away else core) * 16, 16)
+    copies = [
+        pltpu.make_async_copy(jet, jt, sem.at[4]),
+        pltpu.make_async_copy(rhs.at[:, pl.ds(off, 16), :], rv, sem.at[5]),
+        pltpu.make_async_copy(mask.at[pl.ds(off, 16), :], mk, sem.at[6]),
+    ]
+    for n, ref in enumerate((xl, xu, el, eu)):
+        part = dst.at[pl.ds(25 * n, 25)]
+        copies.append(pltpu.make_async_copy(ref.at[:, pl.ds(off, 16), :], part, sem.at[n]))
     for c in copies:
         c.start()
-    copies[0].wait()
-    copies[1].wait()
-    for dst, off in halves:
-        m = mk[pl.ds(off, 16), :].astype(F32)
-        for c in range(N):
-            dst[100 + c] = rv[c, pl.ds(off, 16), :] + m * jet[c]
-    for c in copies[2:]:
+    for c in copies[:3]:
+        c.wait()
+    m = mk[...].astype(F32)
+    for c in range(N):
+        dst[100 + c] = rv[c] + m * jt[c]
+    for c in copies[3:]:
         c.wait()
 
 
@@ -124,7 +123,7 @@
     return flat(n[0]) + list(n[1]) + flat(n[2]) + list(n[3]) + flat(n[4])
 
 
-def up_kernel(keep, recv, msg, store, sl, su, ss, n1, n2, leaf, tree, sem):
+def up_kernel(keep, recv, msg, leaf0, leaf1, store, sl, su, ss, n1, n2, tree, sem):
     _, _, core = place()
     copies = []
     for n, (dst, first, count) in enumerate(((sl, 0, 25), (su, 25, 25), (ss, 100, N))):
@@ -147,10 +146,7 @@
         v1, v2 = zip(*[split(ss, c, r) for c in range(N)])
         u1, u2 = zip(*[split(su, c, r) for c in range(25)])
         for c, x in enumerate(l1 + v1 + l2 + v2 + u1 + u2):
-            leaf[r, c] = x
-        dst = store.at[pl.ds(110 * r, 110)]
-        saves.append(pltpu.make_async_copy(leaf.at[r], dst, sem.at[6 + r]))
-        saves[-1].start()
+            (leaf0, leaf1)[r][c] = x
         l1, l2, u1, u2 = square(l1), square(l2), square(u1), square(u2)
         lb = mm(l2, l1)
         lv = mv(l2, v1, v2)
@@ -171,8 +167,7 @@
             tree[level, c] = left[c]
         for c in range(30, 85):
             tree[level, c] = right[c]
-        dst = store.at[pl.ds(LEAF + 85 * level, 85)]
-        saves.append(pltpu.make_async_copy(tree.at[level], dst, sem.at[8 + level]))
+        saves.append(pltpu.make_async_copy(tree.at[level], store.at[level], sem.at[6 + level]))
         saves[-1].start()
         for c, x in enumerate(values_of(compose(node(left), node(right)))):
             n2[c] = x
@@ -256,17 +251,20 @@
 
 
 def down_kernel(
-    table, flags, got, store, keep, recv, scaled, vecs, sl, su, lf, tr, cs, bh, fl, sem
+    table, flags, got, leaf0, leaf1, store, keep, recv, scaled, vecs,
+    sl, su, tree, cs, bh, fl, tb, sem,
 ):
     chord, z, core = place()
     eta = eta_copies(keep, recv, sl, su, core, sem)
-    pre = [
-        pltpu.make_async_copy(store.at[pl.ds(LEAF, 510)], tr, sem.at[4]),
-        pltpu.make_async_copy(store.at[pl.ds(0, LEAF)], lf, sem.at[5]),
+    fetch = [
+        pltpu.make_async_copy(store.at[level], tree.at[level], sem.at[4 + level])
+        for level in range(LEVELS)
     ]
-    kinds = pltpu.make_async_copy(flags, fl, sem.at[6])
-    kinds.start()
-    for c in pre + eta:
+    kinds = [
+        pltpu.make_async_copy(flags, fl, sem.at[4 + LEVELS]),
+        pltpu.make_async_copy(table, tb, sem.at[5 + LEVELS]),
+    ]
+    for c in fetch[::-1] + kinds + eta:
         c.start()
     lane = lane_iota()
     group = lane // 4
@@ -311,17 +309,16 @@
     a = [pltpu.roll(x, back, 1) for x in a]
     b = [pltpu.roll(x, back, 1) for x in b]
 
-    pre[0].wait()
     for level in range(5, -1, -1):
         dist = 2 << level
-        a_mid = mv(square([tr[85 * level + c] for c in range(25)]), a, [tr[85 * level + 25 + c] for c in range(N)])
-        b_mid = mv(square([tr[85 * level + 30 + c] for c in range(25)]), b, [tr[85 * level + 55 + c] for c in range(N)])
-        b_mid = mv(square([tr[85 * level + 60 + c] for c in range(25)]), a_mid, b_mid)
+        fetch[level].wait()
+        a_mid = mv(square([tree[level, c] for c in range(25)]), a, [tree[level, 25 + c] for c in range(N)])
+        b_mid = mv(square([tree[level, 30 + c] for c in range(25)]), b, [tree[level, 55 + c] for c in range(N)])
+        b_mid = mv(square([tree[level, 60 + c] for c in range(25)]), a_mid, b_mid)
         left = (lane // dist) % 2 == 0
         if level:
             a = [jnp.where(left, x, roll(y, dist)) for x, y in zip(a, a_mid)]
             b = [jnp.where(left, x, roll(y, dist)) for x, y in zip(b_mid, b)]
-    pre[1].wait()
     even = lane % 2 == 0
     for r in range(2):
         if r == 0:
@@ -332,7 +329,7 @@
             rb = [jnp.where(left, roll(x, -2), y) for x, y in zip(b_mid, b)]
 
         def part(first, count):
-            return [lf[110 * r + first + c] for c in range(count)]
+            return [(leaf0, leaf1)[r][first + c] for c in range(count)]
 
         a1 = mv(square(part(0, 25)), ra, part(25, N))
         a2 = mv(square(part(30, 25)), a1, part(55, N))
@@ -342,7 +339,8 @@
             bh[c, r, 0:8, :] = jnp.where(even, b1[c], roll(b2[c], 1))
             bh[c, r, 8:16, :] = jnp.where(even, roll(b1[c], -1), b2[c])
 
-    kinds.wait()
+    for c in kinds:
+        c.wait()
     kind = fl[pl.ds(pl.multiple_of(core * 8, 8), 8), :]
     s = []
     for j in range(4):
@@ -350,7 +348,7 @@
     for c in range(N):
         factor = zero
         for k in range(3):
-            factor = jnp.where(kind == k, table[k, c], factor)
+            factor = jnp.where(kind == k, tb[k : k + 1, c : c + 1], factor)
         s[0][c] = jnp.where(z == 0, factor, 1.0) * s[0][c]
     for j in range(4):
         for c in range(N):
@@ -473,32 +471,46 @@
         return lax.all_to_all(x, "wall", 0, 0, tiled=True, axis_index_groups=groups)
 
     side = pltpu.VMEM((25, 2, 16, 128), F32)
-    send, keep = pl.pallas_call(
-        pack_kernel,
-        out_shape=(shape(105, 16, 128), shape(105, 16, 128)),
-        in_specs=[SM] + [HBM] * 6,
-        out_specs=(VM, VM),
-        scratch_shapes=[pltpu.VMEM((N, 32, 128), F32), pltpu.VMEM((32, 128), jnp.int32), dma(10)],
-        compiler_params=params(),
-        name="pack",
-    )(jet_source, rhs, mask, xl, xu, el, eu)
-    recv = lax.ppermute(send, "wall", swap)
-    msg, store = pl.pallas_call(
+    def pack(away):
+        return pl.pallas_call(
+            functools.partial(pack_kernel, away),
+            out_shape=shape(105, 16, 128),
+            in_specs=[HBM] * 7,
+            out_specs=VM,
+            scratch_shapes=[
+                pltpu.VMEM((N, 16, 128), F32),
+                pltpu.VMEM((16, 128), jnp.int32),
+                pltpu.SMEM((N,), F32),
+                dma(7),
+            ],
+            compiler_params=params(),
+            cost_estimate=cost(0, 2 << 20),
+            name="pack_away" if away else "pack_here",
+        )(far(jet_source, N), rhs, mask, xl, xu, el, eu)
+
+    recv = lax.ppermute(pack(True), "wall", swap)
+    keep = pack(False)
+    msg, leaf0, leaf1, store = pl.pallas_call(
         up_kernel,
-        out_shape=(shape(16, 24, 128), pltpu.HBM((STORE, 8, 128), F32)),
+        out_shape=(
+            shape(16, 24, 128),
+            shape(110, 8, 128),
+            shape(110, 8, 128),
+            pltpu.HBM((LEVELS, 85, 8, 128), F32),
+        ),
         in_specs=[ANY, ANY],
-        out_specs=(VM, HBM),
+        out_specs=(VM, VM, VM, HBM),
         scratch_shapes=[
             side,
             side,
             pltpu.VMEM((N, 2, 16, 128), F32),
             pltpu.VMEM((2, 85, 8, 128), F32),
             pltpu.VMEM((85, 8, 128), F32),
-            pltpu.VMEM((2, 110, 8, 128), F32),
-            pltpu.VMEM((6, 85, 8, 128), F32),
-            dma(14),
+            pltpu.VMEM((LEVELS, 85, 8, 128), F32),
+            dma(12),
         ],
         compiler_params=params(),
+        cost_estimate=cost(9000 * 1024, 4 << 20),
         name="chord_up",
     )(keep, recv)
     mine = pl.pallas_call(
@@ -516,21 +528,22 @@
     scaled, vecs = pl.pallas_call(
         down_kernel,
         out_shape=(shape(4, N, 8, 128), shape(2 * N, 8, 128)),
-        in_specs=[SM, HBM, VM, HBM, ANY, ANY],
+        in_specs=[HBM, HBM, VM, VM, VM, HBM, ANY, ANY],
         out_specs=(VM, VM),
         scratch_shapes=[
             side,
             side,
-            pltpu.VMEM((LEAF, 8, 128), F32),
-            pltpu.VMEM((510, 8, 128), F32),
+            pltpu.VMEM((LEVELS, 85, 8, 128), F32),
             pltpu.VMEM((85, 8, 128), F32),
             pltpu.VMEM((N, 2, 16, 128), F32),
             pltpu.VMEM((16, 128), jnp.int32),
-            dma(7),
+            pltpu.VMEM((3, N), F32),
+            dma(12),
         ],
         compiler_params=params(),
+        cost_estimate=cost(50_000_000_000, 4 << 20),
         name="chord_down",
-    )(bc_table, flags, got, far(store, STORE, 8, 128), keep, recv)
+    )(far(bc_table, 3, N), flags, got, leaf0, leaf1, far(store, LEVELS, 85, 8, 128), keep, recv)
     both = pltpu.VMEM((2, 75, 8, 128), F32)
     zmsg, give = pl.pallas_call(
         pair_kernel,

time: 86.1 us -> 82.6 us (0.959)
  blocking collectives: 36.2 us -> 24.6 us
  waiting for transfers between devices: 11.2 us -> 16.1 us
  starting transfers between devices: 27 us -> 30.4 us
    all_to_all x1 -> x0, blocking collectives: 10 us -> none  [per_device(): got = lax.all_to_all(msg, 'chord', 0, 0, tiled=True)]
    all_to_all x0 -> x1, waiting for transfers between devices: none -> 5.28 us  [per_device(): got = lax.all_to_all(msg, 'chord', 0, 0, tiled=True)]
    all_to_all x0 -> x1, starting transfers between devices: none -> 3.53 us  [per_device(): got = lax.all_to_all(msg, 'chord', 0, 0, tiled=True)]
    all_to_all x1, blocking collectives: 26.2 us -> 24.6 us  [over_z(): return lax.all_to_all(x, 'wall', 0, 0, tiled=True, axis_index_groups=groups)]
    ppermute x1, waiting for transfers between devices: 2 us -> 0.64 us  [per_device(): recv = lax.ppermute(pack(True), 'wall', swap)]
    pallas_call x2 -> x3, Pallas kernels: 4.53 us -> 5.67 us  [the longest x1 3 us: per_device(): pl.pallas_call(up_kernel, out_shape=(shape(16, 24, 128), shape(110, 8, 12...]
    ppermute x1, starting transfers between devices: 6.01 us -> 5.1 us  [per_device(): theirs = lax.ppermute(theirs, 'wall', swap)]
    ppermute x1, waiting for transfers between devices: 0.01 us -> 0.87 us  [per_device(): other = lax.ppermute(mine, 'wall', near)]
  transfers between devices with their start and end apart: 5 -> 6, of which waited for: 4 -> 6; matrix products, arithmetic and copies ran while one was open for 0% -> 0% of each run, Pallas kernels for 6% -> 5%
where the time goes in v7:
time: 82.6 us; the launch traced here: 82.2 us
  starting transfers between devices  30.4 us (37%)
  blocking collectives  24.6 us (30%)
  waiting for transfers between devices  16.1 us (19%)
  Pallas kernels  10.3 us (12%)
    all_to_all x1, blocking collectives, over_z(): return lax.all_to_all(x, 'wall', 0, 0, tiled=True, axis_index_groups=groups)  24.6 us
    ppermute x1, starting transfers between devices, per_device(): recv = lax.ppermute(pack(True), 'wall', swap)  8.79 us
    all_to_all x1, starting transfers between devices, over_z(): return lax.all_to_all(x, 'wall', 0, 0, tiled=True, axis_index_groups=groups)  7.8 us
    all_to_all x1, waiting for transfers between devices, over_z(): return lax.all_to_all(x, 'wall', 0, 0, tiled=True, axis_index_groups=groups)  6.92 us
    all_to_all x1, waiting for transfers between devices, per_device(): got = lax.all_to_all(msg, 'chord', 0, 0, tiled=True)  5.28 us
    ppermute x1, starting transfers between devices, per_device(): theirs = lax.ppermute(theirs, 'wall', swap)  5.1 us
    all_to_all x1, starting transfers between devices, per_device(): got = lax.all_to_all(msg, 'chord', 0, 0, tiled=True)  3.53 us
    ppermute x1, starting transfers between devices, per_device(): taken = lax.ppermute(give, 'wall', near)  3.26 us
  transfers between devices with their start and end apart: 6, of which 6 were waited for; matrix products, arithmetic and copies ran while one was open for 0% of the time, Pallas kernels for 5%

profile of v7, /device:TPU:1, one launch (start us, length us, event | category | flops | bytes accessed | tf_op | source)
XLA Modules:
  0.0 82.2 jit_solution(11530262853331207398)
XLA Ops:
  0.0 1.3 %pack_away.1 = f32[105,16,128]{2,1,0:T(8,128)S(1)} custom-call(f32[5]{0:T(128)} %jet.3, f32[5,32,128]{2,1,0:T(8,128)} %bitcast.22, s32[32,128]{1,0:T(8,128)} %bitcast.24, f32[25,32,128]{2,1,0:T(8,128)} %bitcast.14, f32[25,32,128]{2,1,0:T(8,128)} %bitcast.16, f32[25,32,128]{2,1,0:T(8,128)} %bitcast.18, f32[25,32,128]{2,1,0:T(8,128)} %bitcast.20), custom_call_target="tpu_custom_call" | custom-call | bytes 2097152 | tf_op jit(solution)/shard_map/pack_away/pallas_call | solution.py:475
  1.3 8.8 %collective-permute-start = (f32[105,16,128]{2,1,0:T(8,128)S(1)}, f32[105,16,128]{2,1,0:T(8,128)S(1)}, u32[]{:S(2)}, u32[]{:S(2)}) collective-permute-start(f32[105,16,128]{2,1,0:T(8,128)S(1)} %pack_away.1), channel_id=1, source_target_pairs={{0,1},{1,0},{2,3},{3,2},{4,5},{5,4},{6,7},{7,6},{8,9},{9,8},{10,11... | collective-permute-start | bytes 2580488 | tf_op jit(solution)/shard_map/ppermute | solution.py:491
  10.1 1.3 %pack_here.1.keep = f32[105,16,128]{2,1,0:T(8,128)S(1)} custom-call(f32[5]{0:T(128)} %jet.3, f32[5,32,128]{2,1,0:T(8,128)} %bitcast.23, s32[32,128]{1,0:T(8,128)} %bitcast.25, f32[25,32,128]{2,1,0:T(8,128)} %bitcast.15, f32[25,32,128]{2,1,0:T(8,128)} %bitcast.17, f32[25,32,128]{2,1,0:T(8,128)} %bitcast.19, f32[25,32,128]{2,1,0:T(8,128)} %bitcast.21), custom_call_target="tpu_custom_call" | custom-call | bytes 2097152 | tf_op jit(solution)/shard_map/pack_here/pallas_call | solution.py:475
  11.5 0.6 collective-permute-done.recv
  12.1 3.0 %chord_up.1 = (f32[16,24,128]{2,1,0:T(8,128)}, f32[110,8,128]{2,1,0:T(8,128)S(1)}, f32[110,8,128]{2,1,0:T(8,128)S(1)}, f32[6,85,8,128]{3,2,1,0:T(8,128)}) custom-call(f32[105,16,128]{2,1,0:T(8,128)S(1)} %pack_here.1.keep, f32[105,16,128]{2,1,0:T(8,128)S(1)} %collective-permute-done.recv), custom_call_target="tpu_custom_call" | custom-call | flops 9216000 | bytes 4194304 | tf_op jit(solution)/shard_map/chord_up/pallas_call | solution.py:493
  15.1 3.5 %all-to-all-start = ((f32[16,24,128]{2,1,0:T(8,128)}), f32[16,24,128]{2,1,0:T(8,128)S(1)}, u32[]{:S(2)}, u32[]{:S(2)}) async-start(f32[16,24,128]{2,1,0:T(8,128)} %get-tuple-element.15), calls=%async_computation | async-start | bytes 393216 | tf_op jit(solution)/shard_map/all_to_all | solution.py:527
  18.7 0.5 wall_blocks.1.mine
  19.2 1.9 %collective-permute-start.1 = (f32[75,8,128]{2,1,0:T(8,128)S(1)}, f32[75,8,128]{2,1,0:T(8,128)S(1)}, u32[]{:S(2)}, u32[]{:S(2)}) collective-permute-start(f32[75,8,128]{2,1,0:T(8,128)S(1)} %wall_blocks.1.mine), channel_id=1, source_target_pairs={{0,2},{1,3},{2,0},{3,1},{4,6},{5,7},{6,4},{7,5},{8,10},{9,11},{10,... | collective-permute-start | bytes 921608 | tf_op jit(solution)/shard_map/ppermute | solution.py:526
  21.1 5.3 %all-to-all-done.got = f32[16,24,128]{2,1,0:T(8,128)S(1)} async-done(((f32[16,24,128]{2,1,0:T(8,128)}), f32[16,24,128]{2,1,0:T(8,128)S(1)}, u32[]{:S(2)}, u32[]{:S(2)}) %all-to-all-start) | async-done | bytes 196640 | tf_op jit(solution)/shard_map/all_to_all | solution.py:527
  26.4 2.3 %chord_down.1 = (f32[4,5,8,128]{3,2,1,0:T(8,128)S(1)}, f32[10,8,128]{2,1,0:T(8,128)S(1)}) custom-call(f32[3,5]{1,0:T(4,128)} %table.1, s32[16,128]{1,0:T(8,128)} %flags.1, f32[16,24,128]{2,1,0:T(8,128)S(1)} %all-to-all-done.got, f32[110,8,128]{2,1,0:T(8,128)S(1)} %get-tuple-element.16.leaf0, f32[110,8,128]{2,1,0:T(8,128)S(1)} %get-tuple-element.17.leaf1, ...), custom_call_target="tpu_custom_call" | custom-call | flops 49999998976 | bytes 4194304 | tf_op jit(solution)/shard_map/chord_down/pallas_call | solution.py:528
  28.7 0.9 %collective-permute-done.1.other = f32[75,8,128]{2,1,0:T(8,128)S(1)} collective-permute-done((f32[75,8,128]{2,1,0:T(8,128)S(1)}, f32[75,8,128]{2,1,0:T(8,128)S(1)}, u32[]{:S(2)}, u32[]{:S(2)}) %collective-permute-start.1) | collective-permute-done | bytes 307232 | tf_op jit(solution)/shard_map/ppermute | solution.py:526
  29.5 0.4 wall_pair.1
  30.0 24.6 %all_to_all.15 = f32[16,24,128]{2,1,0:T(8,128)S(1)} all-to-all(f32[16,24,128]{2,1,0:T(8,128)S(1)} %bitcast.13), channel_id=1, replica_groups={{0,2,4,6,8,10,12,14,16,18,20,22,24,26,28,30},{1,3,5,7,9,11,13,15,17,19,..., dimensions={0} | all-to-all | bytes 393216 | tf_op jit(solution)/shard_map/all_to_all | solution.py:471
  54.6 0.9 %wall_solve.1 = f32[128,128]{1,0:T(8,128)} custom-call(f32[384,128]{1,0:T(8,128)S(1)} %bitcast.11), custom_call_target="tpu_custom_call" | custom-call | tf_op jit(solution)/shard_map/wall_solve/pallas_call | solution.py:559
  55.5 7.8 %all-to-all-start.2 = ((f32[16,8,128]{2,1,0:T(8,128)}), f32[16,8,128]{2,1,0:T(8,128)S(1)}, u32[]{:S(2)}, u32[]{:S(2)}) async-start(f32[16,8,128]{2,1,0:T(8,128)} %bitcast.8), calls=%async_computation.2 | async-start | bytes 131072 | tf_op jit(solution)/shard_map/all_to_all | solution.py:471
  63.3 3.3 %collective-permute-start.2 = (f32[5,8,128]{2,1,0:T(8,128)S(1)}, f32[5,8,128]{2,1,0:T(8,128)S(1)}, u32[]{:S(2)}, u32[]{:S(2)}) collective-permute-start(f32[5,8,128]{2,1,0:T(8,128)S(1)} %get-tuple-element.22), channel_id=1, source_target_pairs={{0,2},{1,3},{2,0},{3,1},{4,6},{5,7},{6,4},{7,5},{8,10},{9,11},{10,... | collective-permute-start | bytes 61448 | tf_op jit(solution)/shard_map/ppermute | solution.py:558
  66.6 1.5 %collective-permute-done.2.taken = f32[5,8,128]{2,1,0:T(8,128)S(1)} collective-permute-done((f32[5,8,128]{2,1,0:T(8,128)S(1)}, f32[5,8,128]{2,1,0:T(8,128)S(1)}, u32[]{:S(2)}, u32[]{:S(2)}) %collective-permute-start.2) | collective-permute-done | bytes 20512 | tf_op jit(solution)/shard_map/ppermute | solution.py:558
  68.1 6.9 %all-to-all-done.2 = f32[16,8,128]{2,1,0:T(8,128)S(1)} async-done(((f32[16,8,128]{2,1,0:T(8,128)}), f32[16,8,128]{2,1,0:T(8,128)S(1)}, u32[]{:S(2)}, u32[]{:S(2)}) %all-to-all-start.2) | async-done | bytes 65568 | tf_op jit(solution)/shard_map/all_to_all | solution.py:471
  75.0 0.5 finish.1
  75.6 5.1 %collective-permute-start.3 = (f32[5,16,128]{2,1,0:T(8,128)S(1)}, f32[5,16,128]{2,1,0:T(8,128)S(1)}, u32[]{:S(2)}, u32[]{:S(2)}) collective-permute-start(f32[5,16,128]{2,1,0:T(8,128)S(1)} %get-tuple-element.24), channel_id=1, source_target_pairs={{0,1},{1,0},{2,3},{3,2},{4,5},{5,4},{6,7},{7,6},{8,9},{9,8},{10,11... | collective-permute-start | bytes 122888 | tf_op jit(solution)/shard_map/ppermute | solution.py:578
  80.7 0.8 %collective-permute-done.3 = f32[5,16,128]{2,1,0:T(8,128)S(1)} collective-permute-done((f32[5,16,128]{2,1,0:T(8,128)S(1)}, f32[5,16,128]{2,1,0:T(8,128)S(1)}, u32[]{:S(2)}, u32[]{:S(2)}) %collective-permute-start.3) | collective-permute-done | bytes 40992 | tf_op jit(solution)/shard_map/ppermute | solution.py:578
  81.5 0.6 pad_maximum_fusion
  (1 shorter events, 0.0 us)
Async XLA Ops:
  1.3 10.8 %collective-permute-start = (f32[105,16,128]{2,1,0:T(8,128)S(1)}, f32[105,16,128]{2,1,0:T(8,128)S(1)}, u32[]{:S(2)}, u32[]{:S(2)}) collective-permute-start(f32[105,16,128]{2,1,0:T(8,128)S(1)} %pack_away.1), channel_id=1, source_target_pairs={{0,1},{1,0},{2,3},{3,2},{4,5},{5,4},{6,7},{7,6},{8,9},{9,8},{10,11... | collective-permute-start | bytes 2580488 | tf_op jit(solution)/shard_map/ppermute | solution.py:491
  15.1 11.2 %all-to-all-start = ((f32[16,24,128]{2,1,0:T(8,128)}), f32[16,24,128]{2,1,0:T(8,128)S(1)}, u32[]{:S(2)}, u32[]{:S(2)}) async-start(f32[16,24,128]{2,1,0:T(8,128)} %get-tuple-element.15), calls=%async_computation | async-start | bytes 393216 | tf_op jit(solution)/shard_map/all_to_all | solution.py:527
  19.2 10.4 %collective-permute-start.1 = (f32[75,8,128]{2,1,0:T(8,128)S(1)}, f32[75,8,128]{2,1,0:T(8,128)S(1)}, u32[]{:S(2)}, u32[]{:S(2)}) collective-permute-start(f32[75,8,128]{2,1,0:T(8,128)S(1)} %wall_blocks.1.mine), channel_id=1, source_target_pairs={{0,2},{1,3},{2,0},{3,1},{4,6},{5,7},{6,4},{7,5},{8,10},{9,11},{10,... | collective-permute-start | bytes 921608 | tf_op jit(solution)/shard_map/ppermute | solution.py:526
  55.5 19.5 %all-to-all-start.2 = ((f32[16,8,128]{2,1,0:T(8,128)}), f32[16,8,128]{2,1,0:T(8,128)S(1)}, u32[]{:S(2)}, u32[]{:S(2)}) async-start(f32[16,8,128]{2,1,0:T(8,128)} %bitcast.8), calls=%async_computation.2 | async-start | bytes 131072 | tf_op jit(solution)/shard_map/all_to_all | solution.py:471
  63.3 4.8 %collective-permute-start.2 = (f32[5,8,128]{2,1,0:T(8,128)S(1)}, f32[5,8,128]{2,1,0:T(8,128)S(1)}, u32[]{:S(2)}, u32[]{:S(2)}) collective-permute-start(f32[5,8,128]{2,1,0:T(8,128)S(1)} %get-tuple-element.22), channel_id=1, source_target_pairs={{0,2},{1,3},{2,0},{3,1},{4,6},{5,7},{6,4},{7,5},{8,10},{9,11},{10,... | collective-permute-start | bytes 61448 | tf_op jit(solution)/shard_map/ppermute | solution.py:558
  75.6 6.0 %collective-permute-start.3 = (f32[5,16,128]{2,1,0:T(8,128)S(1)}, f32[5,16,128]{2,1,0:T(8,128)S(1)}, u32[]{:S(2)}, u32[]{:S(2)}) collective-permute-start(f32[5,16,128]{2,1,0:T(8,128)S(1)} %get-tuple-element.24), channel_id=1, source_target_pairs={{0,1},{1,0},{2,3},{3,2},{4,5},{5,4},{6,7},{7,6},{8,9},{9,8},{10,11... | collective-permute-start | bytes 122888 | tf_op jit(solution)/shard_map/ppermute | solution.py:578

commit v8 on v7

--- a/solution.py
+++ b/solution.py
@@ -80,13 +80,14 @@
     core = place()[2]
     off = pl.multiple_of((1 - core if away else core) * 16, 16)
     copies = [
-        pltpu.make_async_copy(jet, jt, sem.at[4]),
-        pltpu.make_async_copy(rhs.at[:, pl.ds(off, 16), :], rv, sem.at[5]),
-        pltpu.make_async_copy(mask.at[pl.ds(off, 16), :], mk, sem.at[6]),
-    ]
-    for n, ref in enumerate((xl, xu, el, eu)):
-        part = dst.at[pl.ds(25 * n, 25)]
-        copies.append(pltpu.make_async_copy(ref.at[:, pl.ds(off, 16), :], part, sem.at[n]))
+        pltpu.make_async_copy(jet, jt, sem.at[20]),
+        pltpu.make_async_copy(rhs.at[:, pl.ds(off, 16), :], rv, sem.at[21]),
+        pltpu.make_async_copy(mask.at[pl.ds(off, 16), :], mk, sem.at[22]),
+    ]
+    for n in range(20):
+        ref = (xl, xu, el, eu)[n // 5]
+        part = ref.at[pl.ds(N * (n % 5), N), pl.ds(off, 16), :]
+        copies.append(pltpu.make_async_copy(part, dst.at[pl.ds(N * n, N)], sem.at[n]))
     for c in copies:
         c.start()
     for c in copies[:3]:
@@ -123,28 +124,23 @@
     return flat(n[0]) + list(n[1]) + flat(n[2]) + list(n[3]) + flat(n[4])
 
 
-def up_kernel(keep, recv, msg, leaf0, leaf1, store, sl, su, ss, n1, n2, tree, sem):
-    _, _, core = place()
-    copies = []
-    for n, (dst, first, count) in enumerate(((sl, 0, 25), (su, 25, 25), (ss, 100, N))):
-        part = pl.ds(first, count)
-        copies.append(pltpu.make_async_copy(keep.at[part], dst.at[:, core], sem.at[2 * n]))
-        copies.append(pltpu.make_async_copy(recv.at[part], dst.at[:, 1 - core], sem.at[2 * n + 1]))
-    copy_all(copies)
+def up_kernel(keep, recv, msg, leaf0, leaf1, store, n1, n2, tree, sem):
+    core = place()[2]
     lane = lane_iota()
     even = lane % 2 == 0
     low = (lane // 2) % 2 == 0
 
-    def split(ref, c, r):
-        a = ref[c, r, 0:8, :]
-        b = ref[c, r, 8:16, :]
+    def split(c, r):
+        stays = core == r
+        a = jnp.where(stays, keep[c, 0:8, :], recv[c, 0:8, :])
+        b = jnp.where(stays, keep[c, 8:16, :], recv[c, 8:16, :])
         return jnp.where(even, a, roll(b, 1)), jnp.where(even, roll(a, -1), b)
 
     saves = []
     for r in range(2):
-        l1, l2 = zip(*[split(sl, c, r) for c in range(25)])
-        v1, v2 = zip(*[split(ss, c, r) for c in range(N)])
-        u1, u2 = zip(*[split(su, c, r) for c in range(25)])
+        l1, l2 = zip(*[split(c, r) for c in range(25)])
+        v1, v2 = zip(*[split(100 + c, r) for c in range(N)])
+        u1, u2 = zip(*[split(25 + c, r) for c in range(25)])
         for c, x in enumerate(l1 + v1 + l2 + v2 + u1 + u2):
             (leaf0, leaf1)[r][c] = x
         l1, l2, u1, u2 = square(l1), square(l2), square(u1), square(u2)
@@ -167,7 +163,7 @@
             tree[level, c] = left[c]
         for c in range(30, 85):
             tree[level, c] = right[c]
-        saves.append(pltpu.make_async_copy(tree.at[level], store.at[level], sem.at[6 + level]))
+        saves.append(pltpu.make_async_copy(tree.at[level], store.at[level], sem.at[level]))
         saves[-1].start()
         for c, x in enumerate(values_of(compose(node(left), node(right)))):
             n2[c] = x
@@ -481,7 +477,7 @@
                 pltpu.VMEM((N, 16, 128), F32),
                 pltpu.VMEM((16, 128), jnp.int32),
                 pltpu.SMEM((N,), F32),
-                dma(7),
+                dma(23),
             ],
             compiler_params=params(),
             cost_estimate=cost(0, 2 << 20),
@@ -498,16 +494,13 @@
             shape(110, 8, 128),
             pltpu.HBM((LEVELS, 85, 8, 128), F32),
         ),
-        in_specs=[ANY, ANY],
+        in_specs=[VM, VM],
         out_specs=(VM, VM, VM, HBM),
         scratch_shapes=[
-            side,
-            side,
-            pltpu.VMEM((N, 2, 16, 128), F32),
             pltpu.VMEM((2, 85, 8, 128), F32),
             pltpu.VMEM((85, 8, 128), F32),
             pltpu.VMEM((LEVELS, 85, 8, 128), F32),
-            dma(12),
+            dma(LEVELS),
         ],
         compiler_params=params(),
         cost_estimate=cost(9000 * 1024, 4 << 20),

time: 82.6 us -> 82.6 us (level)
  no operation moved by 1% of the time
where the time goes in v8:
time: 82.6 us; the launch traced here: 82.1 us
  starting transfers between devices  30.4 us (37%)
  blocking collectives  24.6 us (30%)
  waiting for transfers between devices  16.1 us (19%)
  Pallas kernels  10.2 us (12%)
    all_to_all x1, blocking collectives, over_z(): return lax.all_to_all(x, 'wall', 0, 0, tiled=True, axis_index_groups=groups)  24.6 us
    ppermute x1, starting transfers between devices, per_device(): recv = lax.ppermute(pack(True), 'wall', swap)  8.79 us
    all_to_all x1, starting transfers between devices, over_z(): return lax.all_to_all(x, 'wall', 0, 0, tiled=True, axis_index_groups=groups)  7.8 us
    all_to_all x1, waiting for transfers between devices, over_z(): return lax.all_to_all(x, 'wall', 0, 0, tiled=True, axis_index_groups=groups)  6.92 us
    all_to_all x1, waiting for transfers between devices, per_device(): got = lax.all_to_all(msg, 'chord', 0, 0, tiled=True)  5.28 us
    ppermute x1, starting transfers between devices, per_device(): theirs = lax.ppermute(theirs, 'wall', swap)  5.1 us
    all_to_all x1, starting transfers between devices, per_device(): got = lax.all_to_all(msg, 'chord', 0, 0, tiled=True)  3.53 us
    ppermute x1, starting transfers between devices, per_device(): taken = lax.ppermute(give, 'wall', near)  3.26 us
  transfers between devices with their start and end apart: 6, of which 6 were waited for; matrix products, arithmetic and copies ran while one was open for 0% of the time, Pallas kernels for 5%

profile of v8, /device:TPU:1, one launch (start us, length us, event | category | flops | bytes accessed | tf_op | source)
XLA Modules:
  0.0 82.1 jit_solution(13822922940402545093)
XLA Ops:
  0.0 1.3 %pack_away.1 = f32[105,16,128]{2,1,0:T(8,128)S(1)} custom-call(f32[5]{0:T(128)} %jet.3, f32[5,32,128]{2,1,0:T(8,128)} %bitcast.22, s32[32,128]{1,0:T(8,128)} %bitcast.24, f32[25,32,128]{2,1,0:T(8,128)} %bitcast.14, f32[25,32,128]{2,1,0:T(8,128)} %bitcast.16, f32[25,32,128]{2,1,0:T(8,128)} %bitcast.18, f32[25,32,128]{2,1,0:T(8,128)} %bitcast.20), custom_call_target="tpu_custom_call" | custom-call | bytes 2097152 | tf_op jit(solution)/shard_map/pack_away/pallas_call | solution.py:471
  1.4 8.8 %collective-permute-start = (f32[105,16,128]{2,1,0:T(8,128)S(1)}, f32[105,16,128]{2,1,0:T(8,128)S(1)}, u32[]{:S(2)}, u32[]{:S(2)}) collective-permute-start(f32[105,16,128]{2,1,0:T(8,128)S(1)} %pack_away.1), channel_id=1, source_target_pairs={{0,1},{1,0},{2,3},{3,2},{4,5},{5,4},{6,7},{7,6},{8,9},{9,8},{10,11... | collective-permute-start | bytes 2580488 | tf_op jit(solution)/shard_map/ppermute | solution.py:487
  10.1 1.4 %pack_here.1.keep = f32[105,16,128]{2,1,0:T(8,128)S(1)} custom-call(f32[5]{0:T(128)} %jet.3, f32[5,32,128]{2,1,0:T(8,128)} %bitcast.23, s32[32,128]{1,0:T(8,128)} %bitcast.25, f32[25,32,128]{2,1,0:T(8,128)} %bitcast.15, f32[25,32,128]{2,1,0:T(8,128)} %bitcast.17, f32[25,32,128]{2,1,0:T(8,128)} %bitcast.19, f32[25,32,128]{2,1,0:T(8,128)} %bitcast.21), custom_call_target="tpu_custom_call" | custom-call | bytes 2097152 | tf_op jit(solution)/shard_map/pack_here/pallas_call | solution.py:471
  11.5 0.6 collective-permute-done.recv
  12.1 2.9 %chord_up.1 = (f32[16,24,128]{2,1,0:T(8,128)}, f32[110,8,128]{2,1,0:T(8,128)S(1)}, f32[110,8,128]{2,1,0:T(8,128)S(1)}, f32[6,85,8,128]{3,2,1,0:T(8,128)}) custom-call(f32[105,16,128]{2,1,0:T(8,128)S(1)} %pack_here.1.keep, f32[105,16,128]{2,1,0:T(8,128)S(1)} %collective-permute-done.recv), custom_call_target="tpu_custom_call" | custom-call | flops 9216000 | bytes 4194304 | tf_op jit(solution)/shard_map/chord_up/pallas_call | solution.py:489
  15.0 3.5 %all-to-all-start = ((f32[16,24,128]{2,1,0:T(8,128)}), f32[16,24,128]{2,1,0:T(8,128)S(1)}, u32[]{:S(2)}, u32[]{:S(2)}) async-start(f32[16,24,128]{2,1,0:T(8,128)} %get-tuple-element.15), calls=%async_computation | async-start | bytes 393216 | tf_op jit(solution)/shard_map/all_to_all | solution.py:520
  18.6 0.5 wall_blocks.1.mine
  19.1 1.9 %collective-permute-start.1 = (f32[75,8,128]{2,1,0:T(8,128)S(1)}, f32[75,8,128]{2,1,0:T(8,128)S(1)}, u32[]{:S(2)}, u32[]{:S(2)}) collective-permute-start(f32[75,8,128]{2,1,0:T(8,128)S(1)} %wall_blocks.1.mine), channel_id=1, source_target_pairs={{0,2},{1,3},{2,0},{3,1},{4,6},{5,7},{6,4},{7,5},{8,10},{9,11},{10,... | collective-permute-start | bytes 921608 | tf_op jit(solution)/shard_map/ppermute | solution.py:519
  21.0 5.3 %all-to-all-done.got = f32[16,24,128]{2,1,0:T(8,128)S(1)} async-done(((f32[16,24,128]{2,1,0:T(8,128)}), f32[16,24,128]{2,1,0:T(8,128)S(1)}, u32[]{:S(2)}, u32[]{:S(2)}) %all-to-all-start) | async-done | bytes 196640 | tf_op jit(solution)/shard_map/all_to_all | solution.py:520
  26.3 2.3 %chord_down.1 = (f32[4,5,8,128]{3,2,1,0:T(8,128)S(1)}, f32[10,8,128]{2,1,0:T(8,128)S(1)}) custom-call(f32[3,5]{1,0:T(4,128)} %table.1, s32[16,128]{1,0:T(8,128)} %flags.1, f32[16,24,128]{2,1,0:T(8,128)S(1)} %all-to-all-done.got, f32[110,8,128]{2,1,0:T(8,128)S(1)} %get-tuple-element.16.leaf0, f32[110,8,128]{2,1,0:T(8,128)S(1)} %get-tuple-element.17.leaf1, ...), custom_call_target="tpu_custom_call" | custom-call | flops 49999998976 | bytes 4194304 | tf_op jit(solution)/shard_map/chord_down/pallas_call | solution.py:521
  28.6 0.9 %collective-permute-done.1.other = f32[75,8,128]{2,1,0:T(8,128)S(1)} collective-permute-done((f32[75,8,128]{2,1,0:T(8,128)S(1)}, f32[75,8,128]{2,1,0:T(8,128)S(1)}, u32[]{:S(2)}, u32[]{:S(2)}) %collective-permute-start.1) | collective-permute-done | bytes 307232 | tf_op jit(solution)/shard_map/ppermute | solution.py:519
  29.4 0.4 wall_pair.1
  29.9 24.6 %all_to_all.15 = f32[16,24,128]{2,1,0:T(8,128)S(1)} all-to-all(f32[16,24,128]{2,1,0:T(8,128)S(1)} %bitcast.13), channel_id=1, replica_groups={{0,2,4,6,8,10,12,14,16,18,20,22,24,26,28,30},{1,3,5,7,9,11,13,15,17,19,..., dimensions={0} | all-to-all | bytes 393216 | tf_op jit(solution)/shard_map/all_to_all | solution.py:467
  54.5 0.9 %wall_solve.1 = f32[128,128]{1,0:T(8,128)} custom-call(f32[384,128]{1,0:T(8,128)S(1)} %bitcast.11), custom_call_target="tpu_custom_call" | custom-call | tf_op jit(solution)/shard_map/wall_solve/pallas_call | solution.py:552
  55.4 7.8 %all-to-all-start.2 = ((f32[16,8,128]{2,1,0:T(8,128)}), f32[16,8,128]{2,1,0:T(8,128)S(1)}, u32[]{:S(2)}, u32[]{:S(2)}) async-start(f32[16,8,128]{2,1,0:T(8,128)} %bitcast.8), calls=%async_computation.2 | async-start | bytes 131072 | tf_op jit(solution)/shard_map/all_to_all | solution.py:467
  63.2 3.3 %collective-permute-start.2 = (f32[5,8,128]{2,1,0:T(8,128)S(1)}, f32[5,8,128]{2,1,0:T(8,128)S(1)}, u32[]{:S(2)}, u32[]{:S(2)}) collective-permute-start(f32[5,8,128]{2,1,0:T(8,128)S(1)} %get-tuple-element.22), channel_id=1, source_target_pairs={{0,2},{1,3},{2,0},{3,1},{4,6},{5,7},{6,4},{7,5},{8,10},{9,11},{10,... | collective-permute-start | bytes 61448 | tf_op jit(solution)/shard_map/ppermute | solution.py:551
  66.5 1.5 %collective-permute-done.2.taken = f32[5,8,128]{2,1,0:T(8,128)S(1)} collective-permute-done((f32[5,8,128]{2,1,0:T(8,128)S(1)}, f32[5,8,128]{2,1,0:T(8,128)S(1)}, u32[]{:S(2)}, u32[]{:S(2)}) %collective-permute-start.2) | collective-permute-done | bytes 20512 | tf_op jit(solution)/shard_map/ppermute | solution.py:551
  68.0 6.9 %all-to-all-done.2 = f32[16,8,128]{2,1,0:T(8,128)S(1)} async-done(((f32[16,8,128]{2,1,0:T(8,128)}), f32[16,8,128]{2,1,0:T(8,128)S(1)}, u32[]{:S(2)}, u32[]{:S(2)}) %all-to-all-start.2) | async-done | bytes 65568 | tf_op jit(solution)/shard_map/all_to_all | solution.py:467
  74.9 0.5 finish.1
  75.5 5.1 %collective-permute-start.3 = (f32[5,16,128]{2,1,0:T(8,128)S(1)}, f32[5,16,128]{2,1,0:T(8,128)S(1)}, u32[]{:S(2)}, u32[]{:S(2)}) collective-permute-start(f32[5,16,128]{2,1,0:T(8,128)S(1)} %get-tuple-element.24), channel_id=1, source_target_pairs={{0,1},{1,0},{2,3},{3,2},{4,5},{5,4},{6,7},{7,6},{8,9},{9,8},{10,11... | collective-permute-start | bytes 122888 | tf_op jit(solution)/shard_map/ppermute | solution.py:571
  80.6 0.8 %collective-permute-done.3 = f32[5,16,128]{2,1,0:T(8,128)S(1)} collective-permute-done((f32[5,16,128]{2,1,0:T(8,128)S(1)}, f32[5,16,128]{2,1,0:T(8,128)S(1)}, u32[]{:S(2)}, u32[]{:S(2)}) %collective-permute-start.3) | collective-permute-done | bytes 40992 | tf_op jit(solution)/shard_map/ppermute | solution.py:571
  81.4 0.6 pad_maximum_fusion
  (1 shorter events, 0.0 us)
Async XLA Ops:
  1.4 10.8 %collective-permute-start = (f32[105,16,128]{2,1,0:T(8,128)S(1)}, f32[105,16,128]{2,1,0:T(8,128)S(1)}, u32[]{:S(2)}, u32[]{:S(2)}) collective-permute-start(f32[105,16,128]{2,1,0:T(8,128)S(1)} %pack_away.1), channel_id=1, source_target_pairs={{0,1},{1,0},{2,3},{3,2},{4,5},{5,4},{6,7},{7,6},{8,9},{9,8},{10,11... | collective-permute-start | bytes 2580488 | tf_op jit(solution)/shard_map/ppermute | solution.py:487
  15.0 11.2 %all-to-all-start = ((f32[16,24,128]{2,1,0:T(8,128)}), f32[16,24,128]{2,1,0:T(8,128)S(1)}, u32[]{:S(2)}, u32[]{:S(2)}) async-start(f32[16,24,128]{2,1,0:T(8,128)} %get-tuple-element.15), calls=%async_computation | async-start | bytes 393216 | tf_op jit(solution)/shard_map/all_to_all | solution.py:520
  19.1 10.4 %collective-permute-start.1 = (f32[75,8,128]{2,1,0:T(8,128)S(1)}, f32[75,8,128]{2,1,0:T(8,128)S(1)}, u32[]{:S(2)}, u32[]{:S(2)}) collective-permute-start(f32[75,8,128]{2,1,0:T(8,128)S(1)} %wall_blocks.1.mine), channel_id=1, source_target_pairs={{0,2},{1,3},{2,0},{3,1},{4,6},{5,7},{6,4},{7,5},{8,10},{9,11},{10,... | collective-permute-start | bytes 921608 | tf_op jit(solution)/shard_map/ppermute | solution.py:519
  55.4 19.5 %all-to-all-start.2 = ((f32[16,8,128]{2,1,0:T(8,128)}), f32[16,8,128]{2,1,0:T(8,128)S(1)}, u32[]{:S(2)}, u32[]{:S(2)}) async-start(f32[16,8,128]{2,1,0:T(8,128)} %bitcast.8), calls=%async_computation.2 | async-start | bytes 131072 | tf_op jit(solution)/shard_map/all_to_all | solution.py:467
  63.2 4.8 %collective-permute-start.2 = (f32[5,8,128]{2,1,0:T(8,128)S(1)}, f32[5,8,128]{2,1,0:T(8,128)S(1)}, u32[]{:S(2)}, u32[]{:S(2)}) collective-permute-start(f32[5,8,128]{2,1,0:T(8,128)S(1)} %get-tuple-element.22), channel_id=1, source_target_pairs={{0,2},{1,3},{2,0},{3,1},{4,6},{5,7},{6,4},{7,5},{8,10},{9,11},{10,... | collective-permute-start | bytes 61448 | tf_op jit(solution)/shard_map/ppermute | solution.py:551
  75.5 6.0 %collective-permute-start.3 = (f32[5,16,128]{2,1,0:T(8,128)S(1)}, f32[5,16,128]{2,1,0:T(8,128)S(1)}, u32[]{:S(2)}, u32[]{:S(2)}) collective-permute-start(f32[5,16,128]{2,1,0:T(8,128)S(1)} %get-tuple-element.24), channel_id=1, source_target_pairs={{0,1},{1,0},{2,3},{3,2},{4,5},{5,4},{6,7},{7,6},{8,9},{9,8},{10,11... | collective-permute-start | bytes 122888 | tf_op jit(solution)/shard_map/ppermute | solution.py:571

commit v9 on v8

--- a/solution.py
+++ b/solution.py
@@ -405,18 +405,19 @@
 
 
 def finish_kernel(
-    got, scaled, keep, recv, vecs, taken, mine, other, own, send, sl, su, res, both, sem
+    got, scaled, keep, recv, vecs, taken, mine, other, own, send, res
 ):
     _, z, core = place()
     odd = z % 2
     even = odd == 0
-    copies = eta_copies(keep, recv, sl, su, core, sem)
-    pair = [
-        pltpu.make_async_copy(mine, both.at[odd], sem.at[4]),
-        pltpu.make_async_copy(other, both.at[1 - odd], sem.at[5]),
-    ]
-    for c in pair + copies:
-        c.start()
+
+    def block(head, j):
+        stays = core == j // 2
+        at = pl.ds(j % 2, 8, stride=2)
+        return square(
+            [jnp.where(stays, keep[head + c, at, :], recv[head + c, at, :]) for c in range(25)]
+        )
+
     first = lane_iota() < 64
     a, b = [], []
     for c in range(N):
@@ -424,22 +425,18 @@
         y = got[pl.ds(64 + c, 8, stride=8), :]
         a.append(jnp.where(first, x, roll(y, 64)))
         b.append(jnp.where(first, roll(x, 64), y))
-    for c in pair:
-        c.wait()
     lv_e = [jnp.where(even, vecs[c], taken[c]) for c in range(N)]
-    mid = mv(square([both[0, c] for c in range(25)]), a, lv_e)
-    low = mv(square([both[1, 50 + c] for c in range(25)]), mid, [taken[c] for c in range(N)])
-    low = mv(square([both[1, 25 + c] for c in range(25)]), b, low)
+    mid = mv(square([jnp.where(even, mine[c], other[c]) for c in range(25)]), a, lv_e)
+    low = mv(square([jnp.where(even, other[50 + c], mine[50 + c]) for c in range(25)]), mid, [taken[c] for c in range(N)])
+    low = mv(square([jnp.where(even, other[25 + c], mine[25 + c]) for c in range(25)]), b, low)
     a = [jnp.where(even, x, y) for x, y in zip(a, mid)]
     b = [jnp.where(even, x, y) for x, y in zip(low, b)]
-    for c in copies:
-        c.wait()
     lifted = []
     for j in range(4):
-        a = mv(cell(sl, j), a, [scaled[j, c] for c in range(N)])
+        a = mv(block(50, j), a, [scaled[j, c] for c in range(N)])
         lifted.append(a)
     for j in range(3, -1, -1):
-        b = mv(cell(su, j), b, lifted[j])
+        b = mv(block(75, j), b, lifted[j])
         for c in range(N):
             res[c, j // 2, pl.ds(j % 2, 8, stride=2), :] = b[c]
     for c in range(N):
@@ -562,9 +559,9 @@
     own, theirs = pl.pallas_call(
         finish_kernel,
         out_shape=(shape(N, 16, 128), shape(N, 16, 128)),
-        in_specs=[VM, VM, ANY, ANY, VM, VM, ANY, ANY],
+        in_specs=[VM] * 8,
         out_specs=(VM, VM),
-        scratch_shapes=[side, side, pltpu.VMEM((N, 2, 16, 128), F32), both, dma(6)],
+        scratch_shapes=[pltpu.VMEM((N, 2, 16, 128), F32)],
         compiler_params=params(),
         name="finish",
     )(inflow, scaled, keep, recv, vecs, taken, mine, other)

time: 82.6 us -> 82.4 us (level)
  no operation moved by 1% of the time
where the time goes in v9:
time: 82.4 us; the launch traced here: 81.8 us
  starting transfers between devices  30.4 us (37%)
  blocking collectives  24.6 us (30%)
  waiting for transfers between devices  16.1 us (20%)
  Pallas kernels  10 us (12%)
    all_to_all x1, blocking collectives, over_z(): return lax.all_to_all(x, 'wall', 0, 0, tiled=True, axis_index_groups=groups)  24.6 us
    ppermute x1, starting transfers between devices, per_device(): recv = lax.ppermute(pack(True), 'wall', swap)  8.79 us
    all_to_all x1, starting transfers between devices, over_z(): return lax.all_to_all(x, 'wall', 0, 0, tiled=True, axis_index_groups=groups)  7.8 us
    all_to_all x1, waiting for transfers between devices, over_z(): return lax.all_to_all(x, 'wall', 0, 0, tiled=True, axis_index_groups=groups)  6.92 us
    all_to_all x1, waiting for transfers between devices, per_device(): got = lax.all_to_all(msg, 'chord', 0, 0, tiled=True)  5.28 us
    ppermute x1, starting transfers between devices, per_device(): theirs = lax.ppermute(theirs, 'wall', swap)  5.1 us
    all_to_all x1, starting transfers between devices, per_device(): got = lax.all_to_all(msg, 'chord', 0, 0, tiled=True)  3.53 us
    ppermute x1, starting transfers between devices, per_device(): taken = lax.ppermute(give, 'wall', near)  3.26 us
  transfers between devices with their start and end apart: 6, of which 6 were waited for; matrix products, arithmetic and copies ran while one was open for 0% of the time, Pallas kernels for 5%

profile of v9, /device:TPU:1, one launch (start us, length us, event | category | flops | bytes accessed | tf_op | source)
XLA Modules:
  0.0 81.8 jit_solution(5034673887998748351)
XLA Ops:
  0.0 1.3 %pack_away.1 = f32[105,16,128]{2,1,0:T(8,128)S(1)} custom-call(f32[5]{0:T(128)} %jet.3, f32[5,32,128]{2,1,0:T(8,128)} %bitcast.22, s32[32,128]{1,0:T(8,128)} %bitcast.24, f32[25,32,128]{2,1,0:T(8,128)} %bitcast.14, f32[25,32,128]{2,1,0:T(8,128)} %bitcast.16, f32[25,32,128]{2,1,0:T(8,128)} %bitcast.18, f32[25,32,128]{2,1,0:T(8,128)} %bitcast.20), custom_call_target="tpu_custom_call" | custom-call | bytes 2097152 | tf_op jit(solution)/shard_map/pack_away/pallas_call | solution.py:468
  1.4 8.8 %collective-permute-start = (f32[105,16,128]{2,1,0:T(8,128)S(1)}, f32[105,16,128]{2,1,0:T(8,128)S(1)}, u32[]{:S(2)}, u32[]{:S(2)}) collective-permute-start(f32[105,16,128]{2,1,0:T(8,128)S(1)} %pack_away.1), channel_id=1, source_target_pairs={{0,1},{1,0},{2,3},{3,2},{4,5},{5,4},{6,7},{7,6},{8,9},{9,8},{10,11... | collective-permute-start | bytes 2580488 | tf_op jit(solution)/shard_map/ppermute | solution.py:484
  10.1 1.4 %pack_here.1.keep = f32[105,16,128]{2,1,0:T(8,128)S(1)} custom-call(f32[5]{0:T(128)} %jet.3, f32[5,32,128]{2,1,0:T(8,128)} %bitcast.23, s32[32,128]{1,0:T(8,128)} %bitcast.25, f32[25,32,128]{2,1,0:T(8,128)} %bitcast.15, f32[25,32,128]{2,1,0:T(8,128)} %bitcast.17, f32[25,32,128]{2,1,0:T(8,128)} %bitcast.19, f32[25,32,128]{2,1,0:T(8,128)} %bitcast.21), custom_call_target="tpu_custom_call" | custom-call | bytes 2097152 | tf_op jit(solution)/shard_map/pack_here/pallas_call | solution.py:468
  11.5 0.6 collective-permute-done.recv
  12.1 2.9 %chord_up.1 = (f32[16,24,128]{2,1,0:T(8,128)}, f32[110,8,128]{2,1,0:T(8,128)S(1)}, f32[110,8,128]{2,1,0:T(8,128)S(1)}, f32[6,85,8,128]{3,2,1,0:T(8,128)}) custom-call(f32[105,16,128]{2,1,0:T(8,128)S(1)} %pack_here.1.keep, f32[105,16,128]{2,1,0:T(8,128)S(1)} %collective-permute-done.recv), custom_call_target="tpu_custom_call" | custom-call | flops 9216000 | bytes 4194304 | tf_op jit(solution)/shard_map/chord_up/pallas_call | solution.py:486
  15.0 3.5 %all-to-all-start = ((f32[16,24,128]{2,1,0:T(8,128)}), f32[16,24,128]{2,1,0:T(8,128)S(1)}, u32[]{:S(2)}, u32[]{:S(2)}) async-start(f32[16,24,128]{2,1,0:T(8,128)} %get-tuple-element.15), calls=%async_computation | async-start | bytes 393216 | tf_op jit(solution)/shard_map/all_to_all | solution.py:517
  18.6 0.5 wall_blocks.1.mine
  19.1 1.9 %collective-permute-start.1 = (f32[75,8,128]{2,1,0:T(8,128)S(1)}, f32[75,8,128]{2,1,0:T(8,128)S(1)}, u32[]{:S(2)}, u32[]{:S(2)}) collective-permute-start(f32[75,8,128]{2,1,0:T(8,128)S(1)} %wall_blocks.1.mine), channel_id=1, source_target_pairs={{0,2},{1,3},{2,0},{3,1},{4,6},{5,7},{6,4},{7,5},{8,10},{9,11},{10,... | collective-permute-start | bytes 921608 | tf_op jit(solution)/shard_map/ppermute | solution.py:516
  21.0 5.3 %all-to-all-done.got = f32[16,24,128]{2,1,0:T(8,128)S(1)} async-done(((f32[16,24,128]{2,1,0:T(8,128)}), f32[16,24,128]{2,1,0:T(8,128)S(1)}, u32[]{:S(2)}, u32[]{:S(2)}) %all-to-all-start) | async-done | bytes 196640 | tf_op jit(solution)/shard_map/all_to_all | solution.py:517
  26.3 2.3 %chord_down.1 = (f32[4,5,8,128]{3,2,1,0:T(8,128)S(1)}, f32[10,8,128]{2,1,0:T(8,128)S(1)}) custom-call(f32[3,5]{1,0:T(4,128)} %table.1, s32[16,128]{1,0:T(8,128)} %flags.1, f32[16,24,128]{2,1,0:T(8,128)S(1)} %all-to-all-done.got, f32[110,8,128]{2,1,0:T(8,128)S(1)} %get-tuple-element.16.leaf0, f32[110,8,128]{2,1,0:T(8,128)S(1)} %get-tuple-element.17.leaf1, ...), custom_call_target="tpu_custom_call" | custom-call | flops 49999998976 | bytes 4194304 | tf_op jit(solution)/shard_map/chord_down/pallas_call | solution.py:518
  28.6 0.9 %collective-permute-done.1.other = f32[75,8,128]{2,1,0:T(8,128)S(1)} collective-permute-done((f32[75,8,128]{2,1,0:T(8,128)S(1)}, f32[75,8,128]{2,1,0:T(8,128)S(1)}, u32[]{:S(2)}, u32[]{:S(2)}) %collective-permute-start.1) | collective-permute-done | bytes 307232 | tf_op jit(solution)/shard_map/ppermute | solution.py:516
  29.4 0.4 wall_pair.1
  29.9 24.6 %all_to_all.15 = f32[16,24,128]{2,1,0:T(8,128)S(1)} all-to-all(f32[16,24,128]{2,1,0:T(8,128)S(1)} %bitcast.13), channel_id=1, replica_groups={{0,2,4,6,8,10,12,14,16,18,20,22,24,26,28,30},{1,3,5,7,9,11,13,15,17,19,..., dimensions={0} | all-to-all | bytes 393216 | tf_op jit(solution)/shard_map/all_to_all | solution.py:464
  54.5 0.9 %wall_solve.1 = f32[128,128]{1,0:T(8,128)} custom-call(f32[384,128]{1,0:T(8,128)S(1)} %bitcast.11), custom_call_target="tpu_custom_call" | custom-call | tf_op jit(solution)/shard_map/wall_solve/pallas_call | solution.py:549
  55.4 7.8 %all-to-all-start.2 = ((f32[16,8,128]{2,1,0:T(8,128)}), f32[16,8,128]{2,1,0:T(8,128)S(1)}, u32[]{:S(2)}, u32[]{:S(2)}) async-start(f32[16,8,128]{2,1,0:T(8,128)} %bitcast.8), calls=%async_computation.2 | async-start | bytes 131072 | tf_op jit(solution)/shard_map/all_to_all | solution.py:464
  63.2 3.3 %collective-permute-start.2 = (f32[5,8,128]{2,1,0:T(8,128)S(1)}, f32[5,8,128]{2,1,0:T(8,128)S(1)}, u32[]{:S(2)}, u32[]{:S(2)}) collective-permute-start(f32[5,8,128]{2,1,0:T(8,128)S(1)} %get-tuple-element.22), channel_id=1, source_target_pairs={{0,2},{1,3},{2,0},{3,1},{4,6},{5,7},{6,4},{7,5},{8,10},{9,11},{10,... | collective-permute-start | bytes 61448 | tf_op jit(solution)/shard_map/ppermute | solution.py:548
  66.5 1.5 %collective-permute-done.2.taken = f32[5,8,128]{2,1,0:T(8,128)S(1)} collective-permute-done((f32[5,8,128]{2,1,0:T(8,128)S(1)}, f32[5,8,128]{2,1,0:T(8,128)S(1)}, u32[]{:S(2)}, u32[]{:S(2)}) %collective-permute-start.2) | collective-permute-done | bytes 20512 | tf_op jit(solution)/shard_map/ppermute | solution.py:548
  68.0 6.9 %all-to-all-done.2 = f32[16,8,128]{2,1,0:T(8,128)S(1)} async-done(((f32[16,8,128]{2,1,0:T(8,128)}), f32[16,8,128]{2,1,0:T(8,128)S(1)}, u32[]{:S(2)}, u32[]{:S(2)}) %all-to-all-start.2) | async-done | bytes 65568 | tf_op jit(solution)/shard_map/all_to_all | solution.py:464
  74.9 0.3 finish.1
  75.2 5.1 %collective-permute-start.3 = (f32[5,16,128]{2,1,0:T(8,128)S(1)}, f32[5,16,128]{2,1,0:T(8,128)S(1)}, u32[]{:S(2)}, u32[]{:S(2)}) collective-permute-start(f32[5,16,128]{2,1,0:T(8,128)S(1)} %get-tuple-element.24), channel_id=1, source_target_pairs={{0,1},{1,0},{2,3},{3,2},{4,5},{5,4},{6,7},{7,6},{8,9},{9,8},{10,11... | collective-permute-start | bytes 122888 | tf_op jit(solution)/shard_map/ppermute | solution.py:568
  80.4 0.8 %collective-permute-done.3 = f32[5,16,128]{2,1,0:T(8,128)S(1)} collective-permute-done((f32[5,16,128]{2,1,0:T(8,128)S(1)}, f32[5,16,128]{2,1,0:T(8,128)S(1)}, u32[]{:S(2)}, u32[]{:S(2)}) %collective-permute-start.3) | collective-permute-done | bytes 40992 | tf_op jit(solution)/shard_map/ppermute | solution.py:568
  81.2 0.6 pad_maximum_fusion
  (1 shorter events, 0.0 us)
Async XLA Ops:
  1.4 10.8 %collective-permute-start = (f32[105,16,128]{2,1,0:T(8,128)S(1)}, f32[105,16,128]{2,1,0:T(8,128)S(1)}, u32[]{:S(2)}, u32[]{:S(2)}) collective-permute-start(f32[105,16,128]{2,1,0:T(8,128)S(1)} %pack_away.1), channel_id=1, source_target_pairs={{0,1},{1,0},{2,3},{3,2},{4,5},{5,4},{6,7},{7,6},{8,9},{9,8},{10,11... | collective-permute-start | bytes 2580488 | tf_op jit(solution)/shard_map/ppermute | solution.py:484
  15.0 11.2 %all-to-all-start = ((f32[16,24,128]{2,1,0:T(8,128)}), f32[16,24,128]{2,1,0:T(8,128)S(1)}, u32[]{:S(2)}, u32[]{:S(2)}) async-start(f32[16,24,128]{2,1,0:T(8,128)} %get-tuple-element.15), calls=%async_computation | async-start | bytes 393216 | tf_op jit(solution)/shard_map/all_to_all | solution.py:517
  19.1 10.4 %collective-permute-start.1 = (f32[75,8,128]{2,1,0:T(8,128)S(1)}, f32[75,8,128]{2,1,0:T(8,128)S(1)}, u32[]{:S(2)}, u32[]{:S(2)}) collective-permute-start(f32[75,8,128]{2,1,0:T(8,128)S(1)} %wall_blocks.1.mine), channel_id=1, source_target_pairs={{0,2},{1,3},{2,0},{3,1},{4,6},{5,7},{6,4},{7,5},{8,10},{9,11},{10,... | collective-permute-start | bytes 921608 | tf_op jit(solution)/shard_map/ppermute | solution.py:516
  55.4 19.5 %all-to-all-start.2 = ((f32[16,8,128]{2,1,0:T(8,128)}), f32[16,8,128]{2,1,0:T(8,128)S(1)}, u32[]{:S(2)}, u32[]{:S(2)}) async-start(f32[16,8,128]{2,1,0:T(8,128)} %bitcast.8), calls=%async_computation.2 | async-start | bytes 131072 | tf_op jit(solution)/shard_map/all_to_all | solution.py:464
  63.2 4.8 %collective-permute-start.2 = (f32[5,8,128]{2,1,0:T(8,128)S(1)}, f32[5,8,128]{2,1,0:T(8,128)S(1)}, u32[]{:S(2)}, u32[]{:S(2)}) collective-permute-start(f32[5,8,128]{2,1,0:T(8,128)S(1)} %get-tuple-element.22), channel_id=1, source_target_pairs={{0,2},{1,3},{2,0},{3,1},{4,6},{5,7},{6,4},{7,5},{8,10},{9,11},{10,... | collective-permute-start | bytes 61448 | tf_op jit(solution)/shard_map/ppermute | solution.py:548
  75.2 6.0 %collective-permute-start.3 = (f32[5,16,128]{2,1,0:T(8,128)S(1)}, f32[5,16,128]{2,1,0:T(8,128)S(1)}, u32[]{:S(2)}, u32[]{:S(2)}) collective-permute-start(f32[5,16,128]{2,1,0:T(8,128)S(1)} %get-tuple-element.24), channel_id=1, source_target_pairs={{0,1},{1,0},{2,3},{3,2},{4,5},{5,4},{6,7},{7,6},{8,9},{9,8},{10,11... | collective-permute-start | bytes 122888 | tf_op jit(solution)/shard_map/ppermute | solution.py:568
